TPU v7x, 32 devices: a whole 2x2x4 slice. The times are simulated.
32 devices in a mesh: rec: 2 (over y), gx: 16 (over z, x, core).
Axes of the slice: x: 2, y: 2, z: 4, core: 2. Of those that a mesh axis runs over, the one named last changes fastest.
Arguments:
- velocity: float32 [4, 3, 96, 16, 128], P(None, None, ('rec', 'gx')), parts along dimension 2, may hold values from -6 to 36, as said below
- span_rim: float32 [4, 2, 96, 10, 6], P(None, None, ('rec', 'gx')), parts along dimension 2, may hold values from -6 to 36, as said below
- sketch_old: bfloat16 [3, 96, 10, 128, 256], P(None, ('rec', 'gx')), parts along dimension 1, as said below
- omega: float32 [4, 256], replicated, may hold values from -6 to 6
Outputs:
- basis: bfloat16 [3, 96, 10, 128, 256], P(None, ('rec', 'gx')), parts along dimension 1
- factor: float32 [512, 256], P('rec'), parts along dimension 0
There are 2 independent parts, one for each index of `rec`. A program takes and returns all parts, laid end to end along the dimension named above; an argument that names none is the same for every part. Nothing has to cross between parts.
Inputs may be any that keep to these rules, and one draw needn't show every extreme that they name: `sketch_old`: finite values of order one; rows differ in scale. `velocity`: finite values. `span_rim`: finite values.
All inputs are finite; a program needn't handle non-finite values.
Results may differ from a plain program's by a relative error of at most 0.014.
The roundings to bfloat16 on the way count: a program that leaves them out, or rounds other values in their place, can miss the bound.
Values sent between devices are 32-bit elements; how exact they have to be, the bound alone decides.
No kernel may reach another device: no remote copies, remote signals or barrier semaphores. Data moves between devices by JAX's collectives and lax.ppermute only.
A program may use at most 64 MiB of HBM per device.

v0:
```python
import jax
import jax.numpy as jnp
from jax import lax
from jax.sharding import PartitionSpec as P

COEFS = (0.75, -0.15, 1.0 / 60.0)


def extended_2(cells, sides, width):
    for axis, dim in sides:
        count = lax.axis_size(axis)
        head = lax.slice_in_dim(cells, 0, width, axis=dim)
        tail = lax.slice_in_dim(cells, cells.shape[dim] - width, cells.shape[dim], axis=dim)
        cells = jnp.concatenate(
            [
                lax.ppermute(tail, axis, [(i, (i + 1) % count) for i in range(count)]),
                cells,
                lax.ppermute(head, axis, [((i + 1) % count, i) for i in range(count)]),
            ],
            axis=dim,
        )
    return cells


def band_diff(padded, axis, count):
    out_shape = list(padded.shape)
    out_shape[axis] = count
    total = jnp.zeros(tuple(out_shape), jnp.float32)
    for shift_k, weight in zip((1, 2, 3), COEFS):
        ahead = lax.slice_in_dim(padded, 3 + shift_k, 3 + shift_k + count, axis=axis)
        behind = lax.slice_in_dim(padded, 3 - shift_k, 3 - shift_k + count, axis=axis)
        total = total + weight * (ahead - behind)
    return total


def span_extend(field, rim_part):
    return jnp.concatenate([rim_part[..., :3], field, rim_part[..., 3:]], axis=-1)


def upper_factor(gram):
    order = gram.shape[0]
    index = jnp.arange(order, dtype=jnp.int32)

    def column_step(j, lower):
        pick = (index == j).astype(gram.dtype)
        row = jnp.dot(pick, lower, precision=lax.Precision.HIGHEST)
        column = jnp.dot(gram, pick, precision=lax.Precision.HIGHEST) - jnp.dot(
            lower, row, precision=lax.Precision.HIGHEST
        )
        pivot = jnp.sqrt(jnp.sum(column * pick))
        below = (index > j).astype(gram.dtype)
        fresh = column * below / pivot + pick * pivot
        return lower + fresh[:, None] * pick[None, :]

    lower = lax.fori_loop(0, order, column_step, jnp.zeros_like(gram))
    return lower.T


def inverse_upper(upper):
    order = upper.shape[0]
    index = jnp.arange(order, dtype=jnp.int32)
    lower = upper.T

    def row_step(j, solved):
        pick = (index == j).astype(upper.dtype)
        row = jnp.dot(pick, lower, precision=lax.Precision.HIGHEST)
        pivot = jnp.sum(row * pick)
        fresh = (pick - jnp.dot(row, solved, precision=lax.Precision.HIGHEST)) / pivot
        return solved + pick[:, None] * fresh[None, :]

    solved = lax.fori_loop(0, order, row_step, jnp.zeros_like(upper))
    return solved.T


def gram_of(matrix):
    return lax.dot_general(
        matrix, matrix, (((0,), (0,)), ((), ())), preferred_element_type=jnp.float32
    )


def local(velocity, span_rim, sketch_old, omega):
    slabs = velocity.shape[2]
    band_rows = velocity.shape[3] - 6
    span_cells = velocity.shape[4]
    extended = extended_2(velocity, (("gx", 2),), 3)
    v_ext = extended[:, 1, :, 3 : 3 + band_rows]
    w_ext = extended[:, 2, :, 3 : 3 + band_rows]
    band = velocity[:, :, :, 3 : 3 + band_rows]
    u_span = span_extend(band[:, 0], span_rim[:, 0])
    v_span = span_extend(band[:, 1], span_rim[:, 1])
    vort_x = band_diff(velocity[:, 2], 2, band_rows) - band_diff(v_span, 3, span_cells)
    vort_y = band_diff(u_span, 3, span_cells) - band_diff(w_ext, 1, slabs)
    vort_z = band_diff(v_ext, 1, slabs) - band_diff(velocity[:, 0], 2, band_rows)
    vort = jnp.stack([vort_x, vort_y, vort_z], axis=1)
    sketch = sketch_old.astype(jnp.float32)
    for snap in range(vort.shape[0]):
        sketch = sketch + vort[snap][..., None] * omega[snap]
    sketch = sketch.astype(jnp.bfloat16)
    matrix = sketch.reshape(-1, sketch.shape[-1])
    total = jnp.float32(matrix.shape[0] * lax.axis_size("gx"))
    local_gram = gram_of(matrix) / total
    factor = upper_factor(lax.psum(local_gram, "gx"))
    inverse_one = inverse_upper(factor).astype(jnp.bfloat16)
    basis = jnp.dot(matrix, inverse_one, preferred_element_type=jnp.float32).astype(jnp.bfloat16)
    return (basis.reshape(sketch.shape), factor)


def solution(mesh):
    in_specs = (
        P(None, None, ("rec", "gx"), None, None),
        P(None, None, ("rec", "gx"), None, None),
        P(None, ("rec", "gx"), None, None, None),
        P(),
    )
    out_specs = (P(None, ("rec", "gx"), None, None, None), P("rec", None))
    return jax.shard_map(local, mesh=mesh, in_specs=in_specs, out_specs=out_specs, check_vma=False)
```

profile of v0, /device:TPU:0, one launch (start us, length us, event | category | flops | bytes accessed | tf_op | source)
XLA Modules:
  0.0 1443.6 jit_solution(5448559899833227195)
XLA Ops:
  7.2 5.5 collective-permute-start.1
  17.6 4.2 collective-permute-done
  23.4 7.5 add_convert_fusion
  30.9 2.5 copy-done
  33.5 2.4 fusion.21
  35.9 87.0 %all-reduce.2.cloned.1.call-done = f32[256,256]{1,0:T(8,128)} async-done(((f32[256,256]{1,0:T(8,128)}), f32[256,256]{1,0:T(8,128)}) %all-reduce.2.cloned.1.call-update) | async-done | bytes 262160 | tf_op jit(solution)/shard_map/psum | solution.py:102
  123.0 829.0 %while.30 = (s32[]{:T(128)}, f32[256,256]{1,0:T(8,128)S(1)}, f32[256,256]{1,0:T(8,128)}, s32[]{:T(128)}, s32[]{:T(128)}) while((s32[]{:T(128)}, f32[256,256]{1,0:T(8,128)S(1)}, f32[256,256]{1,0:T(8,128)}, s32[]{:T(128)}, s32[]{:T(128)}) %tuple.85), condition=%wide.region_3.0_spmd.clone.clone, body=%wide.region_1.0_spmd.clone.clone.sunk | while | flops 2690306 | bytes 1324397 | solution.py:55
  126.4 1.2 fusion.114
  142.6 1.2 fusion.114
  145.9 1.2 fusion.114
  149.1 1.2 fusion.114
  152.3 1.2 fusion.114
  155.6 1.2 fusion.114
  158.8 1.2 fusion.114
  162.1 1.2 fusion.114
  165.3 1.2 fusion.114
  168.5 1.2 fusion.114
  171.8 1.2 fusion.114
  175.0 1.2 fusion.114
  178.3 1.2 fusion.114
  181.5 1.2 fusion.114
  184.7 1.2 fusion.114
  188.0 1.2 fusion.114
  204.2 1.2 fusion.114
  207.4 1.2 fusion.114
  210.6 1.2 fusion.114
  213.9 1.2 fusion.114
  217.1 1.2 fusion.114
  220.4 1.2 fusion.114
  223.6 1.2 fusion.114
  226.8 1.2 fusion.114
  230.1 1.2 fusion.114
  233.3 1.2 fusion.114
  236.5 1.2 fusion.114
  239.8 1.2 fusion.114
  243.0 1.2 fusion.114
  246.3 1.2 fusion.114
  249.5 1.2 fusion.114
  265.7 1.2 fusion.114
  268.9 1.2 fusion.114
  272.2 1.2 fusion.114
  275.4 1.2 fusion.114
  278.6 1.2 fusion.114
  281.9 1.2 fusion.114
  285.1 1.2 fusion.114
  288.4 1.2 fusion.114
  952.8 476.9 %while.29 = (s32[]{:T(128)}, f32[256,256]{1,0:T(8,128)S(1)}, f32[256,256]{1,0:T(8,128)S(1)}, s32[]{:T(128)}, s32[]{:T(128)}) while((s32[]{:T(128)}, f32[256,256]{1,0:T(8,128)S(1)}, f32[256,256]{1,0:T(8,128)S(1)}, s32[]{:T(128)}, s32[]{:T(128)}) %tuple.88), condition=%wide.region_6.0_spmd.clone, body=%wide.region_4.0_spmd.clone.sunk | while | flops 1837314 | bytes 1058916 | solution.py:71
  1429.8 7.0 convolution_convert_fusion
  (3831 shorter events, 1066.5 us)
Async XLA Ops:
  7.2 115.8 %all-reduce.2.cloned.1.call-start = ((), (), s32[]{:S(2)}) async-start(), calls=%async_computation | async-start | bytes 524288 | tf_op jit(solution)/shard_map/psum | solution.py:102
  7.2 15.5 %collective-permute-start.1 = (f32[4,3,3,16,128]{4,3,2,1,0:T(8,128)}, f32[4,3,3,16,128]{4,3,2,1,0:T(8,128)S(1)}, u32[]{:S(2)}, u32[]{:S(2)}) collective-permute-start(f32[4,3,3,16,128]{4,3,2,1,0:T(8,128)} %param.8), channel_id=1, source_target_pairs={{1,0},{2,1},{3,2},{4,3},{5,4},{6,5},{7,6},{8,7},{9,8},{10,9},{11,1... | collective-permute-start | bytes 884744 | tf_op jit(solution)/shard_map/ppermute | solution.py:18
  12.7 9.1 collective-permute-start
  17.6 5.8 copy-start.1
  30.9 2.5 copy-start
Sparse Core Ops, SparseCore 0:
  36.0 86.8 all-reduce.1
where the time goes:
time: 1470 us; the launch traced here: 1440 us
  other arithmetic  573 us (39%)
  matrix products  547 us (37%)
  loops' own time  201 us (14%)
  waiting for transfers between devices  91.2 us (6%)
    dot_general x256, matrix products, column_step(): jnp.dot(gram, pick, precision=lax.Precision.HIGHEST)  301 us
    another operation x1, loops' own time, upper_factor(): lower = lax.fori_loop(0, order, column_step, jnp.zeros_like(gram))  189 us
    div x256, other arithmetic, row_step(): (pick - jnp.dot(row, solved, precision=lax.Precision.HIGHEST)) / pivot  170 us
    reduce_sum x256, other arithmetic, column_step(): pivot = jnp.sqrt(jnp.sum(column * pick))  170 us
    reduce_sum x256, other arithmetic, row_step(): pivot = jnp.sum(row * pick)  162 us
    psum x1, waiting for transfers between devices, local(): factor = upper_factor(lax.psum(local_gram, 'gx'))  87 us
    dot_general x256, matrix products, column_step(): jnp.dot(lower, row, precision=lax.Precision.HIGHEST)  81.5 us
    dot_general x256, matrix products, column_step(): row = jnp.dot(pick, lower, precision=lax.Precision.HIGHEST)  53.6 us
  transfers between devices with their start and end apart: 3, of which 2 were waited for; matrix products, arithmetic and copies ran while one was open for 0% of the time, Pallas kernels for 0%

commit v1 on v0

--- a/solution.py
+++ b/solution.py
@@ -1,6 +1,10 @@
+import functools
+
 import jax
 import jax.numpy as jnp
 from jax import lax
+from jax.experimental import pallas as pl
+from jax.experimental.pallas import tpu as pltpu
 from jax.sharding import PartitionSpec as P
 
 COEFS = (0.75, -0.15, 1.0 / 60.0)
@@ -37,39 +41,127 @@
     return jnp.concatenate([rim_part[..., :3], field, rim_part[..., 3:]], axis=-1)
 
 
-def upper_factor(gram):
+def factor_invert(t_ref, u_ref, x_ref):
+    order = t_ref.shape[0]
+    lane = lax.broadcasted_iota(jnp.int32, (8, 128), 1)
+    sub = lax.broadcasted_iota(jnp.int32, (8, 128), 0)
+    full = (8, 128)
+    zero = jnp.zeros(full, jnp.float32)
+    for p in range(order // 8):
+        j0 = 8 * p
+        hd = j0 // 128
+        c0 = j0 % 128
+        halves = [t_ref[j0:j0 + 8, 128 * h:128 * h + 128] for h in range(2)]
+        diag = halves[hd]
+        in_panel = (lane >= c0) & (lane < c0 + 8)
+        ident = jnp.where(lane == sub + c0, 1.0, 0.0)
+        halves[hd] = jnp.where(in_panel, ident, diag)
+        a = {}
+        for j in range(8):
+            for i in range(j + 1):
+                a[i, j] = jnp.broadcast_to(diag[i:i + 1, c0 + j:c0 + j + 1], full)
+        rows = [[jnp.broadcast_to(x[i:i + 1], full) for x in (halves[0], halves[1], diag)] for i in range(8)]
+        l = {}
+        r = [None] * 8
+        rs = [None] * 8
+        for k in range(8):
+            r[k] = 1.0 / a[k, k]
+            rs[k] = lax.rsqrt(a[k, k])
+            for i in range(k + 1, 8):
+                l[i, k] = a[k, i] * r[k]
+            for i in range(k + 1, 8):
+                for j in range(i, 8):
+                    a[i, j] = a[i, j] - l[i, k] * a[k, j]
+                rows[i] = [x - l[i, k] * y for x, y in zip(rows[i], rows[k])]
+        z = [None] * 8
+        for k in reversed(range(8)):
+            zk = [rows[k][h] * r[k] for h in range(2)]
+            for i in range(k + 1, 8):
+                zk = [x - l[i, k] * y for x, y in zip(zk, z[i])]
+            z[k] = zk
+        for q in range(p + 1, order // 8):
+            rr = slice(8 * q, 8 * q + 8)
+            old = [t_ref[rr, 128 * h:128 * h + 128] for h in range(2)]
+            m = [jnp.broadcast_to(old[hd][:, c0 + k:c0 + k + 1], full) for k in range(8)]
+            acc = [old[0], old[1]]
+            acc[hd] = jnp.where(in_panel, 0.0, acc[hd])
+            for h in range(2):
+                s = m[0] * z[0][h]
+                for k in range(1, 8):
+                    s = s + m[k] * z[k][h]
+                t_ref[rr, 128 * h:128 * h + 128] = acc[h] - s
+        outs = [zero, zero, zero]
+        for k in range(8):
+            outs = [jnp.where(sub == k, rows[k][c] * rs[k], outs[c]) for c in range(3)]
+        for h in range(2):
+            col = lane + 128 * h
+            src = outs[2] if h == hd else outs[h]
+            u_ref[j0:j0 + 8, 128 * h:128 * h + 128] = jnp.where(col >= sub + j0, src, 0.0)
+            x_ref[j0:j0 + 8, 128 * h:128 * h + 128] = jnp.where(col <= sub + j0, outs[h], 0.0)
+
+
+def pack_kernel(parity_ref, gram_ref, keep_ref, send_ref):
+    half = gram_ref.shape[0] // 2
+    row = lax.broadcasted_iota(jnp.int32, (half, half), 0)
+    col = lax.broadcasted_iota(jnp.int32, (half, half), 1)
+    low = gram_ref[half:, half:]
+    mixed = jnp.where(row <= col, gram_ref[:half, :half], low)
+    diag = jnp.sum(jnp.where(row == col, low, 0.0), axis=0, keepdims=True)
+    packed = jnp.concatenate([gram_ref[:half, half:], mixed], axis=1)
+    part = half // 2
+    extra = jnp.broadcast_to(jnp.concatenate([diag, diag], axis=1), (8, 2 * half))
+    first = parity_ref[0] == 0
+    upper, lower = packed[:part], packed[part:]
+    keep_ref[:part] = jnp.where(first, upper, lower)
+    send_ref[:part] = jnp.where(first, lower, upper)
+    keep_ref[part:] = extra
+    send_ref[part:] = extra
+
+
+def factor_kernel(scale, parity_ref, mine_ref, other_ref, upper_ref, inverse_ref, work_ref, solved_ref):
+    order = work_ref.shape[0]
+    half = order // 2
+    part = half // 2
+    first = parity_ref[0] == 0
+    mine, other = mine_ref[...] * scale, other_ref[...] * scale
+    packed = jnp.concatenate([jnp.where(first, mine[:part], other[:part]), jnp.where(first, other[:part], mine[:part])], axis=0)
+    cross, mixed = packed[:, :half], packed[:, half:]
+    row = lax.broadcasted_iota(jnp.int32, (half, half), 0)
+    col = lax.broadcasted_iota(jnp.int32, (half, half), 1)
+    turned = mixed.T
+    diag = jnp.broadcast_to(mine[part : part + 1, :half], (half, half))
+    work_ref[:half, :half] = jnp.where(row <= col, mixed, turned)
+    work_ref[:half, half:] = cross
+    work_ref[half:, :half] = cross.T
+    work_ref[half:, half:] = jnp.where(row > col, mixed, jnp.where(row < col, turned, diag))
+    factor_invert(work_ref, upper_ref, solved_ref)
+    inverse_ref[...] = solved_ref[...].T.astype(jnp.bfloat16)
+
+
+def summed_factor(gram, rows, axis):
+    count = lax.axis_size(axis)
     order = gram.shape[0]
-    index = jnp.arange(order, dtype=jnp.int32)
-
-    def column_step(j, lower):
-        pick = (index == j).astype(gram.dtype)
-        row = jnp.dot(pick, lower, precision=lax.Precision.HIGHEST)
-        column = jnp.dot(gram, pick, precision=lax.Precision.HIGHEST) - jnp.dot(
-            lower, row, precision=lax.Precision.HIGHEST
-        )
-        pivot = jnp.sqrt(jnp.sum(column * pick))
-        below = (index > j).astype(gram.dtype)
-        fresh = column * below / pivot + pick * pivot
-        return lower + fresh[:, None] * pick[None, :]
-
-    lower = lax.fori_loop(0, order, column_step, jnp.zeros_like(gram))
-    return lower.T
-
-
-def inverse_upper(upper):
-    order = upper.shape[0]
-    index = jnp.arange(order, dtype=jnp.int32)
-    lower = upper.T
-
-    def row_step(j, solved):
-        pick = (index == j).astype(upper.dtype)
-        row = jnp.dot(pick, lower, precision=lax.Precision.HIGHEST)
-        pivot = jnp.sum(row * pick)
-        fresh = (pick - jnp.dot(row, solved, precision=lax.Precision.HIGHEST)) / pivot
-        return solved + pick[:, None] * fresh[None, :]
-
-    solved = lax.fori_loop(0, order, row_step, jnp.zeros_like(upper))
-    return solved.T
+    parity = (lax.axis_index(axis) % 2).reshape(1)
+    in_smem = pl.BlockSpec(memory_space=pltpu.SMEM)
+    in_vmem = pl.BlockSpec(memory_space=pltpu.VMEM)
+    piece = jax.ShapeDtypeStruct((order // 4 + 8, order), jnp.float32)
+    keep, send = pl.pallas_call(
+        pack_kernel, out_shape=[piece, piece], in_specs=[in_smem, in_vmem], out_specs=[in_vmem, in_vmem]
+    )(parity, gram)
+    swap = lambda k: [(i, i ^ k) for i in range(count)]
+    total = keep + lax.ppermute(send, axis, swap(1))
+    step = 2
+    while step < count:
+        total = total + lax.ppermute(total, axis, swap(step))
+        step *= 2
+    other = lax.ppermute(total, axis, swap(1))
+    return pl.pallas_call(
+        functools.partial(factor_kernel, 1.0 / rows),
+        out_shape=[jax.ShapeDtypeStruct((order, order), jnp.float32), jax.ShapeDtypeStruct((order, order), jnp.bfloat16)],
+        in_specs=[in_smem, in_vmem, in_vmem],
+        out_specs=[in_vmem, in_vmem],
+        scratch_shapes=[pltpu.VMEM((order, order), jnp.float32), pltpu.VMEM((order, order), jnp.float32)],
+    )(parity, total, other)
 
 
 def gram_of(matrix):
@@ -97,10 +189,8 @@
         sketch = sketch + vort[snap][..., None] * omega[snap]
     sketch = sketch.astype(jnp.bfloat16)
     matrix = sketch.reshape(-1, sketch.shape[-1])
-    total = jnp.float32(matrix.shape[0] * lax.axis_size("gx"))
-    local_gram = gram_of(matrix) / total
-    factor = upper_factor(lax.psum(local_gram, "gx"))
-    inverse_one = inverse_upper(factor).astype(jnp.bfloat16)
+    rows = matrix.shape[0] * lax.axis_size("gx")
+    factor, inverse_one = summed_factor(gram_of(matrix), rows, "gx")
     basis = jnp.dot(matrix, inverse_one, preferred_element_type=jnp.float32).astype(jnp.bfloat16)
     return (basis.reshape(sketch.shape), factor)
 

time: 1470 us -> 68.3 us (0.05); the launches traced: 1440 us -> 67.9 us
  other arithmetic: 573 us -> 9.3 us
  matrix products: 547 us -> 9.58 us
  loops' own time: 201 us -> 0 us
  waiting for transfers between devices: 91.2 us -> 21 us
  Pallas kernels: 0 us -> 15.2 us
    dot_general x1280 -> x0, matrix products: 537 us -> none  [the longest x256 301 us: column_step(): jnp.dot(gram, pick, precision=lax.Precision.HIGHEST)]
    reduce_sum x512 -> x0, other arithmetic: 332 us -> none  [the longest x256 170 us: column_step(): pivot = jnp.sqrt(jnp.sum(column * pick))]
    another operation x2 -> x0, loops' own time: 201 us -> none  [the longest x1 189 us: upper_factor(): lower = lax.fori_loop(0, order, column_step, jnp.zeros_like(gram))]
    div x256 -> x0, other arithmetic: 170 us -> none  [row_step(): (pick - jnp.dot(row, solved, precision=lax.Precision.HIGHEST)) / pivot]
    psum x1 -> x0, waiting for transfers between devices: 87 us -> none  [local(): factor = upper_factor(lax.psum(local_gram, 'gx'))]
    add x768 -> x4, other arithmetic: 59.3 us -> 0.93 us  [the longest x1 0.9 us: summed_factor(): total = keep + lax.ppermute(send, axis, swap(1))]
    ppermute x0 -> x5, waiting for transfers between devices: none -> 16.9 us  [the longest x3 14.1 us: summed_factor(): total = total + lax.ppermute(total, axis, swap(step))]
    pallas_call x0 -> x2, Pallas kernels: none -> 15.2 us  [the longest x1 13.6 us: summed_factor(): pl.pallas_call(functools.partial(factor_kernel, 1.0 / rows), out_shape=[j...]
  transfers between devices with their start and end apart: 3 -> 7, of which waited for: 2 -> 6; matrix products, arithmetic and copies ran while one was open for 0% -> 9% of each run, Pallas kernels for 0% -> 0%
where the time goes in v1:
time: 68.3 us; the launch traced here: 67.9 us
  waiting for transfers between devices  21 us (31%)
  Pallas kernels  15.2 us (22%)
  matrix products  9.58 us (14%)
  other arithmetic  9.3 us (14%)
  local copies, waits for them, and re-layouts  6.23 us (9%)
  starting transfers between devices  5.76 us (8%)
  between operations  0.8 us (1%)
    ppermute x3, waiting for transfers between devices, summed_factor(): total = total + lax.ppermute(total, axis, swap(step))  14.1 us
    pallas_call x1, Pallas kernels, summed_factor(): pl.pallas_call(functools.partial(factor_kernel, 1.0 / rows), out_shape=[j...  13.6 us
    convert_element_type x1, other arithmetic, local(): sketch = sketch.astype(jnp.bfloat16)  7.55 us
    dot_general x1, matrix products, local(): jnp.dot(matrix, inverse_one, preferred_element_type=jnp.float32)  6.95 us
    ppermute x1, starting transfers between devices, extended_2(): lax.ppermute(head, axis, [((i + 1) % count, i) for i in range(count)])  5.47 us
    ppermute x1, waiting for transfers between devices, extended_2(): lax.ppermute(tail, axis, [(i, (i + 1) % count) for i in range(count)])  4.17 us
    dot_general x1, matrix products, gram_of(): lax.dot_general(matrix, matrix, (((0,), (0,)), ((), ())), preferred_eleme...  2.63 us
    unnamed x10, local copies, waits for them, and re-layouts  1.64 us
  transfers between devices with their start and end apart: 7, of which 6 were waited for; matrix products, arithmetic and copies ran while one was open for 9% of the time, Pallas kernels for 0%

profile of v1, /device:TPU:0, one launch (start us, length us, event | category | flops | bytes accessed | tf_op | source)
XLA Modules:
  0.0 67.9 jit_solution(17209384763177571536)
XLA Ops:
  0.6 5.5 %collective-permute-start.1 = (f32[4,3,3,16,128]{4,3,2,1,0:T(8,128)}, f32[4,3,3,16,128]{4,3,2,1,0:T(8,128)S(1)}, u32[]{:S(2)}, u32[]{:S(2)}) collective-permute-start(f32[4,3,3,16,128]{4,3,2,1,0:T(8,128)} %param.4), channel_id=1, source_target_pairs={{1,0},{2,1},{3,2},{4,3},{5,4},{6,5},{7,6},{8,7},{9,8},{10,9},{11,1... | collective-permute-start | bytes 884744 | tf_op jit(solution)/shard_map/ppermute | solution.py:22
  6.1 0.0 collective-permute-start
  6.1 1.0 %slice_bitcast_fusion.5 = (f32[4,3,16,128]{3,2,1,0:T(8,128)S(1)}, f32[4,3,16,128]{3,2,1,0:T(8,128)S(1)}) fusion(f32[4,3,3,16,128]{4,3,2,1,0:T(8,128)} %param.4), kind=kLoop, calls=%fused_computation.91 | loop fusion | bytes 393216 | tf_op jit(solution)/shard_map/squeeze | solution.py:183
  7.1 1.0 %slice_bitcast_fusion.4 = (f32[4,3,10,128]{3,2,1,0:T(8,128)S(1)}, f32[4,3,10,128]{3,2,1,0:T(8,128)S(1)}) fusion(f32[4,3,3,16,128]{4,3,2,1,0:T(8,128)} %param.4), kind=kLoop, calls=%fused_computation.90 | loop fusion | bytes 245760 | tf_op jit(solution)/shard_map/squeeze | solution.py:182
  8.0 1.0 %fusion.50 = (f32[4,1,3,10,6]{3,1,4,2,0:T(1,128)S(1)}, f32[4,1,3,10,6]{3,1,4,2,0:T(1,128)S(1)}) fusion(f32[4,2,3,10,6]{3,1,4,2,0:T(2,128)} %param.5), kind=kLoop, calls=%fused_computation.101 | loop fusion | bytes 11520 | tf_op jit(solution)/shard_map/slice | solution.py:182
  9.1 0.2 copy.19
  9.3 0.2 copy.20
  9.4 0.4 fusion.18
  9.8 0.8 %fusion.53 = (f32[1,256]{1,0:T(1,128)S(1)}, f32[1,256]{1,0:T(1,128)S(1)}, f32[1,256]{1,0:T(1,128)S(1)}, f32[1,256]{1,0:T(1,128)S(1)}) fusion(f32[4,256]{1,0:T(4,128)} %param.7), kind=kLoop, calls=%fused_computation.104 | loop fusion | bytes 8192 | tf_op jit(solution)/shard_map/slice | solution.py:189
  10.7 0.2 copy.23
  10.8 0.2 copy.24
  11.0 0.0 copy-start.1
  11.0 4.2 %collective-permute-done = f32[4,3,3,16,128]{4,3,2,1,0:T(8,128)S(1)} collective-permute-done((f32[4,3,3,16,128]{4,3,2,1,0:T(8,128)}, f32[4,3,3,16,128]{4,3,2,1,0:T(8,128)S(1)}, u32[]{:S(2)}, u32[]{:S(2)}) %collective-permute-start) | collective-permute-done | bytes 294944 | tf_op jit(solution)/shard_map/ppermute | solution.py:20
  15.2 1.0 %constant_dynamic-update-slice_fusion.1 = f32[4,3,9,16,128]{4,3,2,1,0:T(8,128)S(1)} fusion(f32[4,3,9,16,128]{4,3,2,1,0:T(8,128)S(1)} %constant_dynamic-update-slice_fusion.2, f32[4,3,3,16,128]{4,3,2,1,0:T(8,128)} %param.4), kind=kLoop, calls=%fused_computation.99 | loop fusion | bytes 589824
  16.2 0.0 collective-permute-done.1
  16.3 0.1 fusion.27
  16.4 0.3 fusion.6
  16.8 0.0 copy-done.1
  16.8 7.5 %add_convert_fusion = bf16[3,3,10,128,256]{4,3,2,1,0:T(8,128)(2,1)S(1)} fusion(bf16[3,3,10,128,256]{4,3,2,1,0:T(8,128)(2,1)S(1)} %copy-done.1, f32[256]{0:T(256)S(1)} %bitcast.59, f32[3,3,10,128]{3,2,1,0:T(8,128)S(1)} %get-tuple-element.13, f32[256]{0:T(256)S(1)} %bitcast.60, f32[3,3,10,128]{3,2,1,0:T(8,128)S(1)} %get-tuple-element.14, f32[256]{0:T(256)S(1)} %bitcast.58, ...), kind=kLoop, calls=%fused_computation.1 | loop fusion | flops 29491200 | bytes 11984896 | tf_op jit(solution)/shard_map/convert_element_type | solution.py:190
  24.3 0.0 copy-start
  24.3 2.6 %convolution_bitcast_fusion.gram_ref = f32[256,256]{1,0:T(8,128)} fusion(bf16[3,3,10,128,256]{4,3,2,1,0:T(8,128)(2,1)S(1)} %add_convert_fusion), kind=kOutput, calls=%fused_computation.2 | convolution fusion | flops 1509949440 | bytes 6160384 | tf_op jit(solution)/shard_map/dot_general | solution.py:168
  27.0 0.0 copy-done
  27.0 1.6 %shard_map.59 = (f32[72,256]{1,0:T(8,128)}, f32[72,256]{1,0:T(8,128)}) custom-call(s32[1]{0:T(128)} %bitcast.20.parity_ref, f32[256,256]{1,0:T(8,128)} %convolution_bitcast_fusion.gram_ref), custom_call_target="tpu_custom_call" | custom-call | tf_op jit(solution)/shard_map/pallas_call | solution.py:148
  28.6 0.0 collective-permute-start.2
  28.6 1.5 %collective-permute-done.2 = f32[72,256]{1,0:T(8,128)S(1)} collective-permute-done((f32[72,256]{1,0:T(8,128)}, f32[72,256]{1,0:T(8,128)S(1)}, u32[]{:S(2)}, u32[]{:S(2)}) %collective-permute-start.2) | collective-permute-done | bytes 73760 | tf_op jit(solution)/shard_map/ppermute | solution.py:152
  30.1 0.9 %add.81 = f32[72,256]{1,0:T(8,128)S(1)} add(f32[72,256]{1,0:T(8,128)} %get-tuple-element.6, f32[72,256]{1,0:T(8,128)S(1)} %collective-permute-done.2) | non-fusion elementwise | flops 18432 | bytes 221184 | tf_op jit(solution)/shard_map/add | solution.py:152
  31.0 0.1 collective-permute-start.3
  31.1 4.3 %collective-permute-done.3 = f32[72,256]{1,0:T(8,128)S(1)} collective-permute-done((f32[72,256]{1,0:T(8,128)S(1)}, f32[72,256]{1,0:T(8,128)S(1)}, u32[]{:S(2)}, u32[]{:S(2)}) %collective-permute-start.3) | collective-permute-done | bytes 73760 | tf_op jit(solution)/shard_map/ppermute | solution.py:155
  35.4 0.1 collective-permute-start.4
  35.5 4.3 %collective-permute-done.4 = f32[72,256]{1,0:T(8,128)S(1)} collective-permute-done((f32[72,256]{1,0:T(8,128)S(1)}, f32[72,256]{1,0:T(8,128)S(1)}, u32[]{:S(2)}, u32[]{:S(2)}) %collective-permute-start.4) | collective-permute-done | bytes 73760 | tf_op jit(solution)/shard_map/ppermute | solution.py:155
  39.9 0.1 collective-permute-start.5
  39.9 5.5 %collective-permute-done.5 = f32[72,256]{1,0:T(8,128)S(1)} collective-permute-done((f32[72,256]{1,0:T(8,128)S(1)}, f32[72,256]{1,0:T(8,128)S(1)}, u32[]{:S(2)}, u32[]{:S(2)}) %collective-permute-start.5) | collective-permute-done | bytes 73760 | tf_op jit(solution)/shard_map/ppermute | solution.py:155
  45.4 0.0 copy-start.2
  45.4 0.1 collective-permute-start.6
  45.5 1.3 %collective-permute-done.6.other_ref = f32[72,256]{1,0:T(8,128)S(1)} collective-permute-done((f32[72,256]{1,0:T(8,128)S(1)}, f32[72,256]{1,0:T(8,128)S(1)}, u32[]{:S(2)}, u32[]{:S(2)}) %collective-permute-start.6) | collective-permute-done | bytes 73760 | tf_op jit(solution)/shard_map/ppermute | solution.py:157
  46.8 0.0 copy-done.2
  46.8 0.0 copy-start.3
  46.8 0.6 copy-done.3
  47.4 13.6 %shard_map.60 = (f32[256,256]{1,0:T(8,128)}, bf16[256,256]{1,0:T(8,128)(2,1)}) custom-call(s32[1]{0:T(128)} %bitcast.20.parity_ref, f32[72,256]{1,0:T(8,128)} %copy-done.2, f32[72,256]{1,0:T(8,128)} %copy-done.3), custom_call_target="tpu_custom_call" | custom-call | tf_op jit(solution)/shard_map/pallas_call | solution.py:158
  61.0 6.9 %convolution_convert_fusion = bf16[11520,256]{1,0:T(8,128)(2,1)} fusion(bf16[11520,256]{1,0:T(8,128)(2,1)} %bitcast.55, bf16[256,256]{1,0:T(8,128)(2,1)} %get-tuple-element.8), kind=kOutput, calls=%fused_computation | convolution fusion | flops 1512898560 | bytes 11927552 | tf_op jit(solution)/shard_map/dot_general | solution.py:194
  (11 shorter events, 0.2 us)
Async XLA Ops:
  0.6 15.5 %collective-permute-start.1 = (f32[4,3,3,16,128]{4,3,2,1,0:T(8,128)}, f32[4,3,3,16,128]{4,3,2,1,0:T(8,128)S(1)}, u32[]{:S(2)}, u32[]{:S(2)}) collective-permute-start(f32[4,3,3,16,128]{4,3,2,1,0:T(8,128)} %param.4), channel_id=1, source_target_pairs={{1,0},{2,1},{3,2},{4,3},{5,4},{6,5},{7,6},{8,7},{9,8},{10,9},{11,1... | collective-permute-start | bytes 884744 | tf_op jit(solution)/shard_map/ppermute | solution.py:22
  6.1 9.1 %collective-permute-start = (f32[4,3,3,16,128]{4,3,2,1,0:T(8,128)}, f32[4,3,3,16,128]{4,3,2,1,0:T(8,128)S(1)}, u32[]{:S(2)}, u32[]{:S(2)}) collective-permute-start(f32[4,3,3,16,128]{4,3,2,1,0:T(8,128)} %param.4), channel_id=1, source_target_pairs={{0,1},{1,2},{2,3},{3,4},{4,5},{5,6},{6,7},{7,8},{8,9},{9,10},{10,1... | collective-permute-start | bytes 884744 | tf_op jit(solution)/shard_map/ppermute | solution.py:20
  11.0 5.8 %copy-start.1 = (bf16[3,3,10,128,256]{4,3,2,1,0:T(8,128)(2,1)S(1)}, bf16[3,3,10,128,256]{4,3,2,1,0:T(8,128)(2,1)}, u32[]{:S(2)}) copy-start(bf16[3,3,10,128,256]{4,3,2,1,0:T(8,128)(2,1)} %param.6) | copy-start | bytes 17694724
  24.3 2.6 %copy-start = (bf16[3,3,10,128,256]{4,3,2,1,0:T(8,128)(2,1)}, bf16[3,3,10,128,256]{4,3,2,1,0:T(8,128)(2,1)S(1)}, u32[]{:S(2)}) copy-start(bf16[3,3,10,128,256]{4,3,2,1,0:T(8,128)(2,1)S(1)} %add_convert_fusion) | copy-start | bytes 17694724
  28.6 1.5 %collective-permute-start.2 = (f32[72,256]{1,0:T(8,128)}, f32[72,256]{1,0:T(8,128)S(1)}, u32[]{:S(2)}, u32[]{:S(2)}) collective-permute-start(f32[72,256]{1,0:T(8,128)} %get-tuple-element.7), channel_id=1, source_target_pairs={{0,1},{1,0},{2,3},{3,2},{4,5},{5,4},{6,7},{7,6},{8,9},{9,8},{10,11... | collective-permute-start | bytes 221192 | tf_op jit(solution)/shard_map/ppermute | solution.py:152
  31.0 4.4 %collective-permute-start.3 = (f32[72,256]{1,0:T(8,128)S(1)}, f32[72,256]{1,0:T(8,128)S(1)}, u32[]{:S(2)}, u32[]{:S(2)}) collective-permute-start(f32[72,256]{1,0:T(8,128)S(1)} %add.81), channel_id=1, source_target_pairs={{0,2},{1,3},{2,0},{3,1},{4,6},{5,7},{6,4},{7,5},{8,10},{9,11},{10,... | collective-permute-start | bytes 221192 | tf_op jit(solution)/shard_map/ppermute | solution.py:155
  35.4 4.4 %collective-permute-start.4 = (f32[72,256]{1,0:T(8,128)S(1)}, f32[72,256]{1,0:T(8,128)S(1)}, u32[]{:S(2)}, u32[]{:S(2)}) collective-permute-start(f32[72,256]{1,0:T(8,128)S(1)} %add.82), channel_id=1, source_target_pairs={{0,4},{1,5},{2,6},{3,7},{4,0},{5,1},{6,2},{7,3},{8,12},{9,13},{10,... | collective-permute-start | bytes 221192 | tf_op jit(solution)/shard_map/ppermute | solution.py:155
  39.9 5.5 %collective-permute-start.5 = (f32[72,256]{1,0:T(8,128)S(1)}, f32[72,256]{1,0:T(8,128)S(1)}, u32[]{:S(2)}, u32[]{:S(2)}) collective-permute-start(f32[72,256]{1,0:T(8,128)S(1)} %add.83), channel_id=1, source_target_pairs={{0,8},{1,9},{2,10},{3,11},{4,12},{5,13},{6,14},{7,15},{8,0},{9,1},... | collective-permute-start | bytes 221192 | tf_op jit(solution)/shard_map/ppermute | solution.py:155
  45.4 1.3 %copy-start.2 = (f32[72,256]{1,0:T(8,128)}, f32[72,256]{1,0:T(8,128)S(1)}, u32[]{:S(2)}) copy-start(f32[72,256]{1,0:T(8,128)S(1)} %add.84.mine_ref) | copy-start | bytes 221188
  45.4 1.3 %collective-permute-start.6 = (f32[72,256]{1,0:T(8,128)S(1)}, f32[72,256]{1,0:T(8,128)S(1)}, u32[]{:S(2)}, u32[]{:S(2)}) collective-permute-start(f32[72,256]{1,0:T(8,128)S(1)} %add.84.mine_ref), channel_id=1, source_target_pairs={{0,1},{1,0},{2,3},{3,2},{4,5},{5,4},{6,7},{7,6},{8,9},{9,8},{10,11... | collective-permute-start | bytes 221192 | tf_op jit(solution)/shard_map/ppermute | solution.py:157
  46.8 0.6 copy-start.3

commit v2 on v1

v2 whole, which is shorter than its diff:
```python
import functools

import jax
import jax.numpy as jnp
from jax import lax
from jax.experimental import pallas as pl
from jax.experimental.pallas import tpu as pltpu
from jax.sharding import PartitionSpec as P

COEFS = (0.75, -0.15, 1.0 / 60.0)
IN_SMEM = pl.BlockSpec(memory_space=pltpu.SMEM)
IN_VMEM = pl.BlockSpec(memory_space=pltpu.VMEM)
ANYWHERE = pl.BlockSpec(memory_space=pl.ANY)


def wall_diff(plane, count):
    total = jnp.zeros((count, plane.shape[1]), jnp.float32)
    for k, weight in zip((1, 2, 3), COEFS):
        total = total + weight * (plane[3 + k : 3 + k + count] - plane[3 - k : 3 - k + count])
    return total


def span_diff(band, edge):
    cells = band.shape[1]
    lane = lax.broadcasted_iota(jnp.int32, band.shape, 1)
    total = jnp.zeros(band.shape, jnp.float32)
    for k, weight in zip((1, 2, 3), COEFS):
        ahead = pltpu.roll(jnp.where(lane < k, edge, band), cells - k, 1)
        behind = pltpu.roll(jnp.where(lane >= cells - k, edge, band), k, 1)
        total = total + weight * (ahead - behind)
    return total


def stream_diff(planes, at):
    total = jnp.zeros(planes[0].shape, jnp.float32)
    for k, weight in zip((1, 2, 3), COEFS):
        total = total + weight * (planes[at + k] - planes[at - k])
    return total


def parts_of(x):
    high = x.astype(jnp.bfloat16).astype(jnp.float32)
    rest = x - high
    mid = rest.astype(jnp.bfloat16).astype(jnp.float32)
    return high, mid, rest - mid


def update_block(vort, omega, new_ref, acc_ref):
    snaps = len(vort)
    pad = [jnp.zeros((8 - snaps % 8, omega.shape[1]), jnp.float32)] if snaps % 8 else []
    o1, o2, o3 = parts_of(omega)
    right = jnp.concatenate([o1, o2, o1, o3, o1, o2], axis=0).astype(jnp.bfloat16)
    split = [parts_of(v) for v in vort]
    for y in range(vort[0].shape[0]):
        a, b, c = ([s[t][y : y + 1] for s in split] for t in range(3))
        left = jnp.concatenate(a + a + b + a + c + b, axis=0)
        turned = left.T.astype(jnp.bfloat16)
        gain = jnp.dot(turned, right, preferred_element_type=jnp.float32)
        new_ref[y] = (new_ref[y].astype(jnp.float32) + gain).astype(jnp.bfloat16)
    rows, cells, rank = new_ref.shape
    block = new_ref[...].reshape(rows * cells, rank)
    acc_ref[...] += lax.dot_general(block, block, (((0,), (0,)), ((), ())), preferred_element_type=jnp.float32)


def fetch(old_ref, first, new_refs, sems):
    return [
        [
            pltpu.make_async_copy(old_ref.at[first + c, i], new_ref.at[i], sems.at[c, i])
            for i in range(new_ref.shape[0])
        ]
        for c, new_ref in enumerate(new_refs)
    ]


def first_component_kernel(vel_ref, edge_ref, omega_ref, old_ref, new_ref, gram_ref, sems):
    snaps, _, slabs, height, _ = vel_ref.shape
    rows = height - 6
    copies = fetch(old_ref, 0, [new_ref], sems)[0]
    for copy in copies:
        copy.start()
    gram_ref[...] = jnp.zeros_like(gram_ref)
    for i in range(slabs):
        vort = [
            wall_diff(vel_ref[s, 2, i], rows) - span_diff(vel_ref[s, 1, i, 3 : 3 + rows], edge_ref[s, 1, i])
            for s in range(snaps)
        ]
        copies[i].wait()
        update_block(vort, omega_ref[...], new_ref.at[i], gram_ref)


def pack(gram_ref, first, keep_ref, send_ref):
    half = gram_ref.shape[0] // 2
    row = lax.broadcasted_iota(jnp.int32, (half, half), 0)
    col = lax.broadcasted_iota(jnp.int32, (half, half), 1)
    low = gram_ref[half:, half:]
    mixed = jnp.where(row <= col, gram_ref[:half, :half], low)
    diag = jnp.sum(jnp.where(row == col, low, 0.0), axis=0, keepdims=True)
    packed = jnp.concatenate([gram_ref[:half, half:], mixed], axis=1)
    part = half // 2
    extra = jnp.broadcast_to(jnp.concatenate([diag, diag], axis=1), (8, 2 * half))
    upper, lower = packed[:part], packed[part:]
    keep_ref[:part] = jnp.where(first, upper, lower)
    send_ref[:part] = jnp.where(first, lower, upper)
    keep_ref[part:] = extra
    send_ref[part:] = extra


def other_components_kernel(
    parity_ref, vel_ref, edge_ref, behind_ref, ahead_ref, omega_ref, start_ref, old_ref,
    new_y_ref, new_z_ref, keep_ref, send_ref, wide_ref, gram_ref, sems,
):
    snaps, _, slabs, height, _ = vel_ref.shape
    rows = height - 6
    new_refs = [new_y_ref, new_z_ref]
    copies = fetch(old_ref, 1, new_refs, sems)
    for i in range(slabs):
        for c in range(2):
            copies[c][i].start()
    gram_ref[...] = start_ref[...]
    for s in range(snaps):
        for c in range(2):
            for k in range(3):
                at = ((s * 2 + c) * 3 + k) * rows
                wide_ref[s, c, k] = behind_ref[at : at + rows]
                wide_ref[s, c, 3 + slabs + k] = ahead_ref[at : at + rows]
            for i in range(slabs):
                wide_ref[s, c, 3 + i] = vel_ref[s, 1 + c, i, 3 : 3 + rows]
    for i in range(slabs):
        for c in range(2):
            vort = []
            for s in range(snaps):
                along = stream_diff([wide_ref[s, 1 - c, i + k] for k in range(7)], 3)
                if c == 0:
                    vort.append(span_diff(vel_ref[s, 0, i, 3 : 3 + rows], edge_ref[s, 0, i]) - along)
                else:
                    vort.append(along - wall_diff(vel_ref[s, 0, i], rows))
            copies[c][i].wait()
            update_block(vort, omega_ref[...], new_refs[c].at[i], gram_ref)
    pack(gram_ref, parity_ref[0] == 0, keep_ref, send_ref)


def factor_invert(t_ref, u_ref, x_ref):
    order = t_ref.shape[0]
    lane = lax.broadcasted_iota(jnp.int32, (8, 128), 1)
    sub = lax.broadcasted_iota(jnp.int32, (8, 128), 0)
    full = (8, 128)
    zero = jnp.zeros(full, jnp.float32)
    for p in range(order // 8):
        j0 = 8 * p
        hd = j0 // 128
        c0 = j0 % 128
        halves = [t_ref[j0:j0 + 8, 128 * h:128 * h + 128] for h in range(2)]
        diag = halves[hd]
        in_panel = (lane >= c0) & (lane < c0 + 8)
        ident = jnp.where(lane == sub + c0, 1.0, 0.0)
        halves[hd] = jnp.where(in_panel, ident, diag)
        a = {}
        for j in range(8):
            for i in range(j + 1):
                a[i, j] = jnp.broadcast_to(diag[i:i + 1, c0 + j:c0 + j + 1], full)
        rows = [[jnp.broadcast_to(x[i:i + 1], full) for x in (halves[0], halves[1], diag)] for i in range(8)]
        l = {}
        r = [None] * 8
        rs = [None] * 8
        for k in range(8):
            r[k] = 1.0 / a[k, k]
            rs[k] = lax.rsqrt(a[k, k])
            for i in range(k + 1, 8):
                l[i, k] = a[k, i] * r[k]
            for i in range(k + 1, 8):
                for j in range(i, 8):
                    a[i, j] = a[i, j] - l[i, k] * a[k, j]
                rows[i] = [x - l[i, k] * y for x, y in zip(rows[i], rows[k])]
        z = [None] * 8
        for k in reversed(range(8)):
            zk = [rows[k][h] * r[k] for h in range(2)]
            for i in range(k + 1, 8):
                zk = [x - l[i, k] * y for x, y in zip(zk, z[i])]
            z[k] = zk
        for q in range(p + 1, order // 8):
            rr = slice(8 * q, 8 * q + 8)
            old = [t_ref[rr, 128 * h:128 * h + 128] for h in range(2)]
            m = [jnp.broadcast_to(old[hd][:, c0 + k:c0 + k + 1], full) for k in range(8)]
            acc = [old[0], old[1]]
            acc[hd] = jnp.where(in_panel, 0.0, acc[hd])
            for h in range(2):
                s = m[0] * z[0][h]
                for k in range(1, 8):
                    s = s + m[k] * z[k][h]
                t_ref[rr, 128 * h:128 * h + 128] = acc[h] - s
        outs = [zero, zero, zero]
        for k in range(8):
            outs = [jnp.where(sub == k, rows[k][c] * rs[k], outs[c]) for c in range(3)]
        for h in range(2):
            col = lane + 128 * h
            src = outs[2] if h == hd else outs[h]
            u_ref[j0:j0 + 8, 128 * h:128 * h + 128] = jnp.where(col >= sub + j0, src, 0.0)
            x_ref[j0:j0 + 8, 128 * h:128 * h + 128] = jnp.where(col <= sub + j0, outs[h], 0.0)


def unpack(packed, part_diag, work_ref):
    half = packed.shape[0]
    cross, mixed = packed[:, :half], packed[:, half:]
    row = lax.broadcasted_iota(jnp.int32, (half, half), 0)
    col = lax.broadcasted_iota(jnp.int32, (half, half), 1)
    turned = mixed.T
    diag = jnp.broadcast_to(part_diag[:, :half], (half, half))
    work_ref[:half, :half] = jnp.where(row <= col, mixed, turned)
    work_ref[:half, half:] = cross
    work_ref[half:, :half] = cross.T
    work_ref[half:, half:] = jnp.where(row > col, mixed, jnp.where(row < col, turned, diag))


def basis_kernel(
    scale, parity_ref, mine_ref, other_ref, x_ref, y_ref, z_ref, upper_ref, basis_ref,
    work_ref, solved_ref, stage_ref, sems,
):
    order = work_ref.shape[0]
    part = order // 4
    first = parity_ref[0] == 0
    mine, other = mine_ref[...] * scale, other_ref[...] * scale
    top, bottom = jnp.where(first, mine[:part], other[:part]), jnp.where(first, other[:part], mine[:part])
    unpack(jnp.concatenate([top, bottom], axis=0), mine[part : part + 1], work_ref)
    factor_invert(work_ref, upper_ref, solved_ref)
    inverse = solved_ref[...].T.astype(jnp.bfloat16)
    copies = []
    for c, sketch_ref in enumerate((x_ref, y_ref, z_ref)):
        slabs, rows, cells, rank = sketch_ref.shape
        for i in range(slabs):
            block = sketch_ref[i].reshape(rows * cells, rank)
            product = jnp.dot(block, inverse, preferred_element_type=jnp.float32)
            stage_ref[c, i] = product.astype(jnp.bfloat16).reshape(rows, cells, rank)
            copy = pltpu.make_async_copy(stage_ref.at[c, i], basis_ref.at[c, i], sems.at[c, i])
            copy.start()
            copies.append(copy)
    for copy in copies:
        copy.wait()


def local(velocity, span_rim, sketch_old, omega):
    snaps, _, slabs, height, cells = velocity.shape
    rows = height - 6
    rank = omega.shape[1]
    count = lax.axis_size("gx")
    limit = pltpu.CompilerParams(vmem_limit_bytes=24 << 20)
    place = lax.axis_index("gx")
    parity = (place % 2).reshape(1)
    band = velocity[:, 1:3, :, 3 : 3 + rows]
    tail = band[:, :, slabs - 3 :].reshape(-1, cells)
    head = band[:, :, :3].reshape(-1, cells)
    behind = lax.ppermute(tail, "gx", [(i, (i + 1) % count) for i in range(count)])
    ahead = lax.ppermute(head, "gx", [((i + 1) % count, i) for i in range(count)])
    gap = jnp.zeros((*span_rim.shape[:-1], cells - 6), jnp.float32)
    edge = jnp.concatenate([span_rim[..., 3:], gap, span_rim[..., :3]], axis=-1)
    block = (slabs, rows, cells, rank)
    sketch_x, gram = pl.pallas_call(
        first_component_kernel,
        out_shape=[pltpu.VMEM(block, jnp.bfloat16), jax.ShapeDtypeStruct((rank, rank), jnp.float32)],
        in_specs=[IN_VMEM, IN_VMEM, IN_VMEM, ANYWHERE],
        out_specs=[IN_VMEM, IN_VMEM],
        scratch_shapes=[pltpu.SemaphoreType.DMA((1, slabs))],
        compiler_params=limit,
    )(velocity, edge, omega, sketch_old)
    piece = jax.ShapeDtypeStruct((rank // 4 + 8, rank), jnp.float32)
    sketch_y, sketch_z, keep, send = pl.pallas_call(
        other_components_kernel,
        out_shape=[pltpu.VMEM(block, jnp.bfloat16), pltpu.VMEM(block, jnp.bfloat16), piece, piece],
        in_specs=[IN_SMEM] + [IN_VMEM] * 6 + [ANYWHERE],
        out_specs=[IN_VMEM] * 4,
        scratch_shapes=[
            pltpu.VMEM((snaps, 2, slabs + 6, rows, cells), jnp.float32),
            pltpu.VMEM((rank, rank), jnp.float32),
            pltpu.SemaphoreType.DMA((2, slabs)),
        ],
        compiler_params=limit,
    )(parity, velocity, edge, behind, ahead, omega, gram, sketch_old)
    swap = lambda k: [(i, i ^ k) for i in range(count)]
    total = keep + lax.ppermute(send, "gx", swap(1))
    step = 2
    while step < count:
        total = total + lax.ppermute(total, "gx", swap(step))
        step *= 2
    other = lax.ppermute(total, "gx", swap(1))
    entries = 3 * slabs * rows * cells * count
    factor, basis = pl.pallas_call(
        functools.partial(basis_kernel, 1.0 / entries),
        out_shape=[
            jax.ShapeDtypeStruct((rank, rank), jnp.float32),
            jax.ShapeDtypeStruct((3, *block), jnp.bfloat16),
        ],
        in_specs=[IN_SMEM] + [IN_VMEM] * 5,
        out_specs=[IN_VMEM, ANYWHERE],
        scratch_shapes=[
            pltpu.VMEM((rank, rank), jnp.float32),
            pltpu.VMEM((rank, rank), jnp.float32),
            pltpu.VMEM((3, *block), jnp.bfloat16),
            pltpu.SemaphoreType.DMA((3, slabs)),
        ],
        compiler_params=limit,
    )(parity, total, other, sketch_x, sketch_y, sketch_z)
    return basis, factor


def solution(mesh):
    in_specs = (
        P(None, None, ("rec", "gx"), None, None),
        P(None, None, ("rec", "gx"), None, None),
        P(None, ("rec", "gx"), None, None, None),
        P(),
    )
    out_specs = (P(None, ("rec", "gx"), None, None, None), P("rec", None))
    return jax.shard_map(local, mesh=mesh, in_specs=in_specs, out_specs=out_specs, check_vma=False)
```

time: 68.3 us -> 56.6 us (0.83)
  Pallas kernels: 15.2 us -> 26.4 us
  matrix products: 9.58 us -> 0 us
  other arithmetic: 9.3 us -> 0.16 us
  waiting for transfers between devices: 21 us -> 15.2 us
  starting transfers between devices: 5.76 us -> 7.84 us
    pallas_call x2 -> x3, Pallas kernels: 15.2 us -> 26.4 us  [the longest x1 17.7 us: local(): pl.pallas_call(functools.partial(basis_kernel, 1.0 / entries), out_shape=...]
    dot_general x2 -> x0, matrix products: 9.58 us -> none  [the longest x1 6.95 us: local(): jnp.dot(matrix, inverse_one, preferred_element_type=jnp.float32)]
    convert_element_type x1 -> x0, other arithmetic: 7.55 us -> none  [local(): sketch = sketch.astype(jnp.bfloat16)]
    ppermute x7, waiting for transfers between devices: 21 us -> 15.2 us  [the longest x3 12.7 us: local(): total = total + lax.ppermute(total, 'gx', swap(step))]
    unnamed x10 -> x8, local copies, waits for them, and re-layouts: 1.64 us -> 3.88 us
    ppermute x7, starting transfers between devices: 5.76 us -> 7.84 us  [the longest x1 5.47 us: local(): lax.ppermute(head, 'gx', [((i + 1) % count, i) for i in range(count)])]
    squeeze x4 -> x0, local copies, waits for them, and re-layouts: 2.01 us -> none  [the longest x1 0.98 us: local(): velocity[:, 2]]
    add x4, other arithmetic: 0.93 us -> 0.04 us  [the longest x3 0.03 us: local(): total = total + lax.ppermute(total, 'gx', swap(step))]
  transfers between devices with their start and end apart: 7 -> 7, of which waited for: 6 -> 5; matrix products, arithmetic and copies ran while one was open for 9% -> 3% of each run, Pallas kernels for 0% -> 5%
where the time goes in v2:
time: 56.6 us; the launch traced here: 56.3 us
  Pallas kernels  26.4 us (47%)
  waiting for transfers between devices  15.2 us (27%)
  starting transfers between devices  7.84 us (14%)
  local copies, waits for them, and re-layouts  5.79 us (10%)
  between operations  0.94 us (2%)
    pallas_call x1, Pallas kernels, local(): pl.pallas_call(functools.partial(basis_kernel, 1.0 / entries), out_shape=...  17.7 us
    ppermute x3, waiting for transfers between devices, local(): total = total + lax.ppermute(total, 'gx', swap(step))  12.7 us
    pallas_call x1, Pallas kernels, local(): pl.pallas_call(other_components_kernel, out_shape=[pltpu.VMEM(block, jnp....  5.78 us
    ppermute x1, starting transfers between devices, local(): lax.ppermute(head, 'gx', [((i + 1) % count, i) for i in range(count)])  5.47 us
    unnamed x8, local copies, waits for them, and re-layouts  3.88 us
    pallas_call x1, Pallas kernels, local(): pl.pallas_call(first_component_kernel, out_shape=[pltpu.VMEM(block, jnp.b...  2.91 us
    ppermute x3, starting transfers between devices, local(): total = total + lax.ppermute(total, 'gx', swap(step))  2.22 us
    ppermute x1, waiting for transfers between devices, local(): other = lax.ppermute(total, 'gx', swap(1))  1.25 us
  transfers between devices with their start and end apart: 7, of which 5 were waited for; matrix products, arithmetic and copies ran while one was open for 3% of the time, Pallas kernels for 5%

profile of v2, /device:TPU:0, one launch (start us, length us, event | category | flops | bytes accessed | tf_op | source)
XLA Modules:
  0.0 56.3 jit_solution(16090470269202385589)
XLA Ops:
  0.6 0.0 copy-start.1
  0.6 1.0 %slice.11 = f32[4,2,3,10,128]{4,3,2,1,0:T(8,128)S(1)} slice(f32[4,3,3,16,128]{4,3,2,1,0:T(8,128)} %vel_ref.3), slice={[0:4], [1:3], [0:3], [3:13], [0:128]} | slice | bytes 245760 | tf_op jit(solution)/shard_map/slice | solution.py:248
  1.7 5.5 %collective-permute-start.1 = (f32[240,128]{1,0:T(8,128)S(1)}, f32[240,128]{1,0:T(8,128)S(1)}, u32[]{:S(2)}, u32[]{:S(2)}) collective-permute-start(f32[240,128]{1,0:T(8,128)S(1)} %reshape.12), channel_id=1, source_target_pairs={{1,0},{2,1},{3,2},{4,3},{5,4},{6,5},{7,6},{8,7},{9,8},{10,9},{11,1... | collective-permute-start | bytes 368648 | tf_op jit(solution)/shard_map/ppermute | solution.py:252
  7.1 0.0 collective-permute-start
  7.1 0.8 %fusion = (f32[4,2,3,10,3]{3,1,4,2,0:T(2,128)S(1)}, f32[4,2,3,10,3]{3,1,4,2,0:T(2,128)S(1)}) fusion(f32[4,2,3,10,6]{3,1,4,2,0:T(2,128)} %param.5), kind=kLoop, calls=%fused_computation.1 | loop fusion | bytes 11520 | tf_op jit(solution)/shard_map/slice | solution.py:254
  8.0 0.3 copy.8
  8.2 0.3 copy.9
  8.5 0.1 pad.1.clone
  8.6 0.1 pad_maximum_fusion.edge_ref
  8.7 0.0 copy-done.1
  8.7 0.0 copy-start
  8.7 2.7 %copy-done = bf16[3,3,10,128,256]{4,3,2,1,0:T(8,128)(2,1)S(1)} copy-done((bf16[3,3,10,128,256]{4,3,2,1,0:T(8,128)(2,1)S(1)}, bf16[3,3,10,128,256]{4,3,2,1,0:T(8,128)(2,1)}, u32[]{:S(2)}) %copy-start) | copy-done | bytes 5898264
  11.4 0.0 copy-start.2
  11.4 0.7 %copy-done.2 = f32[4,256]{1,0:T(4,128)S(1)} copy-done((f32[4,256]{1,0:T(4,128)S(1)}, f32[4,256]{1,0:T(4,128)}, u32[]{:S(2)}) %copy-start.2) | copy-done | bytes 4120
  12.1 2.9 %shard_map.59 = (bf16[3,10,128,256]{3,2,1,0:T(8,128)(2,1)S(1)}, f32[256,256]{1,0:T(8,128)S(1)}) custom-call(f32[4,3,3,16,128]{4,3,2,1,0:T(8,128)S(1)} %copy-done.1, f32[4,2,3,10,128]{4,3,2,1,0:T(8,128)S(1)} %pad_maximum_fusion.edge_ref, f32[4,256]{1,0:T(4,128)S(1)} %copy-done.2, bf16[3,3,10,128,256]{4,3,2,1,0:T(8,128)(2,1)S(1)} %copy-done), custom_call_target="tpu_custom_call" | custom-call | tf_op jit(solution)/shard_map/pallas_call | solution.py:256
  15.0 0.0 collective-permute-done.1.ahead_ref
  15.0 0.0 collective-permute-done.behind_ref
  15.0 5.8 %shard_map.60 = (bf16[3,10,128,256]{3,2,1,0:T(8,128)(2,1)S(1)}, bf16[3,10,128,256]{3,2,1,0:T(8,128)(2,1)S(1)}, f32[72,256]{1,0:T(8,128)S(1)}, f32[72,256]{1,0:T(8,128)S(1)}) custom-call(s32[1]{0:T(128)} %bitcast.parity_ref, f32[4,3,3,16,128]{4,3,2,1,0:T(8,128)S(1)} %copy-done.1, f32[4,2,3,10,128]{4,3,2,1,0:T(8,128)S(1)} %pad_maximum_fusion.edge_ref, ...), custom_call_target="tpu_custom_call" | custom-call | tf_op jit(solution)/shard_map/pallas_call | solution.py:265
  20.8 0.1 collective-permute-start.2
  20.9 1.3 %collective-permute-done.2 = f32[72,256]{1,0:T(8,128)S(1)} collective-permute-done((f32[72,256]{1,0:T(8,128)S(1)}, f32[72,256]{1,0:T(8,128)S(1)}, u32[]{:S(2)}, u32[]{:S(2)}) %collective-permute-start.2) | collective-permute-done | bytes 73760 | tf_op jit(solution)/shard_map/ppermute | solution.py:278
  22.1 0.1 collective-permute-start.3
  22.2 4.3 %collective-permute-done.3 = f32[72,256]{1,0:T(8,128)S(1)} collective-permute-done((f32[72,256]{1,0:T(8,128)S(1)}, f32[72,256]{1,0:T(8,128)S(1)}, u32[]{:S(2)}, u32[]{:S(2)}) %collective-permute-start.3) | collective-permute-done | bytes 73760 | tf_op jit(solution)/shard_map/ppermute | solution.py:281
  26.6 0.1 collective-permute-start.4
  26.6 4.3 %collective-permute-done.4 = f32[72,256]{1,0:T(8,128)S(1)} collective-permute-done((f32[72,256]{1,0:T(8,128)S(1)}, f32[72,256]{1,0:T(8,128)S(1)}, u32[]{:S(2)}, u32[]{:S(2)}) %collective-permute-start.4) | collective-permute-done | bytes 73760 | tf_op jit(solution)/shard_map/ppermute | solution.py:281
  31.0 2.1 %collective-permute-start.5 = (f32[72,256]{1,0:T(8,128)S(1)}, f32[72,256]{1,0:T(8,128)S(1)}, u32[]{:S(2)}, u32[]{:S(2)}) collective-permute-start(f32[72,256]{1,0:T(8,128)S(1)} %add.19), channel_id=1, source_target_pairs={{0,8},{1,9},{2,10},{3,11},{4,12},{5,13},{6,14},{7,15},{8,0},{9,1},... | collective-permute-start | bytes 221192 | tf_op jit(solution)/shard_map/ppermute | solution.py:281
  33.1 4.0 %collective-permute-done.5 = f32[72,256]{1,0:T(8,128)S(1)} collective-permute-done((f32[72,256]{1,0:T(8,128)S(1)}, f32[72,256]{1,0:T(8,128)S(1)}, u32[]{:S(2)}, u32[]{:S(2)}) %collective-permute-start.5) | collective-permute-done | bytes 73760 | tf_op jit(solution)/shard_map/ppermute | solution.py:281
  37.1 0.1 collective-permute-start.6
  37.2 1.3 %collective-permute-done.6.other_ref = f32[72,256]{1,0:T(8,128)S(1)} collective-permute-done((f32[72,256]{1,0:T(8,128)S(1)}, f32[72,256]{1,0:T(8,128)S(1)}, u32[]{:S(2)}, u32[]{:S(2)}) %collective-permute-start.6) | collective-permute-done | bytes 73760 | tf_op jit(solution)/shard_map/ppermute | solution.py:283
  38.4 17.7 %shard_map.61 = (f32[256,256]{1,0:T(8,128)}, bf16[3,3,10,128,256]{4,3,2,1,0:T(8,128)(2,1)}) custom-call(s32[1]{0:T(128)} %bitcast.parity_ref, f32[72,256]{1,0:T(8,128)S(1)} %add.20.mine_ref, f32[72,256]{1,0:T(8,128)S(1)} %collective-permute-done.6.other_ref, bf16[3,10,128,256]{3,2,1,0:T(8,128)(2,1)S(1)} %get-tuple-element.13.x_ref, ...), custom_call_target="tpu_custom_call" | custom-call | tf_op jit(solution)/shard_map/pallas_call | solution.py:285
  (6 shorter events, 0.1 us)
Async XLA Ops:
  0.6 8.1 %copy-start.1 = (f32[4,3,3,16,128]{4,3,2,1,0:T(8,128)S(1)}, f32[4,3,3,16,128]{4,3,2,1,0:T(8,128)}, u32[]{:S(2)}) copy-start(f32[4,3,3,16,128]{4,3,2,1,0:T(8,128)} %vel_ref.3) | copy-start | bytes 884740
  1.7 13.3 %collective-permute-start.1 = (f32[240,128]{1,0:T(8,128)S(1)}, f32[240,128]{1,0:T(8,128)S(1)}, u32[]{:S(2)}, u32[]{:S(2)}) collective-permute-start(f32[240,128]{1,0:T(8,128)S(1)} %reshape.12), channel_id=1, source_target_pairs={{1,0},{2,1},{3,2},{4,3},{5,4},{6,5},{7,6},{8,7},{9,8},{10,9},{11,1... | collective-permute-start | bytes 368648 | tf_op jit(solution)/shard_map/ppermute | solution.py:252
  7.1 7.8 %collective-permute-start = (f32[240,128]{1,0:T(8,128)S(1)}, f32[240,128]{1,0:T(8,128)S(1)}, u32[]{:S(2)}, u32[]{:S(2)}) collective-permute-start(f32[240,128]{1,0:T(8,128)S(1)} %reshape.12), channel_id=1, source_target_pairs={{0,1},{1,2},{2,3},{3,4},{4,5},{5,6},{6,7},{7,8},{8,9},{9,10},{10,1... | collective-permute-start | bytes 368648 | tf_op jit(solution)/shard_map/ppermute | solution.py:251
  8.7 2.7 %copy-start = (bf16[3,3,10,128,256]{4,3,2,1,0:T(8,128)(2,1)S(1)}, bf16[3,3,10,128,256]{4,3,2,1,0:T(8,128)(2,1)}, u32[]{:S(2)}) copy-start(bf16[3,3,10,128,256]{4,3,2,1,0:T(8,128)(2,1)} %old_ref.3) | copy-start | bytes 17694724
  11.4 0.7 %copy-start.2 = (f32[4,256]{1,0:T(4,128)S(1)}, f32[4,256]{1,0:T(4,128)}, u32[]{:S(2)}) copy-start(f32[4,256]{1,0:T(4,128)} %omega_ref.3) | copy-start | bytes 12292
  20.8 1.3 %collective-permute-start.2 = (f32[72,256]{1,0:T(8,128)S(1)}, f32[72,256]{1,0:T(8,128)S(1)}, u32[]{:S(2)}, u32[]{:S(2)}) collective-permute-start(f32[72,256]{1,0:T(8,128)S(1)} %get-tuple-element.12), channel_id=1, source_target_pairs={{0,1},{1,0},{2,3},{3,2},{4,5},{5,4},{6,7},{7,6},{8,9},{9,8},{10,11... | collective-permute-start | bytes 221192 | tf_op jit(solution)/shard_map/ppermute | solution.py:278
  22.1 4.4 %collective-permute-start.3 = (f32[72,256]{1,0:T(8,128)S(1)}, f32[72,256]{1,0:T(8,128)S(1)}, u32[]{:S(2)}, u32[]{:S(2)}) collective-permute-start(f32[72,256]{1,0:T(8,128)S(1)} %add.17), channel_id=1, source_target_pairs={{0,2},{1,3},{2,0},{3,1},{4,6},{5,7},{6,4},{7,5},{8,10},{9,11},{10,... | collective-permute-start | bytes 221192 | tf_op jit(solution)/shard_map/ppermute | solution.py:281
  26.6 4.4 %collective-permute-start.4 = (f32[72,256]{1,0:T(8,128)S(1)}, f32[72,256]{1,0:T(8,128)S(1)}, u32[]{:S(2)}, u32[]{:S(2)}) collective-permute-start(f32[72,256]{1,0:T(8,128)S(1)} %add.18), channel_id=1, source_target_pairs={{0,4},{1,5},{2,6},{3,7},{4,0},{5,1},{6,2},{7,3},{8,12},{9,13},{10,... | collective-permute-start | bytes 221192 | tf_op jit(solution)/shard_map/ppermute | solution.py:281
  31.0 6.1 %collective-permute-start.5 = (f32[72,256]{1,0:T(8,128)S(1)}, f32[72,256]{1,0:T(8,128)S(1)}, u32[]{:S(2)}, u32[]{:S(2)}) collective-permute-start(f32[72,256]{1,0:T(8,128)S(1)} %add.19), channel_id=1, source_target_pairs={{0,8},{1,9},{2,10},{3,11},{4,12},{5,13},{6,14},{7,15},{8,0},{9,1},... | collective-permute-start | bytes 221192 | tf_op jit(solution)/shard_map/ppermute | solution.py:281
  37.1 1.3 %collective-permute-start.6 = (f32[72,256]{1,0:T(8,128)S(1)}, f32[72,256]{1,0:T(8,128)S(1)}, u32[]{:S(2)}, u32[]{:S(2)}) collective-permute-start(f32[72,256]{1,0:T(8,128)S(1)} %add.20.mine_ref), channel_id=1, source_target_pairs={{0,1},{1,0},{2,3},{3,2},{4,5},{5,4},{6,7},{7,6},{8,9},{9,8},{10,11... | collective-permute-start | bytes 221192 | tf_op jit(solution)/shard_map/ppermute | solution.py:283

commit v3 on v2

v3 whole, which is shorter than its diff:
```python
import functools

import jax
import jax.numpy as jnp
from jax import lax
from jax.experimental import pallas as pl
from jax.experimental.pallas import tpu as pltpu
from jax.sharding import PartitionSpec as P

COEFS = (0.75, -0.15, 1.0 / 60.0)
IN_SMEM = pl.BlockSpec(memory_space=pltpu.SMEM)
IN_VMEM = pl.BlockSpec(memory_space=pltpu.VMEM)
IN_HBM = pl.BlockSpec(memory_space=pltpu.HBM)
WIDE = 64


def parts_of(x):
    high = x.astype(jnp.bfloat16).astype(jnp.float32)
    rest = x - high
    mid = rest.astype(jnp.bfloat16).astype(jnp.float32)
    return high, mid, rest - mid


def eliminate_below(t_ref, upper, solved, stop):
    order = t_ref.shape[0]
    col = lax.broadcasted_iota(jnp.int32, upper.shape, 1)
    v, w, y = parts_of(jnp.where(col < stop, solved, upper))
    right = jnp.concatenate([v, w, v, y, v, w], axis=0).astype(jnp.bfloat16)
    for base in range(stop // 128 * 128, order, 128):
        a, b, c = parts_of(upper[:, base : base + 128])
        left = jnp.concatenate([a, a, b, a, c, b], axis=0).astype(jnp.bfloat16)
        product = lax.dot_general(left, right, (((0,), (0,)), ((), ())), preferred_element_type=jnp.float32)
        for top in range(max(base, stop), base + 128, WIDE):
            kept = jnp.where((col >= stop - WIDE) & (col < stop), 0.0, t_ref[top : top + WIDE])
            t_ref[top : top + WIDE] = kept - product[top - base : top - base + WIDE]


def factor_block(w_ref, off):
    full = (8, 128)
    sub = lax.broadcasted_iota(jnp.int32, full, 0)
    for j0 in range(0, WIDE, 8):
        c0 = off + j0
        now = w_ref[j0 : j0 + 8]
        rows = [w_ref[pl.ds(j0 + i, 8, stride=0), :] for i in range(8)]
        a = {}
        for j in range(8):
            for i in range(j + 1):
                a[i, j] = jnp.broadcast_to(rows[i][:, c0 + j : c0 + j + 1], full)
        left, scaled, final = {}, {}, {}
        for k in range(0, 8, 2):
            n = k + 1
            top, mid, low = a[k, k], a[k, n], a[n, n]
            rdet = 1.0 / (top * low - mid * mid)
            for i in range(k + 2, 8):
                left[k, i] = (low * a[k, i] - mid * a[n, i]) * rdet
                left[n, i] = (top * a[n, i] - mid * a[k, i]) * rdet
            for i in range(k + 2, 8):
                for j in range(i, 8):
                    a[i, j] = a[i, j] - left[k, i] * a[k, j] - left[n, i] * a[n, j]
                rows[i] = rows[i] - left[k, i] * rows[k] - left[n, i] * rows[n]
            scaled[k] = (low * rows[k] - mid * rows[n]) * rdet
            scaled[n] = (top * rows[n] - mid * rows[k]) * rdet
            root = lax.rsqrt(top)
            ratio = mid * root * root
            final[k] = rows[k] * root
            final[n] = (rows[n] - ratio * rows[k]) * lax.rsqrt(low - mid * ratio)
        for k in reversed(range(8)):
            for i in reversed(range(k // 2 * 2 + 2, 8)):
                scaled[k] = scaled[k] - left[k, i] * scaled[i]
        for q in range(j0 + 8, WIDE, 8):
            old = w_ref[q : q + 8]
            rest = old
            for k in reversed(range(8)):
                rest = rest - jnp.broadcast_to(old[:, c0 + k : c0 + k + 1], full) * scaled[k]
            w_ref[q : q + 8] = rest
        out = final[0]
        for k in range(1, 8):
            out = jnp.where(sub == k, final[k], out)
        w_ref[j0 : j0 + 8] = out


def factor_invert(t_ref, u_ref, x_ref, w_ref):
    order = t_ref.shape[0]
    lane = lax.broadcasted_iota(jnp.int32, (WIDE, 128), 1)
    sub = lax.broadcasted_iota(jnp.int32, (WIDE, 128), 0)
    for b0 in range(0, order, WIDE):
        stop = b0 + WIDE
        half, off = b0 // 128, b0 % 128
        inside = (lane >= off) & (lane < off + WIDE)
        here = slice(128 * half, 128 * half + 128)
        w_ref[...] = jnp.where(inside, t_ref[b0:stop, here], jnp.where(lane == sub + (WIDE - off), 1.0, 0.0))
        factor_block(w_ref, off)
        done = w_ref[...]
        moved = pltpu.roll(done, 64, 1)
        low, high = (moved, done) if off == 0 else (done, moved)
        x1, x2, x3 = parts_of(low)
        y1, y2, _ = parts_of(high)
        r1, r2, r3 = parts_of(t_ref[b0:stop])
        pair = lambda p, q: jnp.where(lane < WIDE, p, q)
        first = jnp.concatenate([pair(x1, y1), pair(x2, y1), pair(x3, y2)], axis=1).astype(jnp.bfloat16)
        second = jnp.concatenate([r1, r2, r1, r3, r1, r2], axis=0).astype(jnp.bfloat16)
        rows = jnp.dot(first, second, preferred_element_type=jnp.float32)
        upper, solved = [], []
        for h in range(order // 128):
            wide = rows[:, 128 * h : 128 * h + 128]
            zero = jnp.zeros_like(wide)
            if h == half:
                upper.append(jnp.where(inside, jnp.where(lane - off >= sub, done, 0.0), jnp.where(lane >= off + WIDE, wide, 0.0)))
                solved.append(jnp.where(inside, moved, jnp.where(lane < off, wide, 0.0)))
            else:
                upper.append(wide if h > half else zero)
                solved.append(wide if h < half else zero)
        upper, solved = jnp.concatenate(upper, axis=1), jnp.concatenate(solved, axis=1)
        u_ref[b0:stop] = upper
        x_ref[b0:stop] = solved
        if stop < order:
            eliminate_below(t_ref, upper, solved, stop)


def wall_diff(plane, count):
    total = jnp.zeros((count, plane.shape[1]), jnp.float32)
    for k, weight in zip((1, 2, 3), COEFS):
        total = total + weight * (plane[3 + k : 3 + k + count] - plane[3 - k : 3 - k + count])
    return total


def span_diff(band, edges):
    past, before = edges
    cells = band.shape[1]
    lane = lax.broadcasted_iota(jnp.int32, band.shape, 1)
    total = jnp.zeros(band.shape, jnp.float32)
    for k, weight in zip((1, 2, 3), COEFS):
        ahead = pltpu.roll(jnp.where(lane < k, past, band), cells - k, 1)
        behind = pltpu.roll(jnp.where(lane >= cells - k, before, band), k, 1)
        total = total + weight * (ahead - behind)
    return total


def stream_diff(planes, at):
    total = jnp.zeros(planes[0].shape, jnp.float32)
    for k, weight in zip((1, 2, 3), COEFS):
        total = total + weight * (planes[at + k] - planes[at - k])
    return total


def span_edges(rim_ref, which, turn_ref):
    snaps, slabs, _, _, rows = rim_ref.shape
    groups = [(s, i) for s in range(snaps) for i in range(slabs)]
    room = turn_ref.shape[0]
    edges = {}
    for start in range(0, len(groups), room // 8):
        some = groups[start : start + room // 8]
        turn_ref[...] = jnp.zeros_like(turn_ref)
        for g, (s, i) in enumerate(some):
            for at, entry in enumerate((3, 4, 5, None, None, 0, 1, 2)):
                if entry is not None:
                    turn_ref[8 * g + at : 8 * g + at + 1, :rows] = rim_ref[s, i, entry, which : which + 1, :]
        turned = turn_ref[...].T[:rows]
        for g, key in enumerate(some):
            edges[key] = (
                pltpu.roll(turned, (room - 8 * g) % room, 1),
                pltpu.roll(turned, (room - 8 - 8 * g) % room, 1),
            )
    return edges


def gain_matrix(omega, rows):
    snaps, rank = omega.shape
    high = omega.astype(jnp.bfloat16).astype(jnp.float32)
    low = omega - high
    pieces = [jnp.broadcast_to(part[s : s + 1], (rows, rank)) for part in (high, high, low) for s in range(snaps)]
    depth = 3 * snaps * rows
    pieces.append(jnp.zeros((-depth % 128, rank), jnp.float32))
    return jnp.concatenate(pieces, axis=0).astype(jnp.bfloat16)


def update_block(vort, right, new_ref, acc_ref):
    rows, cells, rank = new_ref.shape
    high = [v.astype(jnp.bfloat16).astype(jnp.float32) for v in vort]
    low = [v - h for v, h in zip(vort, high)]
    depth = right.shape[0]
    rest = jnp.zeros((depth - 3 * rows * len(vort), cells), jnp.float32)
    turned = jnp.concatenate(high + low + high + [rest], axis=0).T.astype(jnp.bfloat16)
    lane = lax.broadcasted_iota(jnp.int32, (1, depth), 1)
    for y in range(rows):
        mask = jnp.where(lax.rem(lane, rows) == y, 1.0, 0.0).astype(jnp.bfloat16)
        gain = jnp.dot(turned * mask, right, preferred_element_type=jnp.float32)
        new_ref[y] = (new_ref[y].astype(jnp.float32) + gain).astype(jnp.bfloat16)
    block = new_ref[...].reshape(rows * cells, rank)
    acc_ref[...] += lax.dot_general(block, block, (((0,), (0,)), ((), ())), preferred_element_type=jnp.float32)


def first_component_kernel(
    vel_in, rim_in, omega_in, old_ref,
    x_ref, y_ref, z_ref, gram_ref, vel_ref, rim_ref, omega_ref, turn_ref, small_sems, sems,
):
    small = [
        pltpu.make_async_copy(source, target, small_sems.at[n])
        for n, (source, target) in enumerate(((rim_in, rim_ref), (omega_in, omega_ref), (vel_in, vel_ref)))
    ]
    for copy in small:
        copy.start()
    snaps, _, slabs, height, _ = vel_ref.shape
    rows = height - 6
    copies = [
        [pltpu.make_async_copy(old_ref.at[c, i], new_ref.at[i], sems.at[c, i]) for i in range(slabs)]
        for c, new_ref in enumerate((x_ref, y_ref, z_ref))
    ]
    for row in copies:
        for copy in row:
            copy.start()
    gram_ref[...] = jnp.zeros_like(gram_ref)
    for copy in small:
        copy.wait()
    right = gain_matrix(omega_ref[...], rows)
    edges = span_edges(rim_ref, 1, turn_ref)
    for i in range(slabs):
        vort = [
            wall_diff(vel_ref[s, 2, i], rows) - span_diff(vel_ref[s, 1, i, 3 : 3 + rows], edges[s, i])
            for s in range(snaps)
        ]
        copies[0][i].wait()
        update_block(vort, right, x_ref.at[i], gram_ref)
    for row in copies[1:]:
        for copy in row:
            copy.wait()


def pack(gram_ref, first, keep_ref, send_ref):
    half = gram_ref.shape[0] // 2
    row = lax.broadcasted_iota(jnp.int32, (half, half), 0)
    col = lax.broadcasted_iota(jnp.int32, (half, half), 1)
    low = gram_ref[half:, half:]
    mixed = jnp.where(row <= col, gram_ref[:half, :half], low)
    diag = jnp.sum(jnp.where(row == col, low, 0.0), axis=0, keepdims=True)
    packed = jnp.concatenate([gram_ref[:half, half:], mixed], axis=1)
    part = half // 2
    extra = jnp.broadcast_to(jnp.concatenate([diag, diag], axis=1), (8, 2 * half))
    upper, lower = packed[:part], packed[part:]
    keep_ref[:part] = jnp.where(first, upper, lower)
    send_ref[:part] = jnp.where(first, lower, upper)
    keep_ref[part:] = extra
    send_ref[part:] = extra


def other_components_kernel(
    parity_ref, vel_ref, rim_ref, behind_ref, ahead_ref, omega_ref, start_ref, old_y_ref, old_z_ref,
    y_ref, z_ref, keep_ref, send_ref, wide_ref, gram_ref, turn_ref,
):
    del old_y_ref, old_z_ref
    snaps, _, slabs, height, _ = vel_ref.shape
    rows = height - 6
    gram_ref[...] = start_ref[...]
    right = gain_matrix(omega_ref[...], rows)
    edges = span_edges(rim_ref, 0, turn_ref)
    for s in range(snaps):
        for c in range(2):
            for k in range(3):
                at = ((s * 2 + c) * 3 + k) * rows
                wide_ref[s, c, k] = behind_ref[at : at + rows]
                wide_ref[s, c, 3 + slabs + k] = ahead_ref[at : at + rows]
            for i in range(slabs):
                wide_ref[s, c, 3 + i] = vel_ref[s, 1 + c, i, 3 : 3 + rows]
    for i in range(slabs):
        for c, new_ref in enumerate((y_ref, z_ref)):
            vort = []
            for s in range(snaps):
                along = stream_diff([wide_ref[s, 1 - c, i + k] for k in range(7)], 3)
                if c == 0:
                    vort.append(span_diff(vel_ref[s, 0, i, 3 : 3 + rows], edges[s, i]) - along)
                else:
                    vort.append(along - wall_diff(vel_ref[s, 0, i], rows))
            update_block(vort, right, new_ref.at[i], gram_ref)
    pack(gram_ref, parity_ref[0] == 0, keep_ref, send_ref)


def unpack(packed, part_diag, work_ref):
    half = packed.shape[0]
    cross, mixed = packed[:, :half], packed[:, half:]
    row = lax.broadcasted_iota(jnp.int32, (half, half), 0)
    col = lax.broadcasted_iota(jnp.int32, (half, half), 1)
    turned = mixed.T
    diag = jnp.broadcast_to(part_diag[:, :half], (half, half))
    work_ref[:half, :half] = jnp.where(row <= col, mixed, turned)
    work_ref[:half, half:] = cross
    work_ref[half:, :half] = cross.T
    work_ref[half:, half:] = jnp.where(row > col, mixed, jnp.where(row < col, turned, diag))


def basis_kernel(
    scale, parity_ref, mine_ref, other_ref, x_ref, y_ref, z_ref, upper_ref, basis_ref,
    work_ref, solved_ref, block_ref, stage_ref, sems,
):
    order = work_ref.shape[0]
    part = order // 4
    first = parity_ref[0] == 0
    mine, other = mine_ref[...] * scale, other_ref[...] * scale
    top, bottom = jnp.where(first, mine[:part], other[:part]), jnp.where(first, other[:part], mine[:part])
    unpack(jnp.concatenate([top, bottom], axis=0), mine[part : part + 1], work_ref)
    factor_invert(work_ref, upper_ref, solved_ref, block_ref)
    inverse = solved_ref[...].T.astype(jnp.bfloat16)
    copies = []
    for c, sketch_ref in enumerate((x_ref, y_ref, z_ref)):
        slabs, rows, cells, rank = sketch_ref.shape
        for i in range(slabs):
            block = sketch_ref[i].reshape(rows * cells, rank)
            product = jnp.dot(block, inverse, preferred_element_type=jnp.float32)
            stage_ref[c, i] = product.astype(jnp.bfloat16).reshape(rows, cells, rank)
            copy = pltpu.make_async_copy(stage_ref.at[c, i], basis_ref.at[c, i], sems.at[c, i])
            copy.start()
            copies.append(copy)
    for copy in copies:
        copy.wait()


def local(velocity, span_rim, sketch_old, omega):
    snaps, _, slabs, height, cells = velocity.shape
    rows = height - 6
    rank = omega.shape[1]
    count = lax.axis_size("gx")
    limit = pltpu.CompilerParams(vmem_limit_bytes=24 << 20)
    place = lax.axis_index("gx")
    parity = (place % 2).reshape(1)
    band = velocity[:, 1:3, :, 3 : 3 + rows]
    tail = band[:, :, slabs - 3 :].reshape(-1, cells)
    head = band[:, :, :3].reshape(-1, cells)
    behind = lax.ppermute(tail, "gx", [(i, (i + 1) % count) for i in range(count)])
    ahead = lax.ppermute(head, "gx", [((i + 1) % count, i) for i in range(count)])
    rim = span_rim.transpose(0, 2, 4, 1, 3)
    block = (slabs, rows, cells, rank)
    square = jax.ShapeDtypeStruct((rank, rank), jnp.float32)
    held = pltpu.VMEM(block, jnp.bfloat16)
    inputs = [velocity, rim, omega, sketch_old]
    sketch_x, raw_y, raw_z, gram, near_vel, near_rim, near_omega = pl.pallas_call(
        first_component_kernel,
        out_shape=[held, held, held, square] + [pltpu.VMEM(x.shape, x.dtype) for x in inputs[:3]],
        in_specs=[IN_HBM] * 4,
        out_specs=[IN_VMEM] * 7,
        scratch_shapes=[
            pltpu.VMEM((128, 128), jnp.float32),
            pltpu.SemaphoreType.DMA((3,)),
            pltpu.SemaphoreType.DMA((3, slabs)),
        ],
        compiler_params=limit,
    )(*(pltpu.with_memory_space_constraint(x, pltpu.HBM) for x in inputs))
    piece = jax.ShapeDtypeStruct((rank // 4 + 8, rank), jnp.float32)
    sketch_y, sketch_z, keep, send = pl.pallas_call(
        other_components_kernel,
        out_shape=[held, held, piece, piece],
        in_specs=[IN_SMEM] + [IN_VMEM] * 8,
        out_specs=[IN_VMEM] * 4,
        scratch_shapes=[
            pltpu.VMEM((snaps, 2, slabs + 6, rows, cells), jnp.float32),
            pltpu.VMEM((rank, rank), jnp.float32),
            pltpu.VMEM((128, 128), jnp.float32),
        ],
        input_output_aliases={7: 0, 8: 1},
        compiler_params=limit,
    )(parity, near_vel, near_rim, behind, ahead, near_omega, gram, raw_y, raw_z)
    swap = lambda k: [(i, i ^ k) for i in range(count)]
    total = keep + lax.ppermute(send, "gx", swap(1))
    step = 2
    while step < count:
        total = total + lax.ppermute(total, "gx", swap(step))
        step *= 2
    other = lax.ppermute(total, "gx", swap(1))
    entries = 3 * slabs * rows * cells * count
    factor, basis = pl.pallas_call(
        functools.partial(basis_kernel, 1.0 / entries),
        out_shape=[square, jax.ShapeDtypeStruct((3, *block), jnp.bfloat16)],
        in_specs=[IN_SMEM] + [IN_VMEM] * 5,
        out_specs=[IN_VMEM, IN_HBM],
        scratch_shapes=[
            pltpu.VMEM((rank, rank), jnp.float32),
            pltpu.VMEM((rank, rank), jnp.float32),
            pltpu.VMEM((WIDE, 128), jnp.float32),
            pltpu.VMEM((3, *block), jnp.bfloat16),
            pltpu.SemaphoreType.DMA((3, slabs)),
        ],
        compiler_params=limit,
    )(parity, total, other, sketch_x, sketch_y, sketch_z)
    return basis, factor


def solution(mesh):
    in_specs = (
        P(None, None, ("rec", "gx"), None, None),
        P(None, None, ("rec", "gx"), None, None),
        P(None, ("rec", "gx"), None, None, None),
        P(),
    )
    out_specs = (P(None, ("rec", "gx"), None, None, None), P("rec", None))
    return jax.shard_map(local, mesh=mesh, in_specs=in_specs, out_specs=out_specs, check_vma=False)
```

time: 56.6 us -> 45.5 us (0.80)
  Pallas kernels: 26.4 us -> 19.2 us
  local copies, waits for them, and re-layouts: 5.79 us -> 0.97 us
  waiting for transfers between devices: 15.2 us -> 18.6 us
  starting transfers between devices: 7.84 us -> 5.89 us
    pallas_call x1, Pallas kernels: 17.7 us -> 11.2 us  [local(): pl.pallas_call(functools.partial(basis_kernel, 1.0 / entries), out_shape=...]
    unnamed x8 -> x0, local copies, waits for them, and re-layouts: 3.88 us -> none
    ppermute x1, waiting for transfers between devices: 0.01 us -> 1.97 us  [local(): lax.ppermute(tail, 'gx', [(i, (i + 1) % count) for i in range(count)])]
    ppermute x3, starting transfers between devices: 2.22 us -> 0.28 us  [local(): total = total + lax.ppermute(total, 'gx', swap(step))]
    ppermute x3, waiting for transfers between devices: 12.7 us -> 14.1 us  [local(): total = total + lax.ppermute(total, 'gx', swap(step))]
    slice x1 -> x0, local copies, waits for them, and re-layouts: 0.8 us -> none  [local(): edge = jnp.concatenate([span_rim[..., 3:], gap, span_rim[..., :3]], axis=-1)]
    pallas_call x2, Pallas kernels: 8.69 us -> 8.04 us  [the longest x1 5.01 us: local(): pl.pallas_call(first_component_kernel, out_shape=[held, held, held, squar...]
  transfers between devices with their start and end apart: 7 -> 7, of which waited for: 5 -> 6; matrix products, arithmetic and copies ran while one was open for 3% -> 0% of each run, Pallas kernels for 5% -> 11%
where the time goes in v3:
time: 45.5 us; the launch traced here: 45.4 us
  Pallas kernels  19.2 us (42%)
  waiting for transfers between devices  18.6 us (41%)
  starting transfers between devices  5.89 us (13%)
  local copies, waits for them, and re-layouts  0.97 us (2%)
  between operations  0.71 us (2%)
    ppermute x3, waiting for transfers between devices, local(): total = total + lax.ppermute(total, 'gx', swap(step))  14.1 us
    pallas_call x1, Pallas kernels, local(): pl.pallas_call(functools.partial(basis_kernel, 1.0 / entries), out_shape=...  11.2 us
    ppermute x1, starting transfers between devices, local(): lax.ppermute(head, 'gx', [((i + 1) % count, i) for i in range(count)])  5.47 us
    pallas_call x1, Pallas kernels, local(): pl.pallas_call(first_component_kernel, out_shape=[held, held, held, squar...  5.01 us
    pallas_call x1, Pallas kernels, local(): pl.pallas_call(other_components_kernel, out_shape=[held, held, piece, pie...  3.02 us
    ppermute x1, waiting for transfers between devices, local(): lax.ppermute(tail, 'gx', [(i, (i + 1) % count) for i in range(count)])  1.97 us
    ppermute x1, waiting for transfers between devices, local(): total = keep + lax.ppermute(send, 'gx', swap(1))  1.25 us
    ppermute x1, waiting for transfers between devices, local(): other = lax.ppermute(total, 'gx', swap(1))  1.25 us
  transfers between devices with their start and end apart: 7, of which 6 were waited for; matrix products, arithmetic and copies ran while one was open for 0% of the time, Pallas kernels for 11%

profile of v3, /device:TPU:0, one launch (start us, length us, event | category | flops | bytes accessed | tf_op | source)
XLA Modules:
  0.0 45.4 jit_solution(7816150670777699611)
XLA Ops:
  0.6 1.0 %slice.3 = f32[4,2,3,10,128]{4,3,2,1,0:T(8,128)S(1)} slice(f32[4,3,3,16,128]{4,3,2,1,0:T(8,128)} %vel_in.1), slice={[0:4], [1:3], [0:3], [3:13], [0:128]} | slice | bytes 245760 | tf_op jit(solution)/shard_map/slice | solution.py:324
  1.6 5.5 %collective-permute-start.1 = (f32[240,128]{1,0:T(8,128)S(1)}, f32[240,128]{1,0:T(8,128)S(1)}, u32[]{:S(2)}, u32[]{:S(2)}) collective-permute-start(f32[240,128]{1,0:T(8,128)S(1)} %reshape.12), channel_id=1, source_target_pairs={{1,0},{2,1},{3,2},{4,3},{5,4},{6,5},{7,6},{8,7},{9,8},{10,9},{11,1... | collective-permute-start | bytes 368648 | tf_op jit(solution)/shard_map/ppermute | solution.py:328
  7.1 0.0 collective-permute-start
  7.1 5.0 %shard_map.59 = (bf16[3,10,128,256]{3,2,1,0:T(8,128)(2,1)S(1)}, bf16[3,10,128,256]{3,2,1,0:T(8,128)(2,1)S(1)}, bf16[3,10,128,256]{3,2,1,0:T(8,128)(2,1)S(1)}, f3...) custom-call(f32[4,3,3,16,128]{4,3,2,1,0:T(8,128)} %vel_in.1, ...), custom_call_target="tpu_custom_call" | custom-call | tf_op jit(solution)/shard_map/pallas_call | solution.py:334
  12.1 0.0 collective-permute-done.1.ahead_ref
  12.1 2.0 %collective-permute-done.behind_ref = f32[240,128]{1,0:T(8,128)S(1)} collective-permute-done((f32[240,128]{1,0:T(8,128)S(1)}, f32[240,128]{1,0:T(8,128)S(1)}, u32[]{:S(2)}, u32[]{:S(2)}) %collective-permute-start) | collective-permute-done | bytes 122912 | tf_op jit(solution)/shard_map/ppermute | solution.py:327
  14.1 3.0 %shard_map.60 = (bf16[3,10,128,256]{3,2,1,0:T(8,128)(2,1)S(1)}, bf16[3,10,128,256]{3,2,1,0:T(8,128)(2,1)S(1)}, f32[72,256]{1,0:T(8,128)S(1)}, f32[72,256]{1,0:T(8,128)S(1)}) custom-call(s32[1]{0:T(128)} %bitcast.parity_ref, f32[4,3,3,16,128]{4,3,2,1,0:T(8,128)S(1)} %get-tuple-element.15.vel_ref, ...), custom_call_target="tpu_custom_call", output_to_operand_aliasing={{0}: (7, {}), {1}: (8, {})} | custom-call | tf_op jit(solution)/shard_map/pallas_call | solution.py:347
  17.1 0.1 collective-permute-start.2
  17.2 1.3 %collective-permute-done.2 = f32[72,256]{1,0:T(8,128)S(1)} collective-permute-done((f32[72,256]{1,0:T(8,128)S(1)}, f32[72,256]{1,0:T(8,128)S(1)}, u32[]{:S(2)}, u32[]{:S(2)}) %collective-permute-start.2) | collective-permute-done | bytes 73760 | tf_op jit(solution)/shard_map/ppermute | solution.py:361
  18.5 0.1 collective-permute-start.3
  18.5 4.3 %collective-permute-done.3 = f32[72,256]{1,0:T(8,128)S(1)} collective-permute-done((f32[72,256]{1,0:T(8,128)S(1)}, f32[72,256]{1,0:T(8,128)S(1)}, u32[]{:S(2)}, u32[]{:S(2)}) %collective-permute-start.3) | collective-permute-done | bytes 73760 | tf_op jit(solution)/shard_map/ppermute | solution.py:364
  22.9 0.1 collective-permute-start.4
  23.0 4.3 %collective-permute-done.4 = f32[72,256]{1,0:T(8,128)S(1)} collective-permute-done((f32[72,256]{1,0:T(8,128)S(1)}, f32[72,256]{1,0:T(8,128)S(1)}, u32[]{:S(2)}, u32[]{:S(2)}) %collective-permute-start.4) | collective-permute-done | bytes 73760 | tf_op jit(solution)/shard_map/ppermute | solution.py:364
  27.3 0.1 collective-permute-start.5
  27.5 5.4 %collective-permute-done.5 = f32[72,256]{1,0:T(8,128)S(1)} collective-permute-done((f32[72,256]{1,0:T(8,128)S(1)}, f32[72,256]{1,0:T(8,128)S(1)}, u32[]{:S(2)}, u32[]{:S(2)}) %collective-permute-start.5) | collective-permute-done | bytes 73760 | tf_op jit(solution)/shard_map/ppermute | solution.py:364
  32.9 0.1 collective-permute-start.6
  33.0 1.3 %collective-permute-done.6.other_ref = f32[72,256]{1,0:T(8,128)S(1)} collective-permute-done((f32[72,256]{1,0:T(8,128)S(1)}, f32[72,256]{1,0:T(8,128)S(1)}, u32[]{:S(2)}, u32[]{:S(2)}) %collective-permute-start.6) | collective-permute-done | bytes 73760 | tf_op jit(solution)/shard_map/ppermute | solution.py:366
  34.2 11.2 %shard_map.61 = (f32[256,256]{1,0:T(8,128)}, bf16[3,3,10,128,256]{4,3,2,1,0:T(8,128)(2,1)}) custom-call(s32[1]{0:T(128)} %bitcast.parity_ref, f32[72,256]{1,0:T(8,128)S(1)} %add.20.mine_ref, f32[72,256]{1,0:T(8,128)S(1)} %collective-permute-done.6.other_ref, bf16[3,10,128,256]{3,2,1,0:T(8,128)(2,1)S(1)} %get-tuple-element.23.x_ref, ...), custom_call_target="tpu_custom_call" | custom-call | tf_op jit(solution)/shard_map/pallas_call | solution.py:368
  (5 shorter events, 0.1 us)
Async XLA Ops:
  1.6 10.5 %collective-permute-start.1 = (f32[240,128]{1,0:T(8,128)S(1)}, f32[240,128]{1,0:T(8,128)S(1)}, u32[]{:S(2)}, u32[]{:S(2)}) collective-permute-start(f32[240,128]{1,0:T(8,128)S(1)} %reshape.12), channel_id=1, source_target_pairs={{1,0},{2,1},{3,2},{4,3},{5,4},{6,5},{7,6},{8,7},{9,8},{10,9},{11,1... | collective-permute-start | bytes 368648 | tf_op jit(solution)/shard_map/ppermute | solution.py:328
  7.1 7.0 %collective-permute-start = (f32[240,128]{1,0:T(8,128)S(1)}, f32[240,128]{1,0:T(8,128)S(1)}, u32[]{:S(2)}, u32[]{:S(2)}) collective-permute-start(f32[240,128]{1,0:T(8,128)S(1)} %reshape.12), channel_id=1, source_target_pairs={{0,1},{1,2},{2,3},{3,4},{4,5},{5,6},{6,7},{7,8},{8,9},{9,10},{10,1... | collective-permute-start | bytes 368648 | tf_op jit(solution)/shard_map/ppermute | solution.py:327
  17.1 1.3 %collective-permute-start.2 = (f32[72,256]{1,0:T(8,128)S(1)}, f32[72,256]{1,0:T(8,128)S(1)}, u32[]{:S(2)}, u32[]{:S(2)}) collective-permute-start(f32[72,256]{1,0:T(8,128)S(1)} %get-tuple-element.22), channel_id=1, source_target_pairs={{0,1},{1,0},{2,3},{3,2},{4,5},{5,4},{6,7},{7,6},{8,9},{9,8},{10,11... | collective-permute-start | bytes 221192 | tf_op jit(solution)/shard_map/ppermute | solution.py:361
  18.5 4.4 %collective-permute-start.3 = (f32[72,256]{1,0:T(8,128)S(1)}, f32[72,256]{1,0:T(8,128)S(1)}, u32[]{:S(2)}, u32[]{:S(2)}) collective-permute-start(f32[72,256]{1,0:T(8,128)S(1)} %add.17), channel_id=1, source_target_pairs={{0,2},{1,3},{2,0},{3,1},{4,6},{5,7},{6,4},{7,5},{8,10},{9,11},{10,... | collective-permute-start | bytes 221192 | tf_op jit(solution)/shard_map/ppermute | solution.py:364
  22.9 4.4 %collective-permute-start.4 = (f32[72,256]{1,0:T(8,128)S(1)}, f32[72,256]{1,0:T(8,128)S(1)}, u32[]{:S(2)}, u32[]{:S(2)}) collective-permute-start(f32[72,256]{1,0:T(8,128)S(1)} %add.18), channel_id=1, source_target_pairs={{0,4},{1,5},{2,6},{3,7},{4,0},{5,1},{6,2},{7,3},{8,12},{9,13},{10,... | collective-permute-start | bytes 221192 | tf_op jit(solution)/shard_map/ppermute | solution.py:364
  27.3 5.5 %collective-permute-start.5 = (f32[72,256]{1,0:T(8,128)S(1)}, f32[72,256]{1,0:T(8,128)S(1)}, u32[]{:S(2)}, u32[]{:S(2)}) collective-permute-start(f32[72,256]{1,0:T(8,128)S(1)} %add.19), channel_id=1, source_target_pairs={{0,8},{1,9},{2,10},{3,11},{4,12},{5,13},{6,14},{7,15},{8,0},{9,1},... | collective-permute-start | bytes 221192 | tf_op jit(solution)/shard_map/ppermute | solution.py:364
  32.9 1.3 %collective-permute-start.6 = (f32[72,256]{1,0:T(8,128)S(1)}, f32[72,256]{1,0:T(8,128)S(1)}, u32[]{:S(2)}, u32[]{:S(2)}) collective-permute-start(f32[72,256]{1,0:T(8,128)S(1)} %add.20.mine_ref), channel_id=1, source_target_pairs={{0,1},{1,0},{2,3},{3,2},{4,5},{5,4},{6,7},{7,6},{8,9},{9,8},{10,11... | collective-permute-start | bytes 221192 | tf_op jit(solution)/shard_map/ppermute | solution.py:366

commit v4 on v3

--- a/solution.py
+++ b/solution.py
@@ -190,28 +190,40 @@
     acc_ref[...] += lax.dot_general(block, block, (((0,), (0,)), ((), ())), preferred_element_type=jnp.float32)
 
 
-def first_component_kernel(
-    vel_in, rim_in, omega_in, old_ref,
-    x_ref, y_ref, z_ref, gram_ref, vel_ref, rim_ref, omega_ref, turn_ref, small_sems, sems,
-):
-    small = [
-        pltpu.make_async_copy(source, target, small_sems.at[n])
-        for n, (source, target) in enumerate(((rim_in, rim_ref), (omega_in, omega_ref), (vel_in, vel_ref)))
-    ]
-    for copy in small:
-        copy.start()
+def start_kernel(vel_in, rim_in, omega_in, old_ref, band_ref, x_ref, vel_ref, rim_ref, omega_ref, small_sems, sems):
     snaps, _, slabs, height, _ = vel_ref.shape
     rows = height - 6
     copies = [
-        [pltpu.make_async_copy(old_ref.at[c, i], new_ref.at[i], sems.at[c, i]) for i in range(slabs)]
-        for c, new_ref in enumerate((x_ref, y_ref, z_ref))
+        pltpu.make_async_copy(source, target, small_sems.at[n])
+        for n, (source, target) in enumerate(((vel_in, vel_ref), (rim_in, rim_ref), (omega_in, omega_ref)))
     ]
-    for row in copies:
-        for copy in row:
-            copy.start()
+    copies += [pltpu.make_async_copy(old_ref.at[0, i], x_ref.at[i], sems.at[i]) for i in range(slabs)]
+    for copy in copies:
+        copy.start()
+    copies[0].wait()
+    for s in range(snaps):
+        for c in range(2):
+            for i in range(slabs):
+                at = ((s * 2 + c) * slabs + i) * rows
+                band_ref[at : at + rows] = vel_ref[s, 1 + c, i, 3 : 3 + rows]
+    for copy in copies[1:]:
+        copy.wait()
+
+
+def first_component_kernel(
+    vel_ref, rim_ref, omega_ref, old_x_ref, old_ref, x_ref, y_ref, z_ref, gram_ref, turn_ref, sems
+):
+    del old_x_ref
+    snaps, _, slabs, height, _ = vel_ref.shape
+    rows = height - 6
+    copies = [
+        pltpu.make_async_copy(old_ref.at[1 + c, i], new_ref.at[i], sems.at[c, i])
+        for c, new_ref in enumerate((y_ref, z_ref))
+        for i in range(slabs)
+    ]
+    for copy in copies:
+        copy.start()
     gram_ref[...] = jnp.zeros_like(gram_ref)
-    for copy in small:
-        copy.wait()
     right = gain_matrix(omega_ref[...], rows)
     edges = span_edges(rim_ref, 1, turn_ref)
     for i in range(slabs):
@@ -219,11 +231,9 @@
             wall_diff(vel_ref[s, 2, i], rows) - span_diff(vel_ref[s, 1, i, 3 : 3 + rows], edges[s, i])
             for s in range(snaps)
         ]
-        copies[0][i].wait()
         update_block(vort, right, x_ref.at[i], gram_ref)
-    for row in copies[1:]:
-        for copy in row:
-            copy.wait()
+    for copy in copies:
+        copy.wait()
 
 
 def pack(gram_ref, first, keep_ref, send_ref):
@@ -244,7 +254,7 @@
 
 
 def other_components_kernel(
-    parity_ref, vel_ref, rim_ref, behind_ref, ahead_ref, omega_ref, start_ref, old_y_ref, old_z_ref,
+    parity_ref, vel_ref, rim_ref, inner_ref, outer_ref, omega_ref, start_ref, old_y_ref, old_z_ref,
     y_ref, z_ref, keep_ref, send_ref, wide_ref, gram_ref, turn_ref,
 ):
     del old_y_ref, old_z_ref
@@ -253,12 +263,14 @@
     gram_ref[...] = start_ref[...]
     right = gain_matrix(omega_ref[...], rows)
     edges = span_edges(rim_ref, 0, turn_ref)
+    even = parity_ref[0] == 0
     for s in range(snaps):
         for c in range(2):
             for k in range(3):
                 at = ((s * 2 + c) * 3 + k) * rows
-                wide_ref[s, c, k] = behind_ref[at : at + rows]
-                wide_ref[s, c, 3 + slabs + k] = ahead_ref[at : at + rows]
+                inner, outer = inner_ref[at : at + rows], outer_ref[at : at + rows]
+                wide_ref[s, c, k] = jnp.where(even, outer, inner)
+                wide_ref[s, c, 3 + slabs + k] = jnp.where(even, inner, outer)
             for i in range(slabs):
                 wide_ref[s, c, 3 + i] = vel_ref[s, 1 + c, i, 3 : 3 + rows]
     for i in range(slabs):
@@ -271,7 +283,7 @@
                 else:
                     vort.append(along - wall_diff(vel_ref[s, 0, i], rows))
             update_block(vort, right, new_ref.at[i], gram_ref)
-    pack(gram_ref, parity_ref[0] == 0, keep_ref, send_ref)
+    pack(gram_ref, even, keep_ref, send_ref)
 
 
 def unpack(packed, part_diag, work_ref):
@@ -288,8 +300,8 @@
 
 
 def basis_kernel(
-    scale, parity_ref, mine_ref, other_ref, x_ref, y_ref, z_ref, upper_ref, basis_ref,
-    work_ref, solved_ref, block_ref, stage_ref, sems,
+    scale, parity_ref, mine_ref, other_ref, x_ref, y_ref, z_ref, factor_ref, basis_ref,
+    work_ref, upper_ref, solved_ref, block_ref, stage_ref, factor_sem, sems,
 ):
     order = work_ref.shape[0]
     part = order // 4
@@ -298,8 +310,9 @@
     top, bottom = jnp.where(first, mine[:part], other[:part]), jnp.where(first, other[:part], mine[:part])
     unpack(jnp.concatenate([top, bottom], axis=0), mine[part : part + 1], work_ref)
     factor_invert(work_ref, upper_ref, solved_ref, block_ref)
+    copies = [pltpu.make_async_copy(upper_ref, factor_ref, factor_sem)]
+    copies[0].start()
     inverse = solved_ref[...].T.astype(jnp.bfloat16)
-    copies = []
     for c, sketch_ref in enumerate((x_ref, y_ref, z_ref)):
         slabs, rows, cells, rank = sketch_ref.shape
         for i in range(slabs):
@@ -321,28 +334,39 @@
     limit = pltpu.CompilerParams(vmem_limit_bytes=24 << 20)
     place = lax.axis_index("gx")
     parity = (place % 2).reshape(1)
-    band = velocity[:, 1:3, :, 3 : 3 + rows]
-    tail = band[:, :, slabs - 3 :].reshape(-1, cells)
-    head = band[:, :, :3].reshape(-1, cells)
-    behind = lax.ppermute(tail, "gx", [(i, (i + 1) % count) for i in range(count)])
-    ahead = lax.ppermute(head, "gx", [((i + 1) % count, i) for i in range(count)])
     rim = span_rim.transpose(0, 2, 4, 1, 3)
     block = (slabs, rows, cells, rank)
     square = jax.ShapeDtypeStruct((rank, rank), jnp.float32)
     held = pltpu.VMEM(block, jnp.bfloat16)
-    inputs = [velocity, rim, omega, sketch_old]
-    sketch_x, raw_y, raw_z, gram, near_vel, near_rim, near_omega = pl.pallas_call(
+    old = pltpu.with_memory_space_constraint(sketch_old, pltpu.HBM)
+    small = [pltpu.with_memory_space_constraint(x, pltpu.HBM) for x in (velocity, rim, omega)]
+    planes, raw_x, near_vel, near_rim, near_omega = pl.pallas_call(
+        start_kernel,
+        out_shape=[pltpu.VMEM((snaps * 2 * slabs * rows, cells), jnp.float32), held]
+        + [pltpu.VMEM(x.shape, x.dtype) for x in (velocity, rim, omega)],
+        in_specs=[IN_HBM] * 4,
+        out_specs=[IN_VMEM] * 5,
+        scratch_shapes=[pltpu.SemaphoreType.DMA((3,)), pltpu.SemaphoreType.DMA((slabs,))],
+        compiler_params=limit,
+    )(*small, old)
+    inner, outer = planes, planes
+    if slabs > 3:
+        whole = planes.reshape(snaps * 2, slabs, rows, cells)
+        head, tail = (x.reshape(-1, cells) for x in (whole[:, :3], whole[:, slabs - 3 :]))
+        even = place % 2 == 0
+        inner, outer = jnp.where(even, tail, head), jnp.where(even, head, tail)
+    ring = lambda i: i % count
+    outer = lax.ppermute(outer, "gx", [(i, ring(i + (1 if i % 2 else -1))) for i in range(count)])
+    inner = lax.ppermute(inner, "gx", [(i, i ^ 1) for i in range(count)])
+    sketch_x, raw_y, raw_z, gram = pl.pallas_call(
         first_component_kernel,
-        out_shape=[held, held, held, square] + [pltpu.VMEM(x.shape, x.dtype) for x in inputs[:3]],
-        in_specs=[IN_HBM] * 4,
-        out_specs=[IN_VMEM] * 7,
-        scratch_shapes=[
-            pltpu.VMEM((128, 128), jnp.float32),
-            pltpu.SemaphoreType.DMA((3,)),
-            pltpu.SemaphoreType.DMA((3, slabs)),
-        ],
+        out_shape=[held, held, held, square],
+        in_specs=[IN_VMEM] * 4 + [IN_HBM],
+        out_specs=[IN_VMEM] * 4,
+        scratch_shapes=[pltpu.VMEM((128, 128), jnp.float32), pltpu.SemaphoreType.DMA((2, slabs))],
+        input_output_aliases={3: 0},
         compiler_params=limit,
-    )(*(pltpu.with_memory_space_constraint(x, pltpu.HBM) for x in inputs))
+    )(near_vel, near_rim, near_omega, raw_x, old)
     piece = jax.ShapeDtypeStruct((rank // 4 + 8, rank), jnp.float32)
     sketch_y, sketch_z, keep, send = pl.pallas_call(
         other_components_kernel,
@@ -356,7 +380,7 @@
         ],
         input_output_aliases={7: 0, 8: 1},
         compiler_params=limit,
-    )(parity, near_vel, near_rim, behind, ahead, near_omega, gram, raw_y, raw_z)
+    )(parity, near_vel, near_rim, inner, outer, near_omega, gram, raw_y, raw_z)
     swap = lambda k: [(i, i ^ k) for i in range(count)]
     total = keep + lax.ppermute(send, "gx", swap(1))
     step = 2
@@ -369,12 +393,14 @@
         functools.partial(basis_kernel, 1.0 / entries),
         out_shape=[square, jax.ShapeDtypeStruct((3, *block), jnp.bfloat16)],
         in_specs=[IN_SMEM] + [IN_VMEM] * 5,
-        out_specs=[IN_VMEM, IN_HBM],
+        out_specs=[IN_HBM, IN_HBM],
         scratch_shapes=[
+            pltpu.VMEM((rank, rank), jnp.float32),
             pltpu.VMEM((rank, rank), jnp.float32),
             pltpu.VMEM((rank, rank), jnp.float32),
             pltpu.VMEM((WIDE, 128), jnp.float32),
             pltpu.VMEM((3, *block), jnp.bfloat16),
+            pltpu.SemaphoreType.DMA,
             pltpu.SemaphoreType.DMA((3, slabs)),
         ],
         compiler_params=limit,

time: 45.5 us -> 42.3 us (0.930)
  waiting for transfers between devices: 18.6 us -> 15.6 us
  starting transfers between devices: 5.89 us -> 7.43 us
  local copies, waits for them, and re-layouts: 0.97 us -> 0 us
  Pallas kernels: 19.2 us -> 18.4 us
    ppermute x2, waiting for transfers between devices: 1.97 us -> 0.01 us  [the longest x1 0.01 us: local(): lax.ppermute(outer, 'gx', [(i, ring(i + (1 if i % 2 else -1))) for i in r...]
    pallas_call x1, Pallas kernels: 5.01 us -> 3.13 us  [local(): pl.pallas_call(first_component_kernel, out_shape=[held, held, held, squar...]
    pallas_call x0 -> x1, Pallas kernels: none -> 1.67 us  [local(): pl.pallas_call(start_kernel, out_shape=[pltpu.VMEM((snaps * 2 * slabs * r...]
    ppermute x3, starting transfers between devices: 0.28 us -> 1.31 us  [local(): total = total + lax.ppermute(total, 'gx', swap(step))]
    slice x1 -> x0, local copies, waits for them, and re-layouts: 0.95 us -> none  [local(): band = velocity[:, 1:3, :, 3:3 + rows]]
    ppermute x3, waiting for transfers between devices: 14.1 us -> 13.4 us  [local(): total = total + lax.ppermute(total, 'gx', swap(step))]
    pallas_call x1, Pallas kernels: 11.2 us -> 10.6 us  [local(): pl.pallas_call(functools.partial(basis_kernel, 1.0 / entries), out_shape=...]
    ppermute x1, starting transfers between devices: 0.07 us -> 0.57 us  [local(): total = keep + lax.ppermute(send, 'gx', swap(1))]
  transfers between devices with their start and end apart: 7 -> 7, of which waited for: 6 -> 5; matrix products, arithmetic and copies ran while one was open for 0% -> 0% of each run, Pallas kernels for 11% -> 7%
where the time goes in v4:
time: 42.3 us; the launch traced here: 42.2 us
  Pallas kernels  18.4 us (43%)
  waiting for transfers between devices  15.6 us (37%)
  starting transfers between devices  7.43 us (18%)
  between operations  0.7 us (2%)
    ppermute x3, waiting for transfers between devices, local(): total = total + lax.ppermute(total, 'gx', swap(step))  13.4 us
    pallas_call x1, Pallas kernels, local(): pl.pallas_call(functools.partial(basis_kernel, 1.0 / entries), out_shape=...  10.6 us
    ppermute x1, starting transfers between devices, local(): lax.ppermute(outer, 'gx', [(i, ring(i + (1 if i % 2 else -1))) for i in r...  5.48 us
    pallas_call x1, Pallas kernels, local(): pl.pallas_call(first_component_kernel, out_shape=[held, held, held, squar...  3.13 us
    pallas_call x1, Pallas kernels, local(): pl.pallas_call(other_components_kernel, out_shape=[held, held, piece, pie...  3.04 us
    pallas_call x1, Pallas kernels, local(): pl.pallas_call(start_kernel, out_shape=[pltpu.VMEM((snaps * 2 * slabs * r...  1.67 us
    ppermute x3, starting transfers between devices, local(): total = total + lax.ppermute(total, 'gx', swap(step))  1.31 us
    ppermute x1, waiting for transfers between devices, local(): other = lax.ppermute(total, 'gx', swap(1))  1.25 us
  transfers between devices with their start and end apart: 7, of which 5 were waited for; matrix products, arithmetic and copies ran while one was open for 0% of the time, Pallas kernels for 7%

profile of v4, /device:TPU:0, one launch (start us, length us, event | category | flops | bytes accessed | tf_op | source)
XLA Modules:
  0.0 42.2 jit_solution(3584232866734621974)
XLA Ops:
  0.6 1.7 %shard_map.59 = (f32[240,128]{1,0:T(8,128)S(1)}, bf16[3,10,128,256]{3,2,1,0:T(8,128)(2,1)S(1)}, f32[4,3,3,16,128]{4,3,2,1,0:T(8,128)S(1)}, f32[4,3,6,2,10]{4,3,2,1,0:T(2,128)S(1)}, f32[4,256]{1,0:T(4,128)S(1)}) custom-call(f32[4,3,3,16,128]{4,3,2,1,0:T(8,128)} %vel_in.1, f32[4,3,6,2,10]{4,3,2,1,0:T(2,128)} %bitcast.2, f32[4,256]{1,0:T(4,128)} %omega_in.1, ...), custom_call_target="tpu_custom_call" | custom-call | tf_op jit(solution)/shard_map/pallas_call | solution.py:343
  2.3 5.5 %collective-permute-start.1 = (f32[240,128]{1,0:T(8,128)S(1)}, f32[240,128]{1,0:T(8,128)S(1)}, u32[]{:S(2)}, u32[]{:S(2)}) collective-permute-start(f32[240,128]{1,0:T(8,128)S(1)} %get-tuple-element.19), channel_id=1, source_target_pairs={{0,15},{1,2},{2,1},{3,4},{4,3},{5,6},{6,5},{7,8},{8,7},{9,10},{10,... | collective-permute-start | bytes 368648 | tf_op jit(solution)/shard_map/ppermute | solution.py:359
  7.8 0.0 collective-permute-start
  7.8 3.1 %shard_map.60 = (bf16[3,10,128,256]{3,2,1,0:T(8,128)(2,1)S(1)}, bf16[3,10,128,256]{3,2,1,0:T(8,128)(2,1)S(1)}, bf16[3,10,128,256]{3,2,1,0:T(8,128)(2,1)S(1)}, f32[256,256]{1,0:T(8,128)S(1)}) custom-call(f32[4,3,3,16,128]{4,3,2,1,0:T(8,128)S(1)} %get-tuple-element.17.vel_ref, ...), custom_call_target="tpu_custom_call", output_to_operand_aliasing={{0}: (3, {})} | custom-call | tf_op jit(solution)/shard_map/pallas_call | solution.py:361
  10.9 0.0 collective-permute-done.1.outer_ref
  10.9 0.0 collective-permute-done.inner_ref
  11.0 3.0 %shard_map.61 = (bf16[3,10,128,256]{3,2,1,0:T(8,128)(2,1)S(1)}, bf16[3,10,128,256]{3,2,1,0:T(8,128)(2,1)S(1)}, f32[72,256]{1,0:T(8,128)S(1)}, f32[72,256]{1,0:T(8,128)S(1)}) custom-call(s32[1]{0:T(128)} %bitcast.parity_ref, f32[4,3,3,16,128]{4,3,2,1,0:T(8,128)S(1)} %get-tuple-element.17.vel_ref, ...), custom_call_target="tpu_custom_call", output_to_operand_aliasing={{0}: (7, {}), {1}: (8, {})} | custom-call | tf_op jit(solution)/shard_map/pallas_call | solution.py:371
  14.0 0.6 %collective-permute-start.2 = (f32[72,256]{1,0:T(8,128)S(1)}, f32[72,256]{1,0:T(8,128)S(1)}, u32[]{:S(2)}, u32[]{:S(2)}) collective-permute-start(f32[72,256]{1,0:T(8,128)S(1)} %get-tuple-element.26), channel_id=1, source_target_pairs={{0,1},{1,0},{2,3},{3,2},{4,5},{5,4},{6,7},{7,6},{8,9},{9,8},{10,11... | collective-permute-start | bytes 221192 | tf_op jit(solution)/shard_map/ppermute | solution.py:385
  14.6 0.9 %collective-permute-done.2 = f32[72,256]{1,0:T(8,128)S(1)} collective-permute-done((f32[72,256]{1,0:T(8,128)S(1)}, f32[72,256]{1,0:T(8,128)S(1)}, u32[]{:S(2)}, u32[]{:S(2)}) %collective-permute-start.2) | collective-permute-done | bytes 73760 | tf_op jit(solution)/shard_map/ppermute | solution.py:385
  15.5 0.1 collective-permute-start.3
  15.6 4.5 %collective-permute-done.3 = f32[72,256]{1,0:T(8,128)S(1)} collective-permute-done((f32[72,256]{1,0:T(8,128)S(1)}, f32[72,256]{1,0:T(8,128)S(1)}, u32[]{:S(2)}, u32[]{:S(2)}) %collective-permute-start.3) | collective-permute-done | bytes 73760 | tf_op jit(solution)/shard_map/ppermute | solution.py:388
  20.1 0.1 collective-permute-start.4
  20.2 4.3 %collective-permute-done.4 = f32[72,256]{1,0:T(8,128)S(1)} collective-permute-done((f32[72,256]{1,0:T(8,128)S(1)}, f32[72,256]{1,0:T(8,128)S(1)}, u32[]{:S(2)}, u32[]{:S(2)}) %collective-permute-start.4) | collective-permute-done | bytes 73760 | tf_op jit(solution)/shard_map/ppermute | solution.py:388
  24.5 1.2 %collective-permute-start.5 = (f32[72,256]{1,0:T(8,128)S(1)}, f32[72,256]{1,0:T(8,128)S(1)}, u32[]{:S(2)}, u32[]{:S(2)}) collective-permute-start(f32[72,256]{1,0:T(8,128)S(1)} %add.19), channel_id=1, source_target_pairs={{0,8},{1,9},{2,10},{3,11},{4,12},{5,13},{6,14},{7,15},{8,0},{9,1},... | collective-permute-start | bytes 221192 | tf_op jit(solution)/shard_map/ppermute | solution.py:388
  25.7 4.6 %collective-permute-done.5 = f32[72,256]{1,0:T(8,128)S(1)} collective-permute-done((f32[72,256]{1,0:T(8,128)S(1)}, f32[72,256]{1,0:T(8,128)S(1)}, u32[]{:S(2)}, u32[]{:S(2)}) %collective-permute-start.5) | collective-permute-done | bytes 73760 | tf_op jit(solution)/shard_map/ppermute | solution.py:388
  30.3 0.1 collective-permute-start.6
  30.4 1.3 %collective-permute-done.6.other_ref = f32[72,256]{1,0:T(8,128)S(1)} collective-permute-done((f32[72,256]{1,0:T(8,128)S(1)}, f32[72,256]{1,0:T(8,128)S(1)}, u32[]{:S(2)}, u32[]{:S(2)}) %collective-permute-start.6) | collective-permute-done | bytes 73760 | tf_op jit(solution)/shard_map/ppermute | solution.py:390
  31.6 10.6 %shard_map.62 = (f32[256,256]{1,0:T(8,128)}, bf16[3,3,10,128,256]{4,3,2,1,0:T(8,128)(2,1)}) custom-call(s32[1]{0:T(128)} %bitcast.parity_ref, f32[72,256]{1,0:T(8,128)S(1)} %add.20.mine_ref, f32[72,256]{1,0:T(8,128)S(1)} %collective-permute-done.6.other_ref, bf16[3,10,128,256]{3,2,1,0:T(8,128)(2,1)S(1)} %get-tuple-element.27.x_ref, ...), custom_call_target="tpu_custom_call" | custom-call | tf_op jit(solution)/shard_map/pallas_call | solution.py:392
  (4 shorter events, 0.0 us)
Async XLA Ops:
  2.3 8.6 %collective-permute-start.1 = (f32[240,128]{1,0:T(8,128)S(1)}, f32[240,128]{1,0:T(8,128)S(1)}, u32[]{:S(2)}, u32[]{:S(2)}) collective-permute-start(f32[240,128]{1,0:T(8,128)S(1)} %get-tuple-element.19), channel_id=1, source_target_pairs={{0,15},{1,2},{2,1},{3,4},{4,3},{5,6},{6,5},{7,8},{8,7},{9,10},{10,... | collective-permute-start | bytes 368648 | tf_op jit(solution)/shard_map/ppermute | solution.py:359
  7.8 3.2 %collective-permute-start = (f32[240,128]{1,0:T(8,128)S(1)}, f32[240,128]{1,0:T(8,128)S(1)}, u32[]{:S(2)}, u32[]{:S(2)}) collective-permute-start(f32[240,128]{1,0:T(8,128)S(1)} %get-tuple-element.19), channel_id=1, source_target_pairs={{0,1},{1,0},{2,3},{3,2},{4,5},{5,4},{6,7},{7,6},{8,9},{9,8},{10,11... | collective-permute-start | bytes 368648 | tf_op jit(solution)/shard_map/ppermute | solution.py:360
  14.0 1.5 %collective-permute-start.2 = (f32[72,256]{1,0:T(8,128)S(1)}, f32[72,256]{1,0:T(8,128)S(1)}, u32[]{:S(2)}, u32[]{:S(2)}) collective-permute-start(f32[72,256]{1,0:T(8,128)S(1)} %get-tuple-element.26), channel_id=1, source_target_pairs={{0,1},{1,0},{2,3},{3,2},{4,5},{5,4},{6,7},{7,6},{8,9},{9,8},{10,11... | collective-permute-start | bytes 221192 | tf_op jit(solution)/shard_map/ppermute | solution.py:385
  15.5 4.6 %collective-permute-start.3 = (f32[72,256]{1,0:T(8,128)S(1)}, f32[72,256]{1,0:T(8,128)S(1)}, u32[]{:S(2)}, u32[]{:S(2)}) collective-permute-start(f32[72,256]{1,0:T(8,128)S(1)} %add.17), channel_id=1, source_target_pairs={{0,2},{1,3},{2,0},{3,1},{4,6},{5,7},{6,4},{7,5},{8,10},{9,11},{10,... | collective-permute-start | bytes 221192 | tf_op jit(solution)/shard_map/ppermute | solution.py:388
  20.1 4.4 %collective-permute-start.4 = (f32[72,256]{1,0:T(8,128)S(1)}, f32[72,256]{1,0:T(8,128)S(1)}, u32[]{:S(2)}, u32[]{:S(2)}) collective-permute-start(f32[72,256]{1,0:T(8,128)S(1)} %add.18), channel_id=1, source_target_pairs={{0,4},{1,5},{2,6},{3,7},{4,0},{5,1},{6,2},{7,3},{8,12},{9,13},{10,... | collective-permute-start | bytes 221192 | tf_op jit(solution)/shard_map/ppermute | solution.py:388
  24.5 5.7 %collective-permute-start.5 = (f32[72,256]{1,0:T(8,128)S(1)}, f32[72,256]{1,0:T(8,128)S(1)}, u32[]{:S(2)}, u32[]{:S(2)}) collective-permute-start(f32[72,256]{1,0:T(8,128)S(1)} %add.19), channel_id=1, source_target_pairs={{0,8},{1,9},{2,10},{3,11},{4,12},{5,13},{6,14},{7,15},{8,0},{9,1},... | collective-permute-start | bytes 221192 | tf_op jit(solution)/shard_map/ppermute | solution.py:388
  30.3 1.3 %collective-permute-start.6 = (f32[72,256]{1,0:T(8,128)S(1)}, f32[72,256]{1,0:T(8,128)S(1)}, u32[]{:S(2)}, u32[]{:S(2)}) collective-permute-start(f32[72,256]{1,0:T(8,128)S(1)} %add.20.mine_ref), channel_id=1, source_target_pairs={{0,1},{1,0},{2,3},{3,2},{4,5},{5,4},{6,7},{7,6},{8,9},{9,8},{10,11... | collective-permute-start | bytes 221192 | tf_op jit(solution)/shard_map/ppermute | solution.py:390

commit v5 on v4

--- a/solution.py
+++ b/solution.py
@@ -35,7 +35,7 @@
             t_ref[top : top + WIDE] = kept - product[top - base : top - base + WIDE]
 
 
-def factor_block(w_ref, off):
+def factor_block(w_ref, off, spare):
     full = (8, 128)
     sub = lax.broadcasted_iota(jnp.int32, full, 0)
     for j0 in range(0, WIDE, 8):
@@ -77,9 +77,11 @@
         for k in range(1, 8):
             out = jnp.where(sub == k, final[k], out)
         w_ref[j0 : j0 + 8] = out
-
-
-def factor_invert(t_ref, u_ref, x_ref, w_ref):
+        if spare:
+            spare.pop(0)()
+
+
+def factor_invert(t_ref, u_ref, x_ref, w_ref, spare):
     order = t_ref.shape[0]
     lane = lax.broadcasted_iota(jnp.int32, (WIDE, 128), 1)
     sub = lax.broadcasted_iota(jnp.int32, (WIDE, 128), 0)
@@ -89,7 +91,7 @@
         inside = (lane >= off) & (lane < off + WIDE)
         here = slice(128 * half, 128 * half + 128)
         w_ref[...] = jnp.where(inside, t_ref[b0:stop, here], jnp.where(lane == sub + (WIDE - off), 1.0, 0.0))
-        factor_block(w_ref, off)
+        factor_block(w_ref, off, spare if b0 >= order // 2 else [])
         done = w_ref[...]
         moved = pltpu.roll(done, 64, 1)
         low, high = (moved, done) if off == 0 else (done, moved)
@@ -190,14 +192,13 @@
     acc_ref[...] += lax.dot_general(block, block, (((0,), (0,)), ((), ())), preferred_element_type=jnp.float32)
 
 
-def start_kernel(vel_in, rim_in, omega_in, old_ref, band_ref, x_ref, vel_ref, rim_ref, omega_ref, small_sems, sems):
+def start_kernel(vel_in, rim_in, omega_in, band_ref, vel_ref, rim_ref, omega_ref, sems):
     snaps, _, slabs, height, _ = vel_ref.shape
     rows = height - 6
     copies = [
-        pltpu.make_async_copy(source, target, small_sems.at[n])
+        pltpu.make_async_copy(source, target, sems.at[n])
         for n, (source, target) in enumerate(((vel_in, vel_ref), (rim_in, rim_ref), (omega_in, omega_ref)))
     ]
-    copies += [pltpu.make_async_copy(old_ref.at[0, i], x_ref.at[i], sems.at[i]) for i in range(slabs)]
     for copy in copies:
         copy.start()
     copies[0].wait()
@@ -211,14 +212,13 @@
 
 
 def first_component_kernel(
-    vel_ref, rim_ref, omega_ref, old_x_ref, old_ref, x_ref, y_ref, z_ref, gram_ref, turn_ref, sems
+    vel_ref, rim_ref, omega_ref, old_ref, x_ref, y_ref, z_ref, gram_ref, turn_ref, sems
 ):
-    del old_x_ref
     snaps, _, slabs, height, _ = vel_ref.shape
     rows = height - 6
     copies = [
-        pltpu.make_async_copy(old_ref.at[1 + c, i], new_ref.at[i], sems.at[c, i])
-        for c, new_ref in enumerate((y_ref, z_ref))
+        pltpu.make_async_copy(old_ref.at[c, i], new_ref.at[i], sems.at[c, i])
+        for c, new_ref in enumerate((x_ref, y_ref, z_ref))
         for i in range(slabs)
     ]
     for copy in copies:
@@ -231,8 +231,9 @@
             wall_diff(vel_ref[s, 2, i], rows) - span_diff(vel_ref[s, 1, i, 3 : 3 + rows], edges[s, i])
             for s in range(snaps)
         ]
+        copies[i].wait()
         update_block(vort, right, x_ref.at[i], gram_ref)
-    for copy in copies:
+    for copy in copies[slabs:]:
         copy.wait()
 
 
@@ -301,7 +302,7 @@
 
 def basis_kernel(
     scale, parity_ref, mine_ref, other_ref, x_ref, y_ref, z_ref, factor_ref, basis_ref,
-    work_ref, upper_ref, solved_ref, block_ref, stage_ref, factor_sem, sems,
+    work_ref, upper_ref, solved_ref, block_ref, low_ref, high_ref, factor_sem, sems,
 ):
     order = work_ref.shape[0]
     part = order // 4
@@ -309,20 +310,33 @@
     mine, other = mine_ref[...] * scale, other_ref[...] * scale
     top, bottom = jnp.where(first, mine[:part], other[:part]), jnp.where(first, other[:part], mine[:part])
     unpack(jnp.concatenate([top, bottom], axis=0), mine[part : part + 1], work_ref)
-    factor_invert(work_ref, upper_ref, solved_ref, block_ref)
-    copies = [pltpu.make_async_copy(upper_ref, factor_ref, factor_sem)]
-    copies[0].start()
-    inverse = solved_ref[...].T.astype(jnp.bfloat16)
-    for c, sketch_ref in enumerate((x_ref, y_ref, z_ref)):
-        slabs, rows, cells, rank = sketch_ref.shape
-        for i in range(slabs):
-            block = sketch_ref[i].reshape(rows * cells, rank)
-            product = jnp.dot(block, inverse, preferred_element_type=jnp.float32)
-            stage_ref[c, i] = product.astype(jnp.bfloat16).reshape(rows, cells, rank)
-            copy = pltpu.make_async_copy(stage_ref.at[c, i], basis_ref.at[c, i], sems.at[c, i])
-            copy.start()
-            copies.append(copy)
-    for copy in copies:
+    half = order // 2
+    blocks = [(c, i, ref) for c, ref in enumerate((x_ref, y_ref, z_ref)) for i in range(ref.shape[0])]
+    copies = []
+
+    def multiply(c, i, sketch_ref, stage_ref, side, get_inverse):
+        _, rows, cells, _ = sketch_ref.shape
+        block = sketch_ref[i, :, :, : half * (side + 1)].reshape(rows * cells, half * (side + 1))
+        product = jnp.dot(block, get_inverse(), preferred_element_type=jnp.float32)
+        stage_ref[c, i] = product.astype(jnp.bfloat16).reshape(rows, cells, half)
+        columns = pl.ds(half * side, half)
+        copy = pltpu.make_async_copy(
+            stage_ref.at[c, i], basis_ref.at[c, i, :, :, columns], sems.at[side, c, i]
+        )
+        copy.start()
+        copies.append(copy)
+
+    first_inverse = lambda: solved_ref[:half, :half].T.astype(jnp.bfloat16)
+    spare = [functools.partial(multiply, *block, low_ref, 0, first_inverse) for block in blocks]
+    factor_invert(work_ref, upper_ref, solved_ref, block_ref, spare)
+    for piece in spare:
+        piece()
+    factor_copy = pltpu.make_async_copy(upper_ref, factor_ref, factor_sem)
+    factor_copy.start()
+    inverse = solved_ref[half:].T.astype(jnp.bfloat16)
+    for block in blocks:
+        multiply(*block, high_ref, 1, lambda: inverse)
+    for copy in [factor_copy] + copies:
         copy.wait()
 
 
@@ -340,15 +354,15 @@
     held = pltpu.VMEM(block, jnp.bfloat16)
     old = pltpu.with_memory_space_constraint(sketch_old, pltpu.HBM)
     small = [pltpu.with_memory_space_constraint(x, pltpu.HBM) for x in (velocity, rim, omega)]
-    planes, raw_x, near_vel, near_rim, near_omega = pl.pallas_call(
+    planes, near_vel, near_rim, near_omega = pl.pallas_call(
         start_kernel,
-        out_shape=[pltpu.VMEM((snaps * 2 * slabs * rows, cells), jnp.float32), held]
+        out_shape=[pltpu.VMEM((snaps * 2 * slabs * rows, cells), jnp.float32)]
         + [pltpu.VMEM(x.shape, x.dtype) for x in (velocity, rim, omega)],
-        in_specs=[IN_HBM] * 4,
-        out_specs=[IN_VMEM] * 5,
-        scratch_shapes=[pltpu.SemaphoreType.DMA((3,)), pltpu.SemaphoreType.DMA((slabs,))],
+        in_specs=[IN_HBM] * 3,
+        out_specs=[IN_VMEM] * 4,
+        scratch_shapes=[pltpu.SemaphoreType.DMA((3,))],
         compiler_params=limit,
-    )(*small, old)
+    )(*small)
     inner, outer = planes, planes
     if slabs > 3:
         whole = planes.reshape(snaps * 2, slabs, rows, cells)
@@ -361,12 +375,11 @@
     sketch_x, raw_y, raw_z, gram = pl.pallas_call(
         first_component_kernel,
         out_shape=[held, held, held, square],
-        in_specs=[IN_VMEM] * 4 + [IN_HBM],
+        in_specs=[IN_VMEM] * 3 + [IN_HBM],
         out_specs=[IN_VMEM] * 4,
-        scratch_shapes=[pltpu.VMEM((128, 128), jnp.float32), pltpu.SemaphoreType.DMA((2, slabs))],
-        input_output_aliases={3: 0},
+        scratch_shapes=[pltpu.VMEM((128, 128), jnp.float32), pltpu.SemaphoreType.DMA((3, slabs))],
         compiler_params=limit,
-    )(near_vel, near_rim, near_omega, raw_x, old)
+    )(near_vel, near_rim, near_omega, old)
     piece = jax.ShapeDtypeStruct((rank // 4 + 8, rank), jnp.float32)
     sketch_y, sketch_z, keep, send = pl.pallas_call(
         other_components_kernel,
@@ -399,9 +412,10 @@
             pltpu.VMEM((rank, rank), jnp.float32),
             pltpu.VMEM((rank, rank), jnp.float32),
             pltpu.VMEM((WIDE, 128), jnp.float32),
-            pltpu.VMEM((3, *block), jnp.bfloat16),
+            pltpu.VMEM((3, *block[:-1], rank // 2), jnp.bfloat16),
+            pltpu.VMEM((3, *block[:-1], rank // 2), jnp.bfloat16),
             pltpu.SemaphoreType.DMA,
-            pltpu.SemaphoreType.DMA((3, slabs)),
+            pltpu.SemaphoreType.DMA((2, 3, slabs)),
         ],
         compiler_params=limit,
     )(parity, total, other, sketch_x, sketch_y, sketch_z)

time: 42.3 us -> 41.4 us (0.979)
  Pallas kernels: 18.4 us -> 17.7 us
    pallas_call x1, Pallas kernels: 1.67 us -> 1.01 us  [local(): pl.pallas_call(start_kernel, out_shape=[pltpu.VMEM((snaps * 2 * slabs * r...]
  transfers between devices with their start and end apart: 7 -> 7, of which waited for: 5 -> 5; matrix products, arithmetic and copies ran while one was open for 0% -> 0% of each run, Pallas kernels for 7% -> 8%
where the time goes in v5:
time: 41.4 us; the launch traced here: 41.3 us
  Pallas kernels  17.7 us (43%)
  waiting for transfers between devices  15.6 us (38%)
  starting transfers between devices  7.19 us (17%)
  between operations  0.7 us (2%)
    ppermute x3, waiting for transfers between devices, local(): total = total + lax.ppermute(total, 'gx', swap(step))  13.5 us
    pallas_call x1, Pallas kernels, local(): pl.pallas_call(functools.partial(basis_kernel, 1.0 / entries), out_shape=...  10.3 us
    ppermute x1, starting transfers between devices, local(): lax.ppermute(outer, 'gx', [(i, ring(i + (1 if i % 2 else -1))) for i in r...  5.48 us
    pallas_call x1, Pallas kernels, local(): pl.pallas_call(first_component_kernel, out_shape=[held, held, held, squar...  3.37 us
    pallas_call x1, Pallas kernels, local(): pl.pallas_call(other_components_kernel, out_shape=[held, held, piece, pie...  3.04 us
    ppermute x1, waiting for transfers between devices, local(): other = lax.ppermute(total, 'gx', swap(1))  1.25 us
    ppermute x3, starting transfers between devices, local(): total = total + lax.ppermute(total, 'gx', swap(step))  1.07 us
    pallas_call x1, Pallas kernels, local(): pl.pallas_call(start_kernel, out_shape=[pltpu.VMEM((snaps * 2 * slabs * r...  1.01 us
  transfers between devices with their start and end apart: 7, of which 5 were waited for; matrix products, arithmetic and copies ran while one was open for 0% of the time, Pallas kernels for 8%

profile of v5, /device:TPU:0, one launch (start us, length us, event | category | flops | bytes accessed | tf_op | source)
XLA Modules:
  0.0 41.3 jit_solution(13484734220910840503)
XLA Ops:
  0.6 1.0 %shard_map.59 = (f32[240,128]{1,0:T(8,128)S(1)}, f32[4,3,3,16,128]{4,3,2,1,0:T(8,128)S(1)}, f32[4,3,6,2,10]{4,3,2,1,0:T(2,128)S(1)}, f32[4,256]{1,0:T(4,128)S(1)}) custom-call(f32[4,3,3,16,128]{4,3,2,1,0:T(8,128)} %vel_in.1, f32[4,3,6,2,10]{4,3,2,1,0:T(2,128)} %bitcast.2, f32[4,256]{1,0:T(4,128)} %omega_in.1), custom_call_target="tpu_custom_call" | custom-call | tf_op jit(solution)/shard_map/pallas_call | solution.py:357
  1.6 5.5 %collective-permute-start.1 = (f32[240,128]{1,0:T(8,128)S(1)}, f32[240,128]{1,0:T(8,128)S(1)}, u32[]{:S(2)}, u32[]{:S(2)}) collective-permute-start(f32[240,128]{1,0:T(8,128)S(1)} %get-tuple-element.18), channel_id=1, source_target_pairs={{0,15},{1,2},{2,1},{3,4},{4,3},{5,6},{6,5},{7,8},{8,7},{9,10},{10,... | collective-permute-start | bytes 368648 | tf_op jit(solution)/shard_map/ppermute | solution.py:373
  7.1 0.0 collective-permute-start
  7.1 3.4 %shard_map.60 = (bf16[3,10,128,256]{3,2,1,0:T(8,128)(2,1)S(1)}, bf16[3,10,128,256]{3,2,1,0:T(8,128)(2,1)S(1)}, bf16[3,10,128,256]{3,2,1,0:T(8,128)(2,1)S(1)}, f32[256,256]{1,0:T(8,128)S(1)}) custom-call(f32[4,3,3,16,128]{4,3,2,1,0:T(8,128)S(1)} %get-tuple-element.16.vel_ref, f32[4,3,6,2,10]{4,3,2,1,0:T(2,128)S(1)} %get-tuple-element.17.rim_ref, ...), custom_call_target="tpu_custom_call" | custom-call | tf_op jit(solution)/shard_map/pallas_call | solution.py:375
  10.5 0.0 collective-permute-done.1.outer_ref
  10.5 0.0 collective-permute-done.inner_ref
  10.5 3.0 %shard_map.61 = (bf16[3,10,128,256]{3,2,1,0:T(8,128)(2,1)S(1)}, bf16[3,10,128,256]{3,2,1,0:T(8,128)(2,1)S(1)}, f32[72,256]{1,0:T(8,128)S(1)}, f32[72,256]{1,0:T(8,128)S(1)}) custom-call(s32[1]{0:T(128)} %bitcast.parity_ref, f32[4,3,3,16,128]{4,3,2,1,0:T(8,128)S(1)} %get-tuple-element.16.vel_ref, ...), custom_call_target="tpu_custom_call", output_to_operand_aliasing={{0}: (7, {}), {1}: (8, {})} | custom-call | tf_op jit(solution)/shard_map/pallas_call | solution.py:384
  13.6 0.6 %collective-permute-start.2 = (f32[72,256]{1,0:T(8,128)S(1)}, f32[72,256]{1,0:T(8,128)S(1)}, u32[]{:S(2)}, u32[]{:S(2)}) collective-permute-start(f32[72,256]{1,0:T(8,128)S(1)} %get-tuple-element.24), channel_id=1, source_target_pairs={{0,1},{1,0},{2,3},{3,2},{4,5},{5,4},{6,7},{7,6},{8,9},{9,8},{10,11... | collective-permute-start | bytes 221192 | tf_op jit(solution)/shard_map/ppermute | solution.py:398
  14.1 0.9 %collective-permute-done.2 = f32[72,256]{1,0:T(8,128)S(1)} collective-permute-done((f32[72,256]{1,0:T(8,128)S(1)}, f32[72,256]{1,0:T(8,128)S(1)}, u32[]{:S(2)}, u32[]{:S(2)}) %collective-permute-start.2) | collective-permute-done | bytes 73760 | tf_op jit(solution)/shard_map/ppermute | solution.py:398
  15.1 0.1 collective-permute-start.3
  15.1 4.5 %collective-permute-done.3 = f32[72,256]{1,0:T(8,128)S(1)} collective-permute-done((f32[72,256]{1,0:T(8,128)S(1)}, f32[72,256]{1,0:T(8,128)S(1)}, u32[]{:S(2)}, u32[]{:S(2)}) %collective-permute-start.3) | collective-permute-done | bytes 73760 | tf_op jit(solution)/shard_map/ppermute | solution.py:401
  19.7 0.1 collective-permute-start.4
  19.7 4.3 %collective-permute-done.4 = f32[72,256]{1,0:T(8,128)S(1)} collective-permute-done((f32[72,256]{1,0:T(8,128)S(1)}, f32[72,256]{1,0:T(8,128)S(1)}, u32[]{:S(2)}, u32[]{:S(2)}) %collective-permute-start.4) | collective-permute-done | bytes 73760 | tf_op jit(solution)/shard_map/ppermute | solution.py:401
  24.1 0.9 %collective-permute-start.5 = (f32[72,256]{1,0:T(8,128)S(1)}, f32[72,256]{1,0:T(8,128)S(1)}, u32[]{:S(2)}, u32[]{:S(2)}) collective-permute-start(f32[72,256]{1,0:T(8,128)S(1)} %add.19), channel_id=1, source_target_pairs={{0,8},{1,9},{2,10},{3,11},{4,12},{5,13},{6,14},{7,15},{8,0},{9,1},... | collective-permute-start | bytes 221192 | tf_op jit(solution)/shard_map/ppermute | solution.py:401
  25.0 4.6 %collective-permute-done.5 = f32[72,256]{1,0:T(8,128)S(1)} collective-permute-done((f32[72,256]{1,0:T(8,128)S(1)}, f32[72,256]{1,0:T(8,128)S(1)}, u32[]{:S(2)}, u32[]{:S(2)}) %collective-permute-start.5) | collective-permute-done | bytes 73760 | tf_op jit(solution)/shard_map/ppermute | solution.py:401
  29.7 0.1 collective-permute-start.6
  29.7 1.3 %collective-permute-done.6.other_ref = f32[72,256]{1,0:T(8,128)S(1)} collective-permute-done((f32[72,256]{1,0:T(8,128)S(1)}, f32[72,256]{1,0:T(8,128)S(1)}, u32[]{:S(2)}, u32[]{:S(2)}) %collective-permute-start.6) | collective-permute-done | bytes 73760 | tf_op jit(solution)/shard_map/ppermute | solution.py:403
  31.0 10.3 %shard_map.62 = (f32[256,256]{1,0:T(8,128)}, bf16[3,3,10,128,256]{4,3,2,1,0:T(8,128)(2,1)}) custom-call(s32[1]{0:T(128)} %bitcast.parity_ref, f32[72,256]{1,0:T(8,128)S(1)} %add.20.mine_ref, f32[72,256]{1,0:T(8,128)S(1)} %collective-permute-done.6.other_ref, bf16[3,10,128,256]{3,2,1,0:T(8,128)(2,1)S(1)} %get-tuple-element.25.x_ref, ...), custom_call_target="tpu_custom_call" | custom-call | tf_op jit(solution)/shard_map/pallas_call | solution.py:405
  (4 shorter events, 0.0 us)
Async XLA Ops:
  1.6 8.9 %collective-permute-start.1 = (f32[240,128]{1,0:T(8,128)S(1)}, f32[240,128]{1,0:T(8,128)S(1)}, u32[]{:S(2)}, u32[]{:S(2)}) collective-permute-start(f32[240,128]{1,0:T(8,128)S(1)} %get-tuple-element.18), channel_id=1, source_target_pairs={{0,15},{1,2},{2,1},{3,4},{4,3},{5,6},{6,5},{7,8},{8,7},{9,10},{10,... | collective-permute-start | bytes 368648 | tf_op jit(solution)/shard_map/ppermute | solution.py:373
  7.1 3.4 %collective-permute-start = (f32[240,128]{1,0:T(8,128)S(1)}, f32[240,128]{1,0:T(8,128)S(1)}, u32[]{:S(2)}, u32[]{:S(2)}) collective-permute-start(f32[240,128]{1,0:T(8,128)S(1)} %get-tuple-element.18), channel_id=1, source_target_pairs={{0,1},{1,0},{2,3},{3,2},{4,5},{5,4},{6,7},{7,6},{8,9},{9,8},{10,11... | collective-permute-start | bytes 368648 | tf_op jit(solution)/shard_map/ppermute | solution.py:374
  13.6 1.5 %collective-permute-start.2 = (f32[72,256]{1,0:T(8,128)S(1)}, f32[72,256]{1,0:T(8,128)S(1)}, u32[]{:S(2)}, u32[]{:S(2)}) collective-permute-start(f32[72,256]{1,0:T(8,128)S(1)} %get-tuple-element.24), channel_id=1, source_target_pairs={{0,1},{1,0},{2,3},{3,2},{4,5},{5,4},{6,7},{7,6},{8,9},{9,8},{10,11... | collective-permute-start | bytes 221192 | tf_op jit(solution)/shard_map/ppermute | solution.py:398
  15.1 4.6 %collective-permute-start.3 = (f32[72,256]{1,0:T(8,128)S(1)}, f32[72,256]{1,0:T(8,128)S(1)}, u32[]{:S(2)}, u32[]{:S(2)}) collective-permute-start(f32[72,256]{1,0:T(8,128)S(1)} %add.17), channel_id=1, source_target_pairs={{0,2},{1,3},{2,0},{3,1},{4,6},{5,7},{6,4},{7,5},{8,10},{9,11},{10,... | collective-permute-start | bytes 221192 | tf_op jit(solution)/shard_map/ppermute | solution.py:401
  19.7 4.4 %collective-permute-start.4 = (f32[72,256]{1,0:T(8,128)S(1)}, f32[72,256]{1,0:T(8,128)S(1)}, u32[]{:S(2)}, u32[]{:S(2)}) collective-permute-start(f32[72,256]{1,0:T(8,128)S(1)} %add.18), channel_id=1, source_target_pairs={{0,4},{1,5},{2,6},{3,7},{4,0},{5,1},{6,2},{7,3},{8,12},{9,13},{10,... | collective-permute-start | bytes 221192 | tf_op jit(solution)/shard_map/ppermute | solution.py:401
  24.1 5.5 %collective-permute-start.5 = (f32[72,256]{1,0:T(8,128)S(1)}, f32[72,256]{1,0:T(8,128)S(1)}, u32[]{:S(2)}, u32[]{:S(2)}) collective-permute-start(f32[72,256]{1,0:T(8,128)S(1)} %add.19), channel_id=1, source_target_pairs={{0,8},{1,9},{2,10},{3,11},{4,12},{5,13},{6,14},{7,15},{8,0},{9,1},... | collective-permute-start | bytes 221192 | tf_op jit(solution)/shard_map/ppermute | solution.py:401
  29.7 1.3 %collective-permute-start.6 = (f32[72,256]{1,0:T(8,128)S(1)}, f32[72,256]{1,0:T(8,128)S(1)}, u32[]{:S(2)}, u32[]{:S(2)}) collective-permute-start(f32[72,256]{1,0:T(8,128)S(1)} %add.20.mine_ref), channel_id=1, source_target_pairs={{0,1},{1,0},{2,3},{3,2},{4,5},{5,4},{6,7},{7,6},{8,9},{9,8},{10,11... | collective-permute-start | bytes 221192 | tf_op jit(solution)/shard_map/ppermute | solution.py:403

commit v6 on v5

--- a/solution.py
+++ b/solution.py
@@ -40,24 +40,23 @@
     sub = lax.broadcasted_iota(jnp.int32, full, 0)
     for j0 in range(0, WIDE, 8):
         c0 = off + j0
-        now = w_ref[j0 : j0 + 8]
         rows = [w_ref[pl.ds(j0 + i, 8, stride=0), :] for i in range(8)]
         a = {}
-        for j in range(8):
-            for i in range(j + 1):
+        for i in range(8):
+            for j in range(i, 8):
                 a[i, j] = jnp.broadcast_to(rows[i][:, c0 + j : c0 + j + 1], full)
         left, scaled, final = {}, {}, {}
         for k in range(0, 8, 2):
             n = k + 1
             top, mid, low = a[k, k], a[k, n], a[n, n]
             rdet = 1.0 / (top * low - mid * mid)
-            for i in range(k + 2, 8):
-                left[k, i] = (low * a[k, i] - mid * a[n, i]) * rdet
-                left[n, i] = (top * a[n, i] - mid * a[k, i]) * rdet
+            p = {i: low * a[k, i] - mid * a[n, i] for i in range(k + 2, 8)}
+            q = {i: top * a[n, i] - mid * a[k, i] for i in range(k + 2, 8)}
             for i in range(k + 2, 8):
                 for j in range(i, 8):
-                    a[i, j] = a[i, j] - left[k, i] * a[k, j] - left[n, i] * a[n, j]
-                rows[i] = rows[i] - left[k, i] * rows[k] - left[n, i] * rows[n]
+                    a[i, j] = a[i, j] - (p[i] * a[k, j] + q[i] * a[n, j]) * rdet
+                left[k, i], left[n, i] = p[i] * rdet, q[i] * rdet
+                rows[i] = rows[i] - (left[k, i] * rows[k] + left[n, i] * rows[n])
             scaled[k] = (low * rows[k] - mid * rows[n]) * rdet
             scaled[n] = (top * rows[n] - mid * rows[k]) * rdet
             root = lax.rsqrt(top)
@@ -212,7 +211,8 @@
 
 
 def first_component_kernel(
-    vel_ref, rim_ref, omega_ref, old_ref, x_ref, y_ref, z_ref, gram_ref, turn_ref, sems
+    vel_ref, rim_ref, omega_ref, old_ref,
+    x_ref, y_ref, z_ref, gram_ref, right_ref, part_ref, turn_ref, sems,
 ):
     snaps, _, slabs, height, _ = vel_ref.shape
     rows = height - 6
@@ -225,6 +225,7 @@
         copy.start()
     gram_ref[...] = jnp.zeros_like(gram_ref)
     right = gain_matrix(omega_ref[...], rows)
+    right_ref[...] = right
     edges = span_edges(rim_ref, 1, turn_ref)
     for i in range(slabs):
         vort = [
@@ -233,6 +234,11 @@
         ]
         copies[i].wait()
         update_block(vort, right, x_ref.at[i], gram_ref)
+    edges = span_edges(rim_ref, 0, turn_ref)
+    for s in range(snaps):
+        for i in range(slabs):
+            part_ref[0, s, i] = span_diff(vel_ref[s, 0, i, 3 : 3 + rows], edges[s, i])
+            part_ref[1, s, i] = wall_diff(vel_ref[s, 0, i], rows)
     for copy in copies[slabs:]:
         copy.wait()
 
@@ -255,15 +261,14 @@
 
 
 def other_components_kernel(
-    parity_ref, vel_ref, rim_ref, inner_ref, outer_ref, omega_ref, start_ref, old_y_ref, old_z_ref,
-    y_ref, z_ref, keep_ref, send_ref, wide_ref, gram_ref, turn_ref,
+    parity_ref, vel_ref, part_ref, inner_ref, outer_ref, right_ref, start_ref, old_y_ref, old_z_ref,
+    y_ref, z_ref, keep_ref, send_ref, wide_ref, gram_ref,
 ):
     del old_y_ref, old_z_ref
     snaps, _, slabs, height, _ = vel_ref.shape
     rows = height - 6
     gram_ref[...] = start_ref[...]
-    right = gain_matrix(omega_ref[...], rows)
-    edges = span_edges(rim_ref, 0, turn_ref)
+    right = right_ref[...]
     even = parity_ref[0] == 0
     for s in range(snaps):
         for c in range(2):
@@ -280,9 +285,9 @@
             for s in range(snaps):
                 along = stream_diff([wide_ref[s, 1 - c, i + k] for k in range(7)], 3)
                 if c == 0:
-                    vort.append(span_diff(vel_ref[s, 0, i, 3 : 3 + rows], edges[s, i]) - along)
+                    vort.append(part_ref[0, s, i] - along)
                 else:
-                    vort.append(along - wall_diff(vel_ref[s, 0, i], rows))
+                    vort.append(along - part_ref[1, s, i])
             update_block(vort, right, new_ref.at[i], gram_ref)
     pack(gram_ref, even, keep_ref, send_ref)
 
@@ -316,9 +321,12 @@
 
     def multiply(c, i, sketch_ref, stage_ref, side, get_inverse):
         _, rows, cells, _ = sketch_ref.shape
-        block = sketch_ref[i, :, :, : half * (side + 1)].reshape(rows * cells, half * (side + 1))
-        product = jnp.dot(block, get_inverse(), preferred_element_type=jnp.float32)
-        stage_ref[c, i] = product.astype(jnp.bfloat16).reshape(rows, cells, half)
+        depth = half * (side + 1)
+        step = 2 - rows % 2
+        for y in range(0, rows, step):
+            block = sketch_ref[i, y : y + step, :, :depth].reshape(step * cells, depth)
+            product = jnp.dot(block, get_inverse(), preferred_element_type=jnp.float32)
+            stage_ref[c, i, y : y + step] = product.astype(jnp.bfloat16).reshape(step, cells, half)
         columns = pl.ds(half * side, half)
         copy = pltpu.make_async_copy(
             stage_ref.at[c, i], basis_ref.at[c, i, :, :, columns], sems.at[side, c, i]
@@ -326,7 +334,13 @@
         copy.start()
         copies.append(copy)
 
-    first_inverse = lambda: solved_ref[:half, :half].T.astype(jnp.bfloat16)
+    made = []
+
+    def first_inverse():
+        if not made:
+            made.append(solved_ref[:half, :half].T.astype(jnp.bfloat16))
+        return made[0]
+
     spare = [functools.partial(multiply, *block, low_ref, 0, first_inverse) for block in blocks]
     factor_invert(work_ref, upper_ref, solved_ref, block_ref, spare)
     for piece in spare:
@@ -372,11 +386,14 @@
     ring = lambda i: i % count
     outer = lax.ppermute(outer, "gx", [(i, ring(i + (1 if i % 2 else -1))) for i in range(count)])
     inner = lax.ppermute(inner, "gx", [(i, i ^ 1) for i in range(count)])
-    sketch_x, raw_y, raw_z, gram = pl.pallas_call(
+    depth = 3 * snaps * rows
+    sketch_x, raw_y, raw_z, gram, right, partial = pl.pallas_call(
         first_component_kernel,
-        out_shape=[held, held, held, square],
+        out_shape=[held, held, held, square]
+        + [pltpu.VMEM((depth + -depth % 128, rank), jnp.bfloat16)]
+        + [pltpu.VMEM((2, snaps, slabs, rows, cells), jnp.float32)],
         in_specs=[IN_VMEM] * 3 + [IN_HBM],
-        out_specs=[IN_VMEM] * 4,
+        out_specs=[IN_VMEM] * 6,
         scratch_shapes=[pltpu.VMEM((128, 128), jnp.float32), pltpu.SemaphoreType.DMA((3, slabs))],
         compiler_params=limit,
     )(near_vel, near_rim, near_omega, old)
@@ -389,11 +406,10 @@
         scratch_shapes=[
             pltpu.VMEM((snaps, 2, slabs + 6, rows, cells), jnp.float32),
             pltpu.VMEM((rank, rank), jnp.float32),
-            pltpu.VMEM((128, 128), jnp.float32),
         ],
         input_output_aliases={7: 0, 8: 1},
         compiler_params=limit,
-    )(parity, near_vel, near_rim, inner, outer, near_omega, gram, raw_y, raw_z)
+    )(parity, near_vel, partial, inner, outer, right, gram, raw_y, raw_z)
     swap = lambda k: [(i, i ^ k) for i in range(count)]
     total = keep + lax.ppermute(send, "gx", swap(1))
     step = 2

time: 41.4 us -> 40.5 us (0.978)
  Pallas kernels: 17.7 us -> 16.7 us
    pallas_call x1, Pallas kernels: 10.3 us -> 9.55 us  [local(): pl.pallas_call(functools.partial(basis_kernel, 1.0 / entries), out_shape=...]
  transfers between devices with their start and end apart: 7 -> 7, of which waited for: 5 -> 5; matrix products, arithmetic and copies ran while one was open for 0% -> 0% of each run, Pallas kernels for 8% -> 9%
where the time goes in v6:
time: 40.5 us; the launch traced here: 40.3 us
  Pallas kernels  16.7 us (41%)
  waiting for transfers between devices  15.8 us (39%)
  starting transfers between devices  7.06 us (17%)
  between operations  0.7 us (2%)
    ppermute x3, waiting for transfers between devices, local(): total = total + lax.ppermute(total, 'gx', swap(step))  13.6 us
    pallas_call x1, Pallas kernels, local(): pl.pallas_call(functools.partial(basis_kernel, 1.0 / entries), out_shape=...  9.55 us
    ppermute x1, starting transfers between devices, local(): lax.ppermute(outer, 'gx', [(i, ring(i + (1 if i % 2 else -1))) for i in r...  5.48 us
    pallas_call x1, Pallas kernels, local(): pl.pallas_call(first_component_kernel, out_shape=[held, held, held, squar...  3.5 us
    pallas_call x1, Pallas kernels, local(): pl.pallas_call(other_components_kernel, out_shape=[held, held, piece, pie...  2.65 us
    ppermute x1, waiting for transfers between devices, local(): other = lax.ppermute(total, 'gx', swap(1))  1.25 us
    pallas_call x1, Pallas kernels, local(): pl.pallas_call(start_kernel, out_shape=[pltpu.VMEM((snaps * 2 * slabs * r...  1.01 us
    ppermute x3, starting transfers between devices, local(): total = total + lax.ppermute(total, 'gx', swap(step))  0.93 us
  transfers between devices with their start and end apart: 7, of which 5 were waited for; matrix products, arithmetic and copies ran while one was open for 0% of the time, Pallas kernels for 9%

profile of v6, /device:TPU:0, one launch (start us, length us, event | category | flops | bytes accessed | tf_op | source)
XLA Modules:
  0.0 40.3 jit_solution(892861244785791263)
XLA Ops:
  0.6 1.0 %shard_map.59 = (f32[240,128]{1,0:T(8,128)S(1)}, f32[4,3,3,16,128]{4,3,2,1,0:T(8,128)S(1)}, f32[4,3,6,2,10]{4,3,2,1,0:T(2,128)S(1)}, f32[4,256]{1,0:T(4,128)S(1)}) custom-call(f32[4,3,3,16,128]{4,3,2,1,0:T(8,128)} %vel_in.1, f32[4,3,6,2,10]{4,3,2,1,0:T(2,128)} %bitcast.2, f32[4,256]{1,0:T(4,128)} %omega_in.1), custom_call_target="tpu_custom_call" | custom-call | tf_op jit(solution)/shard_map/pallas_call | solution.py:371
  1.6 5.5 %collective-permute-start.1 = (f32[240,128]{1,0:T(8,128)S(1)}, f32[240,128]{1,0:T(8,128)S(1)}, u32[]{:S(2)}, u32[]{:S(2)}) collective-permute-start(f32[240,128]{1,0:T(8,128)S(1)} %get-tuple-element.22), channel_id=1, source_target_pairs={{0,15},{1,2},{2,1},{3,4},{4,3},{5,6},{6,5},{7,8},{8,7},{9,10},{10,... | collective-permute-start | bytes 368648 | tf_op jit(solution)/shard_map/ppermute | solution.py:387
  7.1 0.0 collective-permute-start
  7.1 3.5 %shard_map.60 = (bf16[3,10,128,256]{3,2,1,0:T(8,128)(2,1)S(1)}, bf16[3,10,128,256]{3,2,1,0:T(8,128)(2,1)S(1)}, bf16[3,10,128,256]{3,2,1,0:T(8,128)(2,1)S(1)}, f3...) custom-call(f32[4,3,3,16,128]{4,3,2,1,0:T(8,128)S(1)} %get-tuple-element.18.vel_ref, ...), custom_call_target="tpu_custom_call" | custom-call | tf_op jit(solution)/shard_map/pallas_call | solution.py:390
  10.6 0.0 collective-permute-done.1.outer_ref
  10.6 0.0 collective-permute-done.inner_ref
  10.7 2.7 %shard_map.61 = (bf16[3,10,128,256]{3,2,1,0:T(8,128)(2,1)S(1)}, bf16[3,10,128,256]{3,2,1,0:T(8,128)(2,1)S(1)}, f32[72,256]{1,0:T(8,128)S(1)}, f32[72,256]{1,0:T(8,128)S(1)}) custom-call(s32[1]{0:T(128)} %bitcast.parity_ref, f32[4,3,3,16,128]{4,3,2,1,0:T(8,128)S(1)} %get-tuple-element.18.vel_ref, ...), custom_call_target="tpu_custom_call", output_to_operand_aliasing={{0}: (7, {}), {1}: (8, {})} | custom-call | tf_op jit(solution)/shard_map/pallas_call | solution.py:401
  13.3 0.6 %collective-permute-start.2 = (f32[72,256]{1,0:T(8,128)S(1)}, f32[72,256]{1,0:T(8,128)S(1)}, u32[]{:S(2)}, u32[]{:S(2)}) collective-permute-start(f32[72,256]{1,0:T(8,128)S(1)} %get-tuple-element.28), channel_id=1, source_target_pairs={{0,1},{1,0},{2,3},{3,2},{4,5},{5,4},{6,7},{7,6},{8,9},{9,8},{10,11... | collective-permute-start | bytes 221192 | tf_op jit(solution)/shard_map/ppermute | solution.py:414
  13.9 0.9 %collective-permute-done.2 = f32[72,256]{1,0:T(8,128)S(1)} collective-permute-done((f32[72,256]{1,0:T(8,128)S(1)}, f32[72,256]{1,0:T(8,128)S(1)}, u32[]{:S(2)}, u32[]{:S(2)}) %collective-permute-start.2) | collective-permute-done | bytes 73760 | tf_op jit(solution)/shard_map/ppermute | solution.py:414
  14.8 0.1 collective-permute-start.3
  14.9 4.5 %collective-permute-done.3 = f32[72,256]{1,0:T(8,128)S(1)} collective-permute-done((f32[72,256]{1,0:T(8,128)S(1)}, f32[72,256]{1,0:T(8,128)S(1)}, u32[]{:S(2)}, u32[]{:S(2)}) %collective-permute-start.3) | collective-permute-done | bytes 73760 | tf_op jit(solution)/shard_map/ppermute | solution.py:417
  19.4 0.1 collective-permute-start.4
  19.5 4.3 %collective-permute-done.4 = f32[72,256]{1,0:T(8,128)S(1)} collective-permute-done((f32[72,256]{1,0:T(8,128)S(1)}, f32[72,256]{1,0:T(8,128)S(1)}, u32[]{:S(2)}, u32[]{:S(2)}) %collective-permute-start.4) | collective-permute-done | bytes 73760 | tf_op jit(solution)/shard_map/ppermute | solution.py:417
  23.9 0.8 %collective-permute-start.5 = (f32[72,256]{1,0:T(8,128)S(1)}, f32[72,256]{1,0:T(8,128)S(1)}, u32[]{:S(2)}, u32[]{:S(2)}) collective-permute-start(f32[72,256]{1,0:T(8,128)S(1)} %add.19), channel_id=1, source_target_pairs={{0,8},{1,9},{2,10},{3,11},{4,12},{5,13},{6,14},{7,15},{8,0},{9,1},... | collective-permute-start | bytes 221192 | tf_op jit(solution)/shard_map/ppermute | solution.py:417
  24.6 4.8 %collective-permute-done.5 = f32[72,256]{1,0:T(8,128)S(1)} collective-permute-done((f32[72,256]{1,0:T(8,128)S(1)}, f32[72,256]{1,0:T(8,128)S(1)}, u32[]{:S(2)}, u32[]{:S(2)}) %collective-permute-start.5) | collective-permute-done | bytes 73760 | tf_op jit(solution)/shard_map/ppermute | solution.py:417
  29.4 0.1 collective-permute-start.6
  29.5 1.3 %collective-permute-done.6.other_ref = f32[72,256]{1,0:T(8,128)S(1)} collective-permute-done((f32[72,256]{1,0:T(8,128)S(1)}, f32[72,256]{1,0:T(8,128)S(1)}, u32[]{:S(2)}, u32[]{:S(2)}) %collective-permute-start.6) | collective-permute-done | bytes 73760 | tf_op jit(solution)/shard_map/ppermute | solution.py:419
  30.8 9.6 %shard_map.62 = (f32[256,256]{1,0:T(8,128)}, bf16[3,3,10,128,256]{4,3,2,1,0:T(8,128)(2,1)}) custom-call(s32[1]{0:T(128)} %bitcast.parity_ref, f32[72,256]{1,0:T(8,128)S(1)} %add.20.mine_ref, f32[72,256]{1,0:T(8,128)S(1)} %collective-permute-done.6.other_ref, bf16[3,10,128,256]{3,2,1,0:T(8,128)(2,1)S(1)} %get-tuple-element.29.x_ref, ...), custom_call_target="tpu_custom_call" | custom-call | tf_op jit(solution)/shard_map/pallas_call | solution.py:421
  (4 shorter events, 0.0 us)
Async XLA Ops:
  1.6 9.0 %collective-permute-start.1 = (f32[240,128]{1,0:T(8,128)S(1)}, f32[240,128]{1,0:T(8,128)S(1)}, u32[]{:S(2)}, u32[]{:S(2)}) collective-permute-start(f32[240,128]{1,0:T(8,128)S(1)} %get-tuple-element.22), channel_id=1, source_target_pairs={{0,15},{1,2},{2,1},{3,4},{4,3},{5,6},{6,5},{7,8},{8,7},{9,10},{10,... | collective-permute-start | bytes 368648 | tf_op jit(solution)/shard_map/ppermute | solution.py:387
  7.1 3.5 %collective-permute-start = (f32[240,128]{1,0:T(8,128)S(1)}, f32[240,128]{1,0:T(8,128)S(1)}, u32[]{:S(2)}, u32[]{:S(2)}) collective-permute-start(f32[240,128]{1,0:T(8,128)S(1)} %get-tuple-element.22), channel_id=1, source_target_pairs={{0,1},{1,0},{2,3},{3,2},{4,5},{5,4},{6,7},{7,6},{8,9},{9,8},{10,11... | collective-permute-start | bytes 368648 | tf_op jit(solution)/shard_map/ppermute | solution.py:388
  13.3 1.5 %collective-permute-start.2 = (f32[72,256]{1,0:T(8,128)S(1)}, f32[72,256]{1,0:T(8,128)S(1)}, u32[]{:S(2)}, u32[]{:S(2)}) collective-permute-start(f32[72,256]{1,0:T(8,128)S(1)} %get-tuple-element.28), channel_id=1, source_target_pairs={{0,1},{1,0},{2,3},{3,2},{4,5},{5,4},{6,7},{7,6},{8,9},{9,8},{10,11... | collective-permute-start | bytes 221192 | tf_op jit(solution)/shard_map/ppermute | solution.py:414
  14.8 4.6 %collective-permute-start.3 = (f32[72,256]{1,0:T(8,128)S(1)}, f32[72,256]{1,0:T(8,128)S(1)}, u32[]{:S(2)}, u32[]{:S(2)}) collective-permute-start(f32[72,256]{1,0:T(8,128)S(1)} %add.17), channel_id=1, source_target_pairs={{0,2},{1,3},{2,0},{3,1},{4,6},{5,7},{6,4},{7,5},{8,10},{9,11},{10,... | collective-permute-start | bytes 221192 | tf_op jit(solution)/shard_map/ppermute | solution.py:417
  19.4 4.4 %collective-permute-start.4 = (f32[72,256]{1,0:T(8,128)S(1)}, f32[72,256]{1,0:T(8,128)S(1)}, u32[]{:S(2)}, u32[]{:S(2)}) collective-permute-start(f32[72,256]{1,0:T(8,128)S(1)} %add.18), channel_id=1, source_target_pairs={{0,4},{1,5},{2,6},{3,7},{4,0},{5,1},{6,2},{7,3},{8,12},{9,13},{10,... | collective-permute-start | bytes 221192 | tf_op jit(solution)/shard_map/ppermute | solution.py:417
  23.9 5.5 %collective-permute-start.5 = (f32[72,256]{1,0:T(8,128)S(1)}, f32[72,256]{1,0:T(8,128)S(1)}, u32[]{:S(2)}, u32[]{:S(2)}) collective-permute-start(f32[72,256]{1,0:T(8,128)S(1)} %add.19), channel_id=1, source_target_pairs={{0,8},{1,9},{2,10},{3,11},{4,12},{5,13},{6,14},{7,15},{8,0},{9,1},... | collective-permute-start | bytes 221192 | tf_op jit(solution)/shard_map/ppermute | solution.py:417
  29.4 1.3 %collective-permute-start.6 = (f32[72,256]{1,0:T(8,128)S(1)}, f32[72,256]{1,0:T(8,128)S(1)}, u32[]{:S(2)}, u32[]{:S(2)}) collective-permute-start(f32[72,256]{1,0:T(8,128)S(1)} %add.20.mine_ref), channel_id=1, source_target_pairs={{0,1},{1,0},{2,3},{3,2},{4,5},{5,4},{6,7},{7,6},{8,9},{9,8},{10,11... | collective-permute-start | bytes 221192 | tf_op jit(solution)/shard_map/ppermute | solution.py:419

commit v7 on v6

--- a/solution.py
+++ b/solution.py
@@ -226,6 +226,11 @@
     gram_ref[...] = jnp.zeros_like(gram_ref)
     right = gain_matrix(omega_ref[...], rows)
     right_ref[...] = right
+    edges = span_edges(rim_ref, 0, turn_ref)
+    for s in range(snaps):
+        for i in range(slabs):
+            part_ref[0, s, i] = span_diff(vel_ref[s, 0, i, 3 : 3 + rows], edges[s, i])
+            part_ref[1, s, i] = wall_diff(vel_ref[s, 0, i], rows)
     edges = span_edges(rim_ref, 1, turn_ref)
     for i in range(slabs):
         vort = [
@@ -234,11 +239,6 @@
         ]
         copies[i].wait()
         update_block(vort, right, x_ref.at[i], gram_ref)
-    edges = span_edges(rim_ref, 0, turn_ref)
-    for s in range(snaps):
-        for i in range(slabs):
-            part_ref[0, s, i] = span_diff(vel_ref[s, 0, i, 3 : 3 + rows], edges[s, i])
-            part_ref[1, s, i] = wall_diff(vel_ref[s, 0, i], rows)
     for copy in copies[slabs:]:
         copy.wait()
 

time: 40.5 us -> 40.3 us (level)
  transfers between devices with their start and end apart: 7 -> 7, of which waited for: 5 -> 5; matrix products, arithmetic and copies ran while one was open for 0% -> 0% of each run, Pallas kernels for 9% -> 8%
where the time goes in v7:
time: 40.3 us; the launch traced here: 40.1 us
  Pallas kernels  16.5 us (41%)
  waiting for transfers between devices  15.6 us (39%)
  starting transfers between devices  7.27 us (18%)
  between operations  0.7 us (2%)
    ppermute x3, waiting for transfers between devices, local(): total = total + lax.ppermute(total, 'gx', swap(step))  13.4 us
    pallas_call x1, Pallas kernels, local(): pl.pallas_call(functools.partial(basis_kernel, 1.0 / entries), out_shape=...  9.55 us
    ppermute x1, starting transfers between devices, local(): lax.ppermute(outer, 'gx', [(i, ring(i + (1 if i % 2 else -1))) for i in r...  5.48 us
    pallas_call x1, Pallas kernels, local(): pl.pallas_call(first_component_kernel, out_shape=[held, held, held, squar...  3.28 us
    pallas_call x1, Pallas kernels, local(): pl.pallas_call(other_components_kernel, out_shape=[held, held, piece, pie...  2.66 us
    ppermute x1, waiting for transfers between devices, local(): other = lax.ppermute(total, 'gx', swap(1))  1.25 us
    ppermute x3, starting transfers between devices, local(): total = total + lax.ppermute(total, 'gx', swap(step))  1.15 us
    pallas_call x1, Pallas kernels, local(): pl.pallas_call(start_kernel, out_shape=[pltpu.VMEM((snaps * 2 * slabs * r...  1.01 us
  transfers between devices with their start and end apart: 7, of which 5 were waited for; matrix products, arithmetic and copies ran while one was open for 0% of the time, Pallas kernels for 8%

profile of v7, /device:TPU:0, one launch (start us, length us, event | category | flops | bytes accessed | tf_op | source)
XLA Modules:
  0.0 40.1 jit_solution(13842637071455759497)
XLA Ops:
  0.6 1.0 %shard_map.59 = (f32[240,128]{1,0:T(8,128)S(1)}, f32[4,3,3,16,128]{4,3,2,1,0:T(8,128)S(1)}, f32[4,3,6,2,10]{4,3,2,1,0:T(2,128)S(1)}, f32[4,256]{1,0:T(4,128)S(1)}) custom-call(f32[4,3,3,16,128]{4,3,2,1,0:T(8,128)} %vel_in.1, f32[4,3,6,2,10]{4,3,2,1,0:T(2,128)} %bitcast.2, f32[4,256]{1,0:T(4,128)} %omega_in.1), custom_call_target="tpu_custom_call" | custom-call | tf_op jit(solution)/shard_map/pallas_call | solution.py:371
  1.6 5.5 %collective-permute-start.1 = (f32[240,128]{1,0:T(8,128)S(1)}, f32[240,128]{1,0:T(8,128)S(1)}, u32[]{:S(2)}, u32[]{:S(2)}) collective-permute-start(f32[240,128]{1,0:T(8,128)S(1)} %get-tuple-element.22), channel_id=1, source_target_pairs={{0,15},{1,2},{2,1},{3,4},{4,3},{5,6},{6,5},{7,8},{8,7},{9,10},{10,... | collective-permute-start | bytes 368648 | tf_op jit(solution)/shard_map/ppermute | solution.py:387
  7.1 0.0 collective-permute-start
  7.1 3.3 %shard_map.60 = (bf16[3,10,128,256]{3,2,1,0:T(8,128)(2,1)S(1)}, bf16[3,10,128,256]{3,2,1,0:T(8,128)(2,1)S(1)}, bf16[3,10,128,256]{3,2,1,0:T(8,128)(2,1)S(1)}, f3...) custom-call(f32[4,3,3,16,128]{4,3,2,1,0:T(8,128)S(1)} %get-tuple-element.18.vel_ref, ...), custom_call_target="tpu_custom_call" | custom-call | tf_op jit(solution)/shard_map/pallas_call | solution.py:390
  10.4 0.0 collective-permute-done.1.outer_ref
  10.4 0.0 collective-permute-done.inner_ref
  10.4 2.7 %shard_map.61 = (bf16[3,10,128,256]{3,2,1,0:T(8,128)(2,1)S(1)}, bf16[3,10,128,256]{3,2,1,0:T(8,128)(2,1)S(1)}, f32[72,256]{1,0:T(8,128)S(1)}, f32[72,256]{1,0:T(8,128)S(1)}) custom-call(s32[1]{0:T(128)} %bitcast.parity_ref, f32[4,3,3,16,128]{4,3,2,1,0:T(8,128)S(1)} %get-tuple-element.18.vel_ref, ...), custom_call_target="tpu_custom_call", output_to_operand_aliasing={{0}: (7, {}), {1}: (8, {})} | custom-call | tf_op jit(solution)/shard_map/pallas_call | solution.py:401
  13.1 0.6 %collective-permute-start.2 = (f32[72,256]{1,0:T(8,128)S(1)}, f32[72,256]{1,0:T(8,128)S(1)}, u32[]{:S(2)}, u32[]{:S(2)}) collective-permute-start(f32[72,256]{1,0:T(8,128)S(1)} %get-tuple-element.28), channel_id=1, source_target_pairs={{0,1},{1,0},{2,3},{3,2},{4,5},{5,4},{6,7},{7,6},{8,9},{9,8},{10,11... | collective-permute-start | bytes 221192 | tf_op jit(solution)/shard_map/ppermute | solution.py:414
  13.7 0.9 %collective-permute-done.2 = f32[72,256]{1,0:T(8,128)S(1)} collective-permute-done((f32[72,256]{1,0:T(8,128)S(1)}, f32[72,256]{1,0:T(8,128)S(1)}, u32[]{:S(2)}, u32[]{:S(2)}) %collective-permute-start.2) | collective-permute-done | bytes 73760 | tf_op jit(solution)/shard_map/ppermute | solution.py:414
  14.6 0.1 collective-permute-start.3
  14.7 4.5 %collective-permute-done.3 = f32[72,256]{1,0:T(8,128)S(1)} collective-permute-done((f32[72,256]{1,0:T(8,128)S(1)}, f32[72,256]{1,0:T(8,128)S(1)}, u32[]{:S(2)}, u32[]{:S(2)}) %collective-permute-start.3) | collective-permute-done | bytes 73760 | tf_op jit(solution)/shard_map/ppermute | solution.py:417
  19.2 0.1 collective-permute-start.4
  19.3 4.3 %collective-permute-done.4 = f32[72,256]{1,0:T(8,128)S(1)} collective-permute-done((f32[72,256]{1,0:T(8,128)S(1)}, f32[72,256]{1,0:T(8,128)S(1)}, u32[]{:S(2)}, u32[]{:S(2)}) %collective-permute-start.4) | collective-permute-done | bytes 73760 | tf_op jit(solution)/shard_map/ppermute | solution.py:417
  23.6 1.0 %collective-permute-start.5 = (f32[72,256]{1,0:T(8,128)S(1)}, f32[72,256]{1,0:T(8,128)S(1)}, u32[]{:S(2)}, u32[]{:S(2)}) collective-permute-start(f32[72,256]{1,0:T(8,128)S(1)} %add.19), channel_id=1, source_target_pairs={{0,8},{1,9},{2,10},{3,11},{4,12},{5,13},{6,14},{7,15},{8,0},{9,1},... | collective-permute-start | bytes 221192 | tf_op jit(solution)/shard_map/ppermute | solution.py:417
  24.6 4.6 %collective-permute-done.5 = f32[72,256]{1,0:T(8,128)S(1)} collective-permute-done((f32[72,256]{1,0:T(8,128)S(1)}, f32[72,256]{1,0:T(8,128)S(1)}, u32[]{:S(2)}, u32[]{:S(2)}) %collective-permute-start.5) | collective-permute-done | bytes 73760 | tf_op jit(solution)/shard_map/ppermute | solution.py:417
  29.2 0.1 collective-permute-start.6
  29.3 1.3 %collective-permute-done.6.other_ref = f32[72,256]{1,0:T(8,128)S(1)} collective-permute-done((f32[72,256]{1,0:T(8,128)S(1)}, f32[72,256]{1,0:T(8,128)S(1)}, u32[]{:S(2)}, u32[]{:S(2)}) %collective-permute-start.6) | collective-permute-done | bytes 73760 | tf_op jit(solution)/shard_map/ppermute | solution.py:419
  30.6 9.6 %shard_map.62 = (f32[256,256]{1,0:T(8,128)}, bf16[3,3,10,128,256]{4,3,2,1,0:T(8,128)(2,1)}) custom-call(s32[1]{0:T(128)} %bitcast.parity_ref, f32[72,256]{1,0:T(8,128)S(1)} %add.20.mine_ref, f32[72,256]{1,0:T(8,128)S(1)} %collective-permute-done.6.other_ref, bf16[3,10,128,256]{3,2,1,0:T(8,128)(2,1)S(1)} %get-tuple-element.29.x_ref, ...), custom_call_target="tpu_custom_call" | custom-call | tf_op jit(solution)/shard_map/pallas_call | solution.py:421
  (4 shorter events, 0.0 us)
Async XLA Ops:
  1.6 8.8 %collective-permute-start.1 = (f32[240,128]{1,0:T(8,128)S(1)}, f32[240,128]{1,0:T(8,128)S(1)}, u32[]{:S(2)}, u32[]{:S(2)}) collective-permute-start(f32[240,128]{1,0:T(8,128)S(1)} %get-tuple-element.22), channel_id=1, source_target_pairs={{0,15},{1,2},{2,1},{3,4},{4,3},{5,6},{6,5},{7,8},{8,7},{9,10},{10,... | collective-permute-start | bytes 368648 | tf_op jit(solution)/shard_map/ppermute | solution.py:387
  7.1 3.3 %collective-permute-start = (f32[240,128]{1,0:T(8,128)S(1)}, f32[240,128]{1,0:T(8,128)S(1)}, u32[]{:S(2)}, u32[]{:S(2)}) collective-permute-start(f32[240,128]{1,0:T(8,128)S(1)} %get-tuple-element.22), channel_id=1, source_target_pairs={{0,1},{1,0},{2,3},{3,2},{4,5},{5,4},{6,7},{7,6},{8,9},{9,8},{10,11... | collective-permute-start | bytes 368648 | tf_op jit(solution)/shard_map/ppermute | solution.py:388
  13.1 1.5 %collective-permute-start.2 = (f32[72,256]{1,0:T(8,128)S(1)}, f32[72,256]{1,0:T(8,128)S(1)}, u32[]{:S(2)}, u32[]{:S(2)}) collective-permute-start(f32[72,256]{1,0:T(8,128)S(1)} %get-tuple-element.28), channel_id=1, source_target_pairs={{0,1},{1,0},{2,3},{3,2},{4,5},{5,4},{6,7},{7,6},{8,9},{9,8},{10,11... | collective-permute-start | bytes 221192 | tf_op jit(solution)/shard_map/ppermute | solution.py:414
  14.6 4.6 %collective-permute-start.3 = (f32[72,256]{1,0:T(8,128)S(1)}, f32[72,256]{1,0:T(8,128)S(1)}, u32[]{:S(2)}, u32[]{:S(2)}) collective-permute-start(f32[72,256]{1,0:T(8,128)S(1)} %add.17), channel_id=1, source_target_pairs={{0,2},{1,3},{2,0},{3,1},{4,6},{5,7},{6,4},{7,5},{8,10},{9,11},{10,... | collective-permute-start | bytes 221192 | tf_op jit(solution)/shard_map/ppermute | solution.py:417
  19.2 4.4 %collective-permute-start.4 = (f32[72,256]{1,0:T(8,128)S(1)}, f32[72,256]{1,0:T(8,128)S(1)}, u32[]{:S(2)}, u32[]{:S(2)}) collective-permute-start(f32[72,256]{1,0:T(8,128)S(1)} %add.18), channel_id=1, source_target_pairs={{0,4},{1,5},{2,6},{3,7},{4,0},{5,1},{6,2},{7,3},{8,12},{9,13},{10,... | collective-permute-start | bytes 221192 | tf_op jit(solution)/shard_map/ppermute | solution.py:417
  23.6 5.6 %collective-permute-start.5 = (f32[72,256]{1,0:T(8,128)S(1)}, f32[72,256]{1,0:T(8,128)S(1)}, u32[]{:S(2)}, u32[]{:S(2)}) collective-permute-start(f32[72,256]{1,0:T(8,128)S(1)} %add.19), channel_id=1, source_target_pairs={{0,8},{1,9},{2,10},{3,11},{4,12},{5,13},{6,14},{7,15},{8,0},{9,1},... | collective-permute-start | bytes 221192 | tf_op jit(solution)/shard_map/ppermute | solution.py:417
  29.2 1.3 %collective-permute-start.6 = (f32[72,256]{1,0:T(8,128)S(1)}, f32[72,256]{1,0:T(8,128)S(1)}, u32[]{:S(2)}, u32[]{:S(2)}) collective-permute-start(f32[72,256]{1,0:T(8,128)S(1)} %add.20.mine_ref), channel_id=1, source_target_pairs={{0,1},{1,0},{2,3},{3,2},{4,5},{5,4},{6,7},{7,6},{8,9},{9,8},{10,11... | collective-permute-start | bytes 221192 | tf_op jit(solution)/shard_map/ppermute | solution.py:419

commit v8 on v7

--- a/solution.py
+++ b/solution.py
@@ -89,9 +89,9 @@
         half, off = b0 // 128, b0 % 128
         inside = (lane >= off) & (lane < off + WIDE)
         here = slice(128 * half, 128 * half + 128)
-        w_ref[...] = jnp.where(inside, t_ref[b0:stop, here], jnp.where(lane == sub + (WIDE - off), 1.0, 0.0))
+        w_ref[:WIDE] = jnp.where(inside, t_ref[b0:stop, here], jnp.where(lane == sub + (WIDE - off), 1.0, 0.0))
         factor_block(w_ref, off, spare if b0 >= order // 2 else [])
-        done = w_ref[...]
+        done = w_ref[:WIDE]
         moved = pltpu.roll(done, 64, 1)
         low, high = (moved, done) if off == 0 else (done, moved)
         x1, x2, x3 = parts_of(low)
@@ -427,7 +427,7 @@
             pltpu.VMEM((rank, rank), jnp.float32),
             pltpu.VMEM((rank, rank), jnp.float32),
             pltpu.VMEM((rank, rank), jnp.float32),
-            pltpu.VMEM((WIDE, 128), jnp.float32),
+            pltpu.VMEM((WIDE + 8, 128), jnp.float32),
             pltpu.VMEM((3, *block[:-1], rank // 2), jnp.bfloat16),
             pltpu.VMEM((3, *block[:-1], rank // 2), jnp.bfloat16),
             pltpu.SemaphoreType.DMA,

time: 40.3 us -> 40.3 us (level)
  no operation moved by 1% of the time
where the time goes in v8:
time: 40.3 us; the launch traced here: 40.1 us
  Pallas kernels  16.5 us (41%)
  waiting for transfers between devices  15.6 us (39%)
  starting transfers between devices  7.27 us (18%)
  between operations  0.7 us (2%)
    ppermute x3, waiting for transfers between devices, local(): total = total + lax.ppermute(total, 'gx', swap(step))  13.4 us
    pallas_call x1, Pallas kernels, local(): pl.pallas_call(functools.partial(basis_kernel, 1.0 / entries), out_shape=...  9.55 us
    ppermute x1, starting transfers between devices, local(): lax.ppermute(outer, 'gx', [(i, ring(i + (1 if i % 2 else -1))) for i in r...  5.48 us
    pallas_call x1, Pallas kernels, local(): pl.pallas_call(first_component_kernel, out_shape=[held, held, held, squar...  3.28 us
    pallas_call x1, Pallas kernels, local(): pl.pallas_call(other_components_kernel, out_shape=[held, held, piece, pie...  2.66 us
    ppermute x1, waiting for transfers between devices, local(): other = lax.ppermute(total, 'gx', swap(1))  1.25 us
    ppermute x3, starting transfers between devices, local(): total = total + lax.ppermute(total, 'gx', swap(step))  1.15 us
    pallas_call x1, Pallas kernels, local(): pl.pallas_call(start_kernel, out_shape=[pltpu.VMEM((snaps * 2 * slabs * r...  1.01 us
  transfers between devices with their start and end apart: 7, of which 5 were waited for; matrix products, arithmetic and copies ran while one was open for 0% of the time, Pallas kernels for 8%

profile of v8, /device:TPU:0, one launch (start us, length us, event | category | flops | bytes accessed | tf_op | source)
XLA Modules:
  0.0 40.1 jit_solution(5604566605910716643)
XLA Ops:
  0.6 1.0 %shard_map.59 = (f32[240,128]{1,0:T(8,128)S(1)}, f32[4,3,3,16,128]{4,3,2,1,0:T(8,128)S(1)}, f32[4,3,6,2,10]{4,3,2,1,0:T(2,128)S(1)}, f32[4,256]{1,0:T(4,128)S(1)}) custom-call(f32[4,3,3,16,128]{4,3,2,1,0:T(8,128)} %vel_in.1, f32[4,3,6,2,10]{4,3,2,1,0:T(2,128)} %bitcast.2, f32[4,256]{1,0:T(4,128)} %omega_in.1), custom_call_target="tpu_custom_call" | custom-call | tf_op jit(solution)/shard_map/pallas_call | solution.py:371
  1.6 5.5 %collective-permute-start.1 = (f32[240,128]{1,0:T(8,128)S(1)}, f32[240,128]{1,0:T(8,128)S(1)}, u32[]{:S(2)}, u32[]{:S(2)}) collective-permute-start(f32[240,128]{1,0:T(8,128)S(1)} %get-tuple-element.22), channel_id=1, source_target_pairs={{0,15},{1,2},{2,1},{3,4},{4,3},{5,6},{6,5},{7,8},{8,7},{9,10},{10,... | collective-permute-start | bytes 368648 | tf_op jit(solution)/shard_map/ppermute | solution.py:387
  7.1 0.0 collective-permute-start
  7.1 3.3 %shard_map.60 = (bf16[3,10,128,256]{3,2,1,0:T(8,128)(2,1)S(1)}, bf16[3,10,128,256]{3,2,1,0:T(8,128)(2,1)S(1)}, bf16[3,10,128,256]{3,2,1,0:T(8,128)(2,1)S(1)}, f3...) custom-call(f32[4,3,3,16,128]{4,3,2,1,0:T(8,128)S(1)} %get-tuple-element.18.vel_ref, ...), custom_call_target="tpu_custom_call" | custom-call | tf_op jit(solution)/shard_map/pallas_call | solution.py:390
  10.4 0.0 collective-permute-done.1.outer_ref
  10.4 0.0 collective-permute-done.inner_ref
  10.4 2.7 %shard_map.61 = (bf16[3,10,128,256]{3,2,1,0:T(8,128)(2,1)S(1)}, bf16[3,10,128,256]{3,2,1,0:T(8,128)(2,1)S(1)}, f32[72,256]{1,0:T(8,128)S(1)}, f32[72,256]{1,0:T(8,128)S(1)}) custom-call(s32[1]{0:T(128)} %bitcast.parity_ref, f32[4,3,3,16,128]{4,3,2,1,0:T(8,128)S(1)} %get-tuple-element.18.vel_ref, ...), custom_call_target="tpu_custom_call", output_to_operand_aliasing={{0}: (7, {}), {1}: (8, {})} | custom-call | tf_op jit(solution)/shard_map/pallas_call | solution.py:401
  13.1 0.6 %collective-permute-start.2 = (f32[72,256]{1,0:T(8,128)S(1)}, f32[72,256]{1,0:T(8,128)S(1)}, u32[]{:S(2)}, u32[]{:S(2)}) collective-permute-start(f32[72,256]{1,0:T(8,128)S(1)} %get-tuple-element.28), channel_id=1, source_target_pairs={{0,1},{1,0},{2,3},{3,2},{4,5},{5,4},{6,7},{7,6},{8,9},{9,8},{10,11... | collective-permute-start | bytes 221192 | tf_op jit(solution)/shard_map/ppermute | solution.py:414
  13.7 0.9 %collective-permute-done.2 = f32[72,256]{1,0:T(8,128)S(1)} collective-permute-done((f32[72,256]{1,0:T(8,128)S(1)}, f32[72,256]{1,0:T(8,128)S(1)}, u32[]{:S(2)}, u32[]{:S(2)}) %collective-permute-start.2) | collective-permute-done | bytes 73760 | tf_op jit(solution)/shard_map/ppermute | solution.py:414
  14.6 0.1 collective-permute-start.3
  14.7 4.5 %collective-permute-done.3 = f32[72,256]{1,0:T(8,128)S(1)} collective-permute-done((f32[72,256]{1,0:T(8,128)S(1)}, f32[72,256]{1,0:T(8,128)S(1)}, u32[]{:S(2)}, u32[]{:S(2)}) %collective-permute-start.3) | collective-permute-done | bytes 73760 | tf_op jit(solution)/shard_map/ppermute | solution.py:417
  19.2 0.1 collective-permute-start.4
  19.3 4.3 %collective-permute-done.4 = f32[72,256]{1,0:T(8,128)S(1)} collective-permute-done((f32[72,256]{1,0:T(8,128)S(1)}, f32[72,256]{1,0:T(8,128)S(1)}, u32[]{:S(2)}, u32[]{:S(2)}) %collective-permute-start.4) | collective-permute-done | bytes 73760 | tf_op jit(solution)/shard_map/ppermute | solution.py:417
  23.6 1.0 %collective-permute-start.5 = (f32[72,256]{1,0:T(8,128)S(1)}, f32[72,256]{1,0:T(8,128)S(1)}, u32[]{:S(2)}, u32[]{:S(2)}) collective-permute-start(f32[72,256]{1,0:T(8,128)S(1)} %add.19), channel_id=1, source_target_pairs={{0,8},{1,9},{2,10},{3,11},{4,12},{5,13},{6,14},{7,15},{8,0},{9,1},... | collective-permute-start | bytes 221192 | tf_op jit(solution)/shard_map/ppermute | solution.py:417
  24.6 4.6 %collective-permute-done.5 = f32[72,256]{1,0:T(8,128)S(1)} collective-permute-done((f32[72,256]{1,0:T(8,128)S(1)}, f32[72,256]{1,0:T(8,128)S(1)}, u32[]{:S(2)}, u32[]{:S(2)}) %collective-permute-start.5) | collective-permute-done | bytes 73760 | tf_op jit(solution)/shard_map/ppermute | solution.py:417
  29.2 0.1 collective-permute-start.6
  29.3 1.3 %collective-permute-done.6.other_ref = f32[72,256]{1,0:T(8,128)S(1)} collective-permute-done((f32[72,256]{1,0:T(8,128)S(1)}, f32[72,256]{1,0:T(8,128)S(1)}, u32[]{:S(2)}, u32[]{:S(2)}) %collective-permute-start.6) | collective-permute-done | bytes 73760 | tf_op jit(solution)/shard_map/ppermute | solution.py:419
  30.6 9.6 %shard_map.62 = (f32[256,256]{1,0:T(8,128)}, bf16[3,3,10,128,256]{4,3,2,1,0:T(8,128)(2,1)}) custom-call(s32[1]{0:T(128)} %bitcast.parity_ref, f32[72,256]{1,0:T(8,128)S(1)} %add.20.mine_ref, f32[72,256]{1,0:T(8,128)S(1)} %collective-permute-done.6.other_ref, bf16[3,10,128,256]{3,2,1,0:T(8,128)(2,1)S(1)} %get-tuple-element.29.x_ref, ...), custom_call_target="tpu_custom_call" | custom-call | tf_op jit(solution)/shard_map/pallas_call | solution.py:421
  (4 shorter events, 0.0 us)
Async XLA Ops:
  1.6 8.8 %collective-permute-start.1 = (f32[240,128]{1,0:T(8,128)S(1)}, f32[240,128]{1,0:T(8,128)S(1)}, u32[]{:S(2)}, u32[]{:S(2)}) collective-permute-start(f32[240,128]{1,0:T(8,128)S(1)} %get-tuple-element.22), channel_id=1, source_target_pairs={{0,15},{1,2},{2,1},{3,4},{4,3},{5,6},{6,5},{7,8},{8,7},{9,10},{10,... | collective-permute-start | bytes 368648 | tf_op jit(solution)/shard_map/ppermute | solution.py:387
  7.1 3.3 %collective-permute-start = (f32[240,128]{1,0:T(8,128)S(1)}, f32[240,128]{1,0:T(8,128)S(1)}, u32[]{:S(2)}, u32[]{:S(2)}) collective-permute-start(f32[240,128]{1,0:T(8,128)S(1)} %get-tuple-element.22), channel_id=1, source_target_pairs={{0,1},{1,0},{2,3},{3,2},{4,5},{5,4},{6,7},{7,6},{8,9},{9,8},{10,11... | collective-permute-start | bytes 368648 | tf_op jit(solution)/shard_map/ppermute | solution.py:388
  13.1 1.5 %collective-permute-start.2 = (f32[72,256]{1,0:T(8,128)S(1)}, f32[72,256]{1,0:T(8,128)S(1)}, u32[]{:S(2)}, u32[]{:S(2)}) collective-permute-start(f32[72,256]{1,0:T(8,128)S(1)} %get-tuple-element.28), channel_id=1, source_target_pairs={{0,1},{1,0},{2,3},{3,2},{4,5},{5,4},{6,7},{7,6},{8,9},{9,8},{10,11... | collective-permute-start | bytes 221192 | tf_op jit(solution)/shard_map/ppermute | solution.py:414
  14.6 4.6 %collective-permute-start.3 = (f32[72,256]{1,0:T(8,128)S(1)}, f32[72,256]{1,0:T(8,128)S(1)}, u32[]{:S(2)}, u32[]{:S(2)}) collective-permute-start(f32[72,256]{1,0:T(8,128)S(1)} %add.17), channel_id=1, source_target_pairs={{0,2},{1,3},{2,0},{3,1},{4,6},{5,7},{6,4},{7,5},{8,10},{9,11},{10,... | collective-permute-start | bytes 221192 | tf_op jit(solution)/shard_map/ppermute | solution.py:417
  19.2 4.4 %collective-permute-start.4 = (f32[72,256]{1,0:T(8,128)S(1)}, f32[72,256]{1,0:T(8,128)S(1)}, u32[]{:S(2)}, u32[]{:S(2)}) collective-permute-start(f32[72,256]{1,0:T(8,128)S(1)} %add.18), channel_id=1, source_target_pairs={{0,4},{1,5},{2,6},{3,7},{4,0},{5,1},{6,2},{7,3},{8,12},{9,13},{10,... | collective-permute-start | bytes 221192 | tf_op jit(solution)/shard_map/ppermute | solution.py:417
  23.6 5.6 %collective-permute-start.5 = (f32[72,256]{1,0:T(8,128)S(1)}, f32[72,256]{1,0:T(8,128)S(1)}, u32[]{:S(2)}, u32[]{:S(2)}) collective-permute-start(f32[72,256]{1,0:T(8,128)S(1)} %add.19), channel_id=1, source_target_pairs={{0,8},{1,9},{2,10},{3,11},{4,12},{5,13},{6,14},{7,15},{8,0},{9,1},... | collective-permute-start | bytes 221192 | tf_op jit(solution)/shard_map/ppermute | solution.py:417
  29.2 1.3 %collective-permute-start.6 = (f32[72,256]{1,0:T(8,128)S(1)}, f32[72,256]{1,0:T(8,128)S(1)}, u32[]{:S(2)}, u32[]{:S(2)}) collective-permute-start(f32[72,256]{1,0:T(8,128)S(1)} %add.20.mine_ref), channel_id=1, source_target_pairs={{0,1},{1,0},{2,3},{3,2},{4,5},{5,4},{6,7},{7,6},{8,9},{9,8},{10,11... | collective-permute-start | bytes 221192 | tf_op jit(solution)/shard_map/ppermute | solution.py:419

commit v9 on v8

--- a/solution.py
+++ b/solution.py
@@ -191,7 +191,7 @@
     acc_ref[...] += lax.dot_general(block, block, (((0,), (0,)), ((), ())), preferred_element_type=jnp.float32)
 
 
-def start_kernel(vel_in, rim_in, omega_in, band_ref, vel_ref, rim_ref, omega_ref, sems):
+def start_kernel(vel_in, rim_in, omega_in, v_ref, w_ref, vel_ref, rim_ref, omega_ref, sems):
     snaps, _, slabs, height, _ = vel_ref.shape
     rows = height - 6
     copies = [
@@ -204,8 +204,8 @@
     for s in range(snaps):
         for c in range(2):
             for i in range(slabs):
-                at = ((s * 2 + c) * slabs + i) * rows
-                band_ref[at : at + rows] = vel_ref[s, 1 + c, i, 3 : 3 + rows]
+                at = (s * slabs + i) * rows
+                (v_ref, w_ref)[c][at : at + rows] = vel_ref[s, 1 + c, i, 3 : 3 + rows]
     for copy in copies[1:]:
         copy.wait()
 
@@ -260,36 +260,35 @@
     send_ref[part:] = extra
 
 
-def other_components_kernel(
-    parity_ref, vel_ref, part_ref, inner_ref, outer_ref, right_ref, start_ref, old_y_ref, old_z_ref,
-    y_ref, z_ref, keep_ref, send_ref, wide_ref, gram_ref,
+def other_component_kernel(
+    which, parity_ref, vel_ref, part_ref, inner_ref, outer_ref, right_ref, start_ref, old_ref, new_ref, *rest
 ):
-    del old_y_ref, old_z_ref
+    del old_ref
     snaps, _, slabs, height, _ = vel_ref.shape
     rows = height - 6
+    *outs, wide_ref, gram_ref = rest
     gram_ref[...] = start_ref[...]
     right = right_ref[...]
     even = parity_ref[0] == 0
     for s in range(snaps):
-        for c in range(2):
-            for k in range(3):
-                at = ((s * 2 + c) * 3 + k) * rows
-                inner, outer = inner_ref[at : at + rows], outer_ref[at : at + rows]
-                wide_ref[s, c, k] = jnp.where(even, outer, inner)
-                wide_ref[s, c, 3 + slabs + k] = jnp.where(even, inner, outer)
-            for i in range(slabs):
-                wide_ref[s, c, 3 + i] = vel_ref[s, 1 + c, i, 3 : 3 + rows]
+        for k in range(3):
+            at = (s * 3 + k) * rows
+            inner, outer = inner_ref[at : at + rows], outer_ref[at : at + rows]
+            wide_ref[s, k] = jnp.where(even, outer, inner)
+            wide_ref[s, 3 + slabs + k] = jnp.where(even, inner, outer)
+        for i in range(slabs):
+            wide_ref[s, 3 + i] = vel_ref[s, 3 - which, i, 3 : 3 + rows]
     for i in range(slabs):
-        for c, new_ref in enumerate((y_ref, z_ref)):
-            vort = []
-            for s in range(snaps):
-                along = stream_diff([wide_ref[s, 1 - c, i + k] for k in range(7)], 3)
-                if c == 0:
-                    vort.append(part_ref[0, s, i] - along)
-                else:
-                    vort.append(along - part_ref[1, s, i])
-            update_block(vort, right, new_ref.at[i], gram_ref)
-    pack(gram_ref, even, keep_ref, send_ref)
+        vort = []
+        for s in range(snaps):
+            along = stream_diff([wide_ref[s, i + k] for k in range(7)], 3)
+            part = part_ref[which - 1, s, i]
+            vort.append(part - along if which == 1 else along - part)
+        update_block(vort, right, new_ref.at[i], gram_ref)
+    if which == 1:
+        outs[0][...] = gram_ref[...]
+    else:
+        pack(gram_ref, even, *outs)
 
 
 def unpack(packed, part_diag, work_ref):
@@ -368,24 +367,32 @@
     held = pltpu.VMEM(block, jnp.bfloat16)
     old = pltpu.with_memory_space_constraint(sketch_old, pltpu.HBM)
     small = [pltpu.with_memory_space_constraint(x, pltpu.HBM) for x in (velocity, rim, omega)]
-    planes, near_vel, near_rim, near_omega = pl.pallas_call(
+    planes_v, planes_w, near_vel, near_rim, near_omega = pl.pallas_call(
         start_kernel,
-        out_shape=[pltpu.VMEM((snaps * 2 * slabs * rows, cells), jnp.float32)]
+        out_shape=[pltpu.VMEM((snaps * slabs * rows, cells), jnp.float32)] * 2
         + [pltpu.VMEM(x.shape, x.dtype) for x in (velocity, rim, omega)],
         in_specs=[IN_HBM] * 3,
-        out_specs=[IN_VMEM] * 4,
+        out_specs=[IN_VMEM] * 5,
         scratch_shapes=[pltpu.SemaphoreType.DMA((3,))],
         compiler_params=limit,
     )(*small)
-    inner, outer = planes, planes
-    if slabs > 3:
-        whole = planes.reshape(snaps * 2, slabs, rows, cells)
+    ring = lambda i: i % count
+    across = [(i, ring(i + (1 if i % 2 else -1))) for i in range(count)]
+    within = [(i, i ^ 1) for i in range(count)]
+
+    def sides(planes):
+        if slabs == 3:
+            return planes, planes
+        whole = planes.reshape(snaps, slabs, rows, cells)
         head, tail = (x.reshape(-1, cells) for x in (whole[:, :3], whole[:, slabs - 3 :]))
         even = place % 2 == 0
-        inner, outer = jnp.where(even, tail, head), jnp.where(even, head, tail)
-    ring = lambda i: i % count
-    outer = lax.ppermute(outer, "gx", [(i, ring(i + (1 if i % 2 else -1))) for i in range(count)])
-    inner = lax.ppermute(inner, "gx", [(i, i ^ 1) for i in range(count)])
+        return jnp.where(even, tail, head), jnp.where(even, head, tail)
+
+    (inner_w, outer_w), (inner_v, outer_v) = sides(planes_w), sides(planes_v)
+    outer_w = lax.ppermute(outer_w, "gx", across)
+    outer_v = lax.ppermute(outer_v, "gx", across)
+    inner_w = lax.ppermute(inner_w, "gx", within)
+    inner_v = lax.ppermute(inner_v, "gx", within)
     depth = 3 * snaps * rows
     sketch_x, raw_y, raw_z, gram, right, partial = pl.pallas_call(
         first_component_kernel,
@@ -398,18 +405,23 @@
         compiler_params=limit,
     )(near_vel, near_rim, near_omega, old)
     piece = jax.ShapeDtypeStruct((rank // 4 + 8, rank), jnp.float32)
-    sketch_y, sketch_z, keep, send = pl.pallas_call(
-        other_components_kernel,
-        out_shape=[held, held, piece, piece],
-        in_specs=[IN_SMEM] + [IN_VMEM] * 8,
-        out_specs=[IN_VMEM] * 4,
-        scratch_shapes=[
-            pltpu.VMEM((snaps, 2, slabs + 6, rows, cells), jnp.float32),
-            pltpu.VMEM((rank, rank), jnp.float32),
-        ],
-        input_output_aliases={7: 0, 8: 1},
-        compiler_params=limit,
-    )(parity, near_vel, partial, inner, outer, right, gram, raw_y, raw_z)
+
+    def other_component(which, outs, inner, outer, gram, raw):
+        return pl.pallas_call(
+            functools.partial(other_component_kernel, which),
+            out_shape=[held] + outs,
+            in_specs=[IN_SMEM] + [IN_VMEM] * 7,
+            out_specs=[IN_VMEM] * (1 + len(outs)),
+            scratch_shapes=[
+                pltpu.VMEM((snaps, slabs + 6, rows, cells), jnp.float32),
+                pltpu.VMEM((rank, rank), jnp.float32),
+            ],
+            input_output_aliases={7: 0},
+            compiler_params=limit,
+        )(parity, near_vel, partial, inner, outer, right, gram, raw)
+
+    sketch_y, gram = other_component(1, [square], inner_w, outer_w, gram, raw_y)
+    sketch_z, keep, send = other_component(2, [piece, piece], inner_v, outer_v, gram, raw_z)
     swap = lambda k: [(i, i ^ k) for i in range(count)]
     total = keep + lax.ppermute(send, "gx", swap(1))
     step = 2

time: 40.3 us -> 41.9 us (1.040)
  starting transfers between devices: 7.27 us -> 8.21 us
  Pallas kernels: 16.5 us -> 17 us
    ppermute x3, waiting for transfers between devices: 13.4 us -> 12.5 us  [local(): total = total + lax.ppermute(total, 'gx', swap(step))]
    ppermute x2 -> x4, starting transfers between devices: 5.48 us -> 6.24 us  [the longest x1 5.48 us: local(): outer_w = lax.ppermute(outer_w, 'gx', across)]
    ppermute x2 -> x4, waiting for transfers between devices: 0.01 us -> 0.7 us  [the longest x1 0.7 us: local(): outer_v = lax.ppermute(outer_v, 'gx', across)]
    ppermute x3, starting transfers between devices: 1.15 us -> 1.83 us  [local(): total = total + lax.ppermute(total, 'gx', swap(step))]
    pallas_call x2 -> x3, Pallas kernels: 3.66 us -> 4.18 us  [the longest x2 3.17 us: other_component(): pl.pallas_call(functools.partial(other_component_kernel, which), out_shap...]
    ppermute x1, starting transfers between devices: 0.57 us -> 0.07 us  [local(): total = keep + lax.ppermute(send, 'gx', swap(1))]
  transfers between devices with their start and end apart: 7 -> 9, of which waited for: 5 -> 6; matrix products, arithmetic and copies ran while one was open for 0% -> 0% of each run, Pallas kernels for 8% -> 12%
where the time goes in v9:
time: 41.9 us; the launch traced here: 41.7 us
  Pallas kernels  17 us (41%)
  waiting for transfers between devices  15.8 us (38%)
  starting transfers between devices  8.21 us (20%)
  between operations  0.71 us (2%)
    ppermute x3, waiting for transfers between devices, local(): total = total + lax.ppermute(total, 'gx', swap(step))  12.5 us
    pallas_call x1, Pallas kernels, local(): pl.pallas_call(functools.partial(basis_kernel, 1.0 / entries), out_shape=...  9.55 us
    ppermute x1, starting transfers between devices, local(): outer_w = lax.ppermute(outer_w, 'gx', across)  5.48 us
    pallas_call x1, Pallas kernels, local(): pl.pallas_call(first_component_kernel, out_shape=[held, held, held, squar...  3.28 us
    pallas_call x2, Pallas kernels, other_component(): pl.pallas_call(functools.partial(other_component_kernel, which), out_shap...  3.17 us
    ppermute x3, starting transfers between devices, local(): total = total + lax.ppermute(total, 'gx', swap(step))  1.83 us
    ppermute x1, waiting for transfers between devices, local(): total = keep + lax.ppermute(send, 'gx', swap(1))  1.25 us
    ppermute x1, waiting for transfers between devices, local(): other = lax.ppermute(total, 'gx', swap(1))  1.25 us
  transfers between devices with their start and end apart: 9, of which 6 were waited for; matrix products, arithmetic and copies ran while one was open for 0% of the time, Pallas kernels for 12%

profile of v9, /device:TPU:0, one launch (start us, length us, event | category | flops | bytes accessed | tf_op | source)
XLA Modules:
  0.0 41.7 jit_solution(5641647370101420101)
XLA Ops:
  0.6 1.0 %shard_map.59 = (f32[120,128]{1,0:T(8,128)S(1)}, f32[120,128]{1,0:T(8,128)S(1)}, f32[4,3,3,16,128]{4,3,2,1,0:T(8,128)S(1)}, f32[4,3,6,2,10]{4,3,2,1,0:T(2,128)S(1)}, f32[4,256]{1,0:T(4,128)S(1)}) custom-call(f32[4,3,3,16,128]{4,3,2,1,0:T(8,128)} %vel_in.1, f32[4,3,6,2,10]{4,3,2,1,0:T(2,128)} %bitcast.2, f32[4,256]{1,0:T(4,128)} %omega_in.1), custom_call_target="tpu_custom_call" | custom-call | tf_op jit(solution)/shard_map/pallas_call | solution.py:370
  1.6 5.5 %collective-permute-start.3 = (f32[120,128]{1,0:T(8,128)S(1)}, f32[120,128]{1,0:T(8,128)S(1)}, u32[]{:S(2)}, u32[]{:S(2)}) collective-permute-start(f32[120,128]{1,0:T(8,128)S(1)} %get-tuple-element.26), channel_id=1, source_target_pairs={{0,15},{1,2},{2,1},{3,4},{4,3},{5,6},{6,5},{7,8},{8,7},{9,10},{10,... | collective-permute-start | bytes 184328 | tf_op jit(solution)/shard_map/ppermute | solution.py:392
  7.1 0.0 collective-permute-start.2
  7.1 0.8 %collective-permute-start.1 = (f32[120,128]{1,0:T(8,128)S(1)}, f32[120,128]{1,0:T(8,128)S(1)}, u32[]{:S(2)}, u32[]{:S(2)}) collective-permute-start(f32[120,128]{1,0:T(8,128)S(1)} %get-tuple-element.24), channel_id=1, source_target_pairs={{0,15},{1,2},{2,1},{3,4},{4,3},{5,6},{6,5},{7,8},{8,7},{9,10},{10,... | collective-permute-start | bytes 184328 | tf_op jit(solution)/shard_map/ppermute | solution.py:393
  7.9 0.0 collective-permute-start
  7.9 3.3 %shard_map.60 = (bf16[3,10,128,256]{3,2,1,0:T(8,128)(2,1)S(1)}, bf16[3,10,128,256]{3,2,1,0:T(8,128)(2,1)S(1)}, bf16[3,10,128,256]{3,2,1,0:T(8,128)(2,1)S(1)}, f3...) custom-call(f32[4,3,3,16,128]{4,3,2,1,0:T(8,128)S(1)} %get-tuple-element.20.vel_ref, ...), custom_call_target="tpu_custom_call" | custom-call | tf_op jit(solution)/shard_map/pallas_call | solution.py:397
  11.2 0.0 collective-permute-done.3.outer_ref
  11.2 0.0 collective-permute-done.2.inner_ref
  11.2 1.6 %shard_map.61 = (bf16[3,10,128,256]{3,2,1,0:T(8,128)(2,1)S(1)}, f32[256,256]{1,0:T(8,128)S(1)}) custom-call(s32[1]{0:T(128)} %bitcast.parity_ref, f32[4,3,3,16,128]{4,3,2,1,0:T(8,128)S(1)} %get-tuple-element.20.vel_ref, f32[2,4,3,10,128]{4,3,2,1,0:T(8,128)S(1)} %get-tuple-element.23.part_ref, ...), custom_call_target="tpu_custom_call", output_to_operand_aliasing={{0}: (7, {})} | custom-call | tf_op jit(solution)/shard_map/pallas_call | solution.py:410
  12.8 0.7 %collective-permute-done.1.outer_ref = f32[120,128]{1,0:T(8,128)S(1)} collective-permute-done((f32[120,128]{1,0:T(8,128)S(1)}, f32[120,128]{1,0:T(8,128)S(1)}, u32[]{:S(2)}, u32[]{:S(2)}) %collective-permute-start.1) | collective-permute-done | bytes 61472 | tf_op jit(solution)/shard_map/ppermute | solution.py:393
  13.5 0.0 collective-permute-done.inner_ref
  13.5 1.6 %shard_map.62 = (bf16[3,10,128,256]{3,2,1,0:T(8,128)(2,1)S(1)}, f32[72,256]{1,0:T(8,128)S(1)}, f32[72,256]{1,0:T(8,128)S(1)}) custom-call(s32[1]{0:T(128)} %bitcast.parity_ref, f32[4,3,3,16,128]{4,3,2,1,0:T(8,128)S(1)} %get-tuple-element.20.vel_ref, f32[2,4,3,10,128]{4,3,2,1,0:T(8,128)S(1)} %get-tuple-element.23.part_ref, ...), custom_call_target="tpu_custom_call", output_to_operand_aliasing={{0}: (7, {})} | custom-call | tf_op jit(solution)/shard_map/pallas_call | solution.py:410
  15.1 0.1 collective-permute-start.4
  15.1 1.3 %collective-permute-done.4 = f32[72,256]{1,0:T(8,128)S(1)} collective-permute-done((f32[72,256]{1,0:T(8,128)S(1)}, f32[72,256]{1,0:T(8,128)S(1)}, u32[]{:S(2)}, u32[]{:S(2)}) %collective-permute-start.4) | collective-permute-done | bytes 73760 | tf_op jit(solution)/shard_map/ppermute | solution.py:426
  16.4 0.9 %collective-permute-start.5 = (f32[72,256]{1,0:T(8,128)S(1)}, f32[72,256]{1,0:T(8,128)S(1)}, u32[]{:S(2)}, u32[]{:S(2)}) collective-permute-start(f32[72,256]{1,0:T(8,128)S(1)} %add.17), channel_id=1, source_target_pairs={{0,2},{1,3},{2,0},{3,1},{4,6},{5,7},{6,4},{7,5},{8,10},{9,11},{10,... | collective-permute-start | bytes 221192 | tf_op jit(solution)/shard_map/ppermute | solution.py:429
  17.4 3.5 %collective-permute-done.5 = f32[72,256]{1,0:T(8,128)S(1)} collective-permute-done((f32[72,256]{1,0:T(8,128)S(1)}, f32[72,256]{1,0:T(8,128)S(1)}, u32[]{:S(2)}, u32[]{:S(2)}) %collective-permute-start.5) | collective-permute-done | bytes 73760 | tf_op jit(solution)/shard_map/ppermute | solution.py:429
  20.8 0.1 collective-permute-start.6
  20.9 4.3 %collective-permute-done.6 = f32[72,256]{1,0:T(8,128)S(1)} collective-permute-done((f32[72,256]{1,0:T(8,128)S(1)}, f32[72,256]{1,0:T(8,128)S(1)}, u32[]{:S(2)}, u32[]{:S(2)}) %collective-permute-start.6) | collective-permute-done | bytes 73760 | tf_op jit(solution)/shard_map/ppermute | solution.py:429
  25.3 0.8 %collective-permute-start.7 = (f32[72,256]{1,0:T(8,128)S(1)}, f32[72,256]{1,0:T(8,128)S(1)}, u32[]{:S(2)}, u32[]{:S(2)}) collective-permute-start(f32[72,256]{1,0:T(8,128)S(1)} %add.19), channel_id=1, source_target_pairs={{0,8},{1,9},{2,10},{3,11},{4,12},{5,13},{6,14},{7,15},{8,0},{9,1},... | collective-permute-start | bytes 221192 | tf_op jit(solution)/shard_map/ppermute | solution.py:429
  26.1 4.7 %collective-permute-done.7 = f32[72,256]{1,0:T(8,128)S(1)} collective-permute-done((f32[72,256]{1,0:T(8,128)S(1)}, f32[72,256]{1,0:T(8,128)S(1)}, u32[]{:S(2)}, u32[]{:S(2)}) %collective-permute-start.7) | collective-permute-done | bytes 73760 | tf_op jit(solution)/shard_map/ppermute | solution.py:429
  30.8 0.1 collective-permute-start.8
  30.9 1.3 %collective-permute-done.8.other_ref = f32[72,256]{1,0:T(8,128)S(1)} collective-permute-done((f32[72,256]{1,0:T(8,128)S(1)}, f32[72,256]{1,0:T(8,128)S(1)}, u32[]{:S(2)}, u32[]{:S(2)}) %collective-permute-start.8) | collective-permute-done | bytes 73760 | tf_op jit(solution)/shard_map/ppermute | solution.py:431
  32.2 9.6 %shard_map.63 = (f32[256,256]{1,0:T(8,128)}, bf16[3,3,10,128,256]{4,3,2,1,0:T(8,128)(2,1)}) custom-call(s32[1]{0:T(128)} %bitcast.parity_ref, f32[72,256]{1,0:T(8,128)S(1)} %add.20.mine_ref, f32[72,256]{1,0:T(8,128)S(1)} %collective-permute-done.8.other_ref, bf16[3,10,128,256]{3,2,1,0:T(8,128)(2,1)S(1)} %get-tuple-element.33.x_ref, ...), custom_call_target="tpu_custom_call" | custom-call | tf_op jit(solution)/shard_map/pallas_call | solution.py:433
  (4 shorter events, 0.0 us)
Async XLA Ops:
  1.6 9.5 %collective-permute-start.3 = (f32[120,128]{1,0:T(8,128)S(1)}, f32[120,128]{1,0:T(8,128)S(1)}, u32[]{:S(2)}, u32[]{:S(2)}) collective-permute-start(f32[120,128]{1,0:T(8,128)S(1)} %get-tuple-element.26), channel_id=1, source_target_pairs={{0,15},{1,2},{2,1},{3,4},{4,3},{5,6},{6,5},{7,8},{8,7},{9,10},{10,... | collective-permute-start | bytes 184328 | tf_op jit(solution)/shard_map/ppermute | solution.py:392
  7.1 4.1 %collective-permute-start.2 = (f32[120,128]{1,0:T(8,128)S(1)}, f32[120,128]{1,0:T(8,128)S(1)}, u32[]{:S(2)}, u32[]{:S(2)}) collective-permute-start(f32[120,128]{1,0:T(8,128)S(1)} %get-tuple-element.26), channel_id=1, source_target_pairs={{0,1},{1,0},{2,3},{3,2},{4,5},{5,4},{6,7},{7,6},{8,9},{9,8},{10,11... | collective-permute-start | bytes 184328 | tf_op jit(solution)/shard_map/ppermute | solution.py:394
  7.1 6.3 %collective-permute-start.1 = (f32[120,128]{1,0:T(8,128)S(1)}, f32[120,128]{1,0:T(8,128)S(1)}, u32[]{:S(2)}, u32[]{:S(2)}) collective-permute-start(f32[120,128]{1,0:T(8,128)S(1)} %get-tuple-element.24), channel_id=1, source_target_pairs={{0,15},{1,2},{2,1},{3,4},{4,3},{5,6},{6,5},{7,8},{8,7},{9,10},{10,... | collective-permute-start | bytes 184328 | tf_op jit(solution)/shard_map/ppermute | solution.py:393
  7.9 5.6 %collective-permute-start = (f32[120,128]{1,0:T(8,128)S(1)}, f32[120,128]{1,0:T(8,128)S(1)}, u32[]{:S(2)}, u32[]{:S(2)}) collective-permute-start(f32[120,128]{1,0:T(8,128)S(1)} %get-tuple-element.24), channel_id=1, source_target_pairs={{0,1},{1,0},{2,3},{3,2},{4,5},{5,4},{6,7},{7,6},{8,9},{9,8},{10,11... | collective-permute-start | bytes 184328 | tf_op jit(solution)/shard_map/ppermute | solution.py:395
  15.1 1.3 %collective-permute-start.4 = (f32[72,256]{1,0:T(8,128)S(1)}, f32[72,256]{1,0:T(8,128)S(1)}, u32[]{:S(2)}, u32[]{:S(2)}) collective-permute-start(f32[72,256]{1,0:T(8,128)S(1)} %get-tuple-element.32), channel_id=1, source_target_pairs={{0,1},{1,0},{2,3},{3,2},{4,5},{5,4},{6,7},{7,6},{8,9},{9,8},{10,11... | collective-permute-start | bytes 221192 | tf_op jit(solution)/shard_map/ppermute | solution.py:426
  16.4 4.4 %collective-permute-start.5 = (f32[72,256]{1,0:T(8,128)S(1)}, f32[72,256]{1,0:T(8,128)S(1)}, u32[]{:S(2)}, u32[]{:S(2)}) collective-permute-start(f32[72,256]{1,0:T(8,128)S(1)} %add.17), channel_id=1, source_target_pairs={{0,2},{1,3},{2,0},{3,1},{4,6},{5,7},{6,4},{7,5},{8,10},{9,11},{10,... | collective-permute-start | bytes 221192 | tf_op jit(solution)/shard_map/ppermute | solution.py:429
  20.8 4.4 %collective-permute-start.6 = (f32[72,256]{1,0:T(8,128)S(1)}, f32[72,256]{1,0:T(8,128)S(1)}, u32[]{:S(2)}, u32[]{:S(2)}) collective-permute-start(f32[72,256]{1,0:T(8,128)S(1)} %add.18), channel_id=1, source_target_pairs={{0,4},{1,5},{2,6},{3,7},{4,0},{5,1},{6,2},{7,3},{8,12},{9,13},{10,... | collective-permute-start | bytes 221192 | tf_op jit(solution)/shard_map/ppermute | solution.py:429
  25.3 5.5 %collective-permute-start.7 = (f32[72,256]{1,0:T(8,128)S(1)}, f32[72,256]{1,0:T(8,128)S(1)}, u32[]{:S(2)}, u32[]{:S(2)}) collective-permute-start(f32[72,256]{1,0:T(8,128)S(1)} %add.19), channel_id=1, source_target_pairs={{0,8},{1,9},{2,10},{3,11},{4,12},{5,13},{6,14},{7,15},{8,0},{9,1},... | collective-permute-start | bytes 221192 | tf_op jit(solution)/shard_map/ppermute | solution.py:429
  30.8 1.3 %collective-permute-start.8 = (f32[72,256]{1,0:T(8,128)S(1)}, f32[72,256]{1,0:T(8,128)S(1)}, u32[]{:S(2)}, u32[]{:S(2)}) collective-permute-start(f32[72,256]{1,0:T(8,128)S(1)} %add.20.mine_ref), channel_id=1, source_target_pairs={{0,1},{1,0},{2,3},{3,2},{4,5},{5,4},{6,7},{7,6},{8,9},{9,8},{10,11... | collective-permute-start | bytes 221192 | tf_op jit(solution)/shard_map/ppermute | solution.py:431
